TPU v7x, 32 devices: a whole 2x2x4 slice. The times are simulated.
32 devices in a mesh: groups: 2 (over x), row: 8 (over z, y), rep: 2 (over core).
Axes of the slice: x: 2, y: 2, z: 4, core: 2. Of those that a mesh axis runs over, the one named last changes fastest.
Arguments:
- features: float32 [16384, 512], P(('groups', 'row')), parts along dimension 0, may hold values from -6 to 6
- weight: float32 [512, 512], replicated, may hold values from -0.25 to 0.25
- cotangent: float32 [16384, 512], P(('groups', 'row')), parts along dimension 0, may hold values from -6 to 6
- tile_vals: float32 [128, 2, 16, 128, 128], P(('groups', 'row'), 'rep'), parts along dimension 0, may hold values from -0.1875 to 0.1875
- col_tile: int32 [128, 2, 16], P(('groups', 'row'), 'rep'), parts along dimension 0, may hold values from 0 to 63, as said below
- counts: int32 [128, 2], P(('groups', 'row'), 'rep'), parts along dimension 0, may hold values from 1 to 16, as said below
Outputs:
- output: float32 [16384, 512], P(('groups', 'row')), parts along dimension 0
- input_grad: float32 [16384, 512], P(('groups', 'row')), parts along dimension 0
- weight_grad: float32 [1024, 512], P('groups'), parts along dimension 0
There are 2 independent parts, one for each index of `groups`. A program takes and returns all parts, laid end to end along the dimension named above; an argument that names none is the same for every part. Nothing has to cross between parts.
Inputs may be any that keep to these rules, and one draw needn't show every extreme that they name: `col_tile`: for row tile i and replica k the 16 column tiles are distinct, and each column tile j has j // 8 = (i // 8 - k * 4 - t) mod 8 for some t below 4. `counts`: slots at or past the count are not part of the graph.
All inputs are finite; a program needn't handle non-finite values.
Results may differ from a plain program's by a relative error of at most 0.0003.
Values sent between devices are 32-bit elements; how exact they have to be, the bound alone decides.
No kernel may reach another device: no remote copies, remote signals or barrier semaphores. Data moves between devices by JAX's collectives and lax.ppermute only.
A program may use at most 256 MiB of HBM per device.

v0:
```python
import jax
import jax.numpy as jnp
from jax import lax
from jax.sharding import PartitionSpec as P


def shifted(block, axis, distance):
    devices = range(lax.axis_size(axis))
    route = [((i - distance) % len(devices), i) for i in devices]
    return lax.ppermute(block, axis, route)


def slot_positions(col_tile, counts, row_index, rep_index, cycle_size, half_size):
    tiles_here = col_tile.shape[0]
    slot_count = col_tile.shape[2]
    columns = col_tile[:, 0]
    column_block = columns // tiles_here
    within = columns % tiles_here
    position = (
        jnp.mod(row_index - rep_index * half_size - column_block, cycle_size) * tiles_here + within
    )
    slot_ids = lax.broadcasted_iota(jnp.int32, (tiles_here, slot_count), 1)
    active = (slot_ids < counts[:, 0][:, None]).astype(jnp.float32)
    return (position, active)


def densify(tile_block, position, half_size):
    tiles_here = tile_block.shape[0]
    slot_count = tile_block.shape[1]
    tile_size = tile_block.shape[2]
    row_ids = lax.broadcasted_iota(jnp.int32, (tiles_here, slot_count), 0)
    placed = jnp.zeros((tiles_here, half_size * tiles_here, tile_size, tile_size), jnp.float32)
    placed = placed.at[row_ids, position].add(tile_block)
    return placed.transpose(0, 2, 1, 3).reshape(
        tiles_here * tile_size, half_size * tiles_here * tile_size
    )


def silu_slope(pre):
    sigma = jax.nn.sigmoid(pre)
    return (pre * sigma, sigma * (1.0 + pre * (1.0 - sigma)))


def per_device(features, weight, cotangent, tile_vals, col_tile, counts):
    highest = lax.Precision.HIGHEST
    cycle_size = lax.axis_size("row")
    replicas = lax.axis_size("rep")
    half_size = cycle_size // replicas
    row_index = lax.axis_index("row")
    rep_index = lax.axis_index("rep")
    block_rows = features.shape[0]
    position, active = slot_positions(col_tile, counts, row_index, rep_index, cycle_size, half_size)
    masked_tiles = tile_vals[:, 0] * active[:, :, None, None]
    adjacent = densify(masked_tiles, position, half_size)

    def block_product(block, offset):
        selected = lax.dynamic_slice_in_dim(adjacent, offset * block_rows, block_rows, 1)
        return jnp.dot(selected, block, precision=highest, preferred_element_type=jnp.float32)

    jumped = shifted(features, "row", half_size)
    current = jnp.where(rep_index == 0, features, jumped)
    running = block_product(current, 0)

    def advance(offset, carried):
        holding, partial_value = carried
        holding = shifted(holding, "row", 1)
        return (holding, partial_value + block_product(holding, offset))

    _, aggregated = lax.fori_loop(1, half_size, advance, (current, running))
    share_rows = block_rows // replicas
    summed = lax.psum(aggregated, "rep")
    pre = jnp.dot(summed, weight, precision=highest, preferred_element_type=jnp.float32)
    output, slope = silu_slope(pre)
    grad_pre = cotangent * slope
    summed_share = lax.dynamic_slice_in_dim(summed, rep_index * share_rows, share_rows, 0)
    grad_share = lax.dynamic_slice_in_dim(grad_pre, rep_index * share_rows, share_rows, 0)
    weight_part = lax.dot_general(
        summed_share,
        grad_share,
        (((0,), (0,)), ((), ())),
        precision=highest,
        preferred_element_type=jnp.float32,
    )
    grad_agg = jnp.dot(grad_pre, weight.T, precision=highest, preferred_element_type=jnp.float32)
    weight_grad = lax.psum(weight_part, ("row", "rep"))

    def give_back(offset):
        selected = lax.dynamic_slice_in_dim(adjacent, offset * block_rows, block_rows, 1)
        return lax.dot_general(
            selected,
            grad_agg,
            (((0,), (0,)), ((), ())),
            precision=highest,
            preferred_element_type=jnp.float32,
        )

    partial_value = give_back(half_size - 1)

    def pass_along(offset, holding):
        holding = shifted(holding, "row", cycle_size - 1)
        return holding + give_back(half_size - 1 - offset)

    partial_value = lax.fori_loop(1, half_size, pass_along, partial_value)
    homed = shifted(partial_value, "row", half_size)
    gathered_grad = jnp.where(rep_index == 0, partial_value, homed)
    input_grad = lax.psum(gathered_grad, "rep")
    return (output, input_grad, weight_grad)


def solution(mesh):
    return jax.shard_map(
        per_device,
        mesh=mesh,
        in_specs=(
            P(("groups", "row"), None),
            P(),
            P(("groups", "row"), None),
            P(("groups", "row"), "rep", None, None, None),
            P(("groups", "row"), "rep", None),
            P(("groups", "row"), "rep"),
        ),
        out_specs=(P(("groups", "row"), None), P(("groups", "row"), None), P("groups", None)),
        check_vma=False,
    )
```

profile of v0, /device:TPU:0, one launch (start us, length us, event | category | flops | bytes accessed | tf_op | source)
XLA Modules:
  0.0 706.8 jit_solution(248135751046731666)
XLA Ops:
  7.2 4.1 collective-permute-start.2
  11.3 0.7 fusion.22
  12.0 0.1 reshape.189
  12.1 0.7 fusion.28
  12.8 7.2 %bitcast_multiply_fusion = f32[8,16,128,128]{3,2,1,0:T(8,128)} fusion(f32[8,1,16,128,128]{4,3,2,1,0:T(8,128)} %param.13, f32[8,16]{1,0:T(8,128)S(1)} %fusion.28), kind=kLoop, calls=%fused_computation.10 | loop fusion | flops 2097152 | bytes 16777728 | tf_op jit(solution)/shard_map/mul | solution.py:53
  20.1 7.9 %broadcast_in_dim.2 = f32[8,32,128,128]{3,2,1,0:T(8,128)} broadcast(f32[]{:T(128)} %constant.109.clone.1), dimensions={} | broadcast | bytes 16777220 | tf_op jit(solution)/shard_map/broadcast_in_dim | solution.py:32
  28.0 27.5 %scatter_fusion = f32[8,32,128,128]{3,2,1,0:T(8,128)} fusion(f32[8,32,128,128]{3,2,1,0:T(8,128)} %broadcast_in_dim.2, s32[128]{0:T(128)S(1)} %reshape.189, f32[128,128,128]{2,1,0:T(8,128)} %bitcast.29), kind=kCustom, calls=%fused_computation | custom fusion | flops 2097152 | bytes 25166848 | tf_op jit(solution)/shard_map/scatter-add | solution.py:33
  55.5 15.2 %copy.10 = f32[8,128,32,128]{3,2,1,0:T(8,128)S(1)} copy(f32[8,128,32,128]{3,1,2,0:T(8,128)} %bitcast.27) | data formatting | bytes 33554432 | tf_op jit(solution)/shard_map/transpose | solution.py:34
  70.7 10.6 %copy.13 = f32[128,8,32,128]{3,1,2,0:T(8,128)S(1)} copy(f32[128,8,32,128]{3,2,1,0:T(8,128)S(1)} %bitcast.28) | data formatting | bytes 33554432
  81.3 20.8 %collective-permute-done.2 = f32[1024,512]{1,0:T(8,128)S(1)} collective-permute-done((f32[1024,512]{1,0:T(8,128)}, f32[1024,512]{1,0:T(8,128)S(1)}, u32[]{:S(2)}, u32[]{:S(2)}) %collective-permute-start.2) | collective-permute-done | bytes 2097184 | tf_op jit(solution)/shard_map/ppermute | solution.py:10
  102.1 0.5 broadcast_select_fusion.1
  102.6 8.0 %fusion.14 = f32[1024,512]{1,0:T(8,128)} fusion(f32[1024,512]{1,0:T(8,128)S(1)} %broadcast_select_fusion.1, f32[1024,4096]{1,0:T(8,128)S(1)} %bitcast.25), kind=kOutput, calls=%fused_computation.13 | convolution fusion | flops 6442450944 | bytes 8388608 | tf_op jit(solution)/shard_map/dot_general | solution.py:58
  110.6 183.1 %while.28 = (s32[]{:T(128)}, f32[1024,512]{1,0:T(8,128)}, f32[1024,512]{1,0:T(8,128)}, f32[1024,4096]{1,0:T(8,128)}, s32[]{:T(128)}, /*index=5*/s32[]{:T(128)}, s32[]{:T(128)}, s32[]{:T(128)}) while((s32[]{:T(128)}, f32[1024,512]{1,0:T(8,128)}, f32[1024,512]{1,0:T(8,128)}, f32[1024,4096]{1,0:T(8,128)}, s32[]{:T(128)}, /*index=5*/s32[]{:T(128)}, ...), condition=%wide.region_2.3_spmd, body=%wide.region_1.2_spmd.sunk | while | flops 6442975232 | bytes 39846116 | solution.py:69
  110.6 1.6 collective-permute-start
  112.2 48.9 %collective-permute-done = f32[1024,512]{1,0:T(8,128)S(1)} collective-permute-done((f32[1024,512]{1,0:T(8,128)}, f32[1024,512]{1,0:T(8,128)S(1)}, u32[]{:S(2)}, u32[]{:S(2)}) %collective-permute-start) | collective-permute-done | bytes 2097184 | tf_op jit(solution)/shard_map/while/body/eval_jaxpr/ppermute | solution.py:10
  161.1 1.3 copy.22
  162.5 8.7 %fusion.48 = f32[1024,512]{1,0:T(8,128)S(1)} fusion(f32[1024,512]{1,0:T(8,128)S(1)} %copy-done.2, f32[1024,512]{1,0:T(8,128)S(1)} %collective-permute-done, f32[1024,4096]{1,0:T(8,128)} %get-tuple-element.250, s32[]{:T(128)S(6)} %select_n.117), kind=kOutput, calls=%fused_computation.3.clone.1 | convolution fusion | flops 6442975232 | bytes 10485764 | tf_op jit(solution)/shard_map/while/body/eval_jaxpr/dot_general | solution.py:58
  171.2 1.3 copy-done.3
  172.5 49.7 %collective-permute-done = f32[1024,512]{1,0:T(8,128)S(1)} collective-permute-done((f32[1024,512]{1,0:T(8,128)}, f32[1024,512]{1,0:T(8,128)S(1)}, u32[]{:S(2)}, u32[]{:S(2)}) %collective-permute-start) | collective-permute-done | bytes 2097184 | tf_op jit(solution)/shard_map/while/body/eval_jaxpr/ppermute | solution.py:10
  222.2 1.3 copy.22
  223.5 8.7 %fusion.48 = f32[1024,512]{1,0:T(8,128)S(1)} fusion(f32[1024,512]{1,0:T(8,128)S(1)} %copy-done.2, f32[1024,512]{1,0:T(8,128)S(1)} %collective-permute-done, f32[1024,4096]{1,0:T(8,128)} %get-tuple-element.250, s32[]{:T(128)S(6)} %select_n.117), kind=kOutput, calls=%fused_computation.3.clone.1 | convolution fusion | flops 6442975232 | bytes 10485764 | tf_op jit(solution)/shard_map/while/body/eval_jaxpr/dot_general | solution.py:58
  232.3 1.3 copy-done.3
  233.6 48.7 %collective-permute-done = f32[1024,512]{1,0:T(8,128)S(1)} collective-permute-done((f32[1024,512]{1,0:T(8,128)}, f32[1024,512]{1,0:T(8,128)S(1)}, u32[]{:S(2)}, u32[]{:S(2)}) %collective-permute-start) | collective-permute-done | bytes 2097184 | tf_op jit(solution)/shard_map/while/body/eval_jaxpr/ppermute | solution.py:10
  282.3 1.3 copy.22
  283.7 8.7 %fusion.48 = f32[1024,512]{1,0:T(8,128)S(1)} fusion(f32[1024,512]{1,0:T(8,128)S(1)} %copy-done.2, f32[1024,512]{1,0:T(8,128)S(1)} %collective-permute-done, f32[1024,4096]{1,0:T(8,128)} %get-tuple-element.250, s32[]{:T(128)S(6)} %select_n.117), kind=kOutput, calls=%fused_computation.3.clone.1 | convolution fusion | flops 6442975232 | bytes 10485764 | tf_op jit(solution)/shard_map/while/body/eval_jaxpr/dot_general | solution.py:58
  292.4 1.3 copy-done.3
  293.8 18.5 %all-reduce.4.cloned.1.call-done = f32[1024,512]{1,0:T(8,128)} async-done(((f32[1024,512]{1,0:T(8,128)}), f32[1024,512]{1,0:T(8,128)}) %all-reduce.4.cloned.1.call-update) | async-done | bytes 2097168 | tf_op jit(solution)/shard_map/psum | solution.py:71
  312.3 7.0 multiply_multiply_fusion
  319.3 3.5 fusion.31
  322.8 9.8 %fusion.12 = f32[1024,512]{1,0:T(8,128)} fusion(f32[1024,512]{1,0:T(8,128)S(1)} %fusion.31, f32[1024,4096]{1,0:T(8,128)} %get-tuple-element.288), kind=kOutput, calls=%fused_computation.11 | convolution fusion | flops 6442450944 | bytes 8388608 | tf_op jit(solution)/shard_map/dot_general | solution.py:89
  332.6 178.8 %while.29 = (s32[]{:T(128)}, f32[1024,512]{1,0:T(8,128)}, f32[1024,4096]{1,0:T(8,128)}, f32[1024,512]{1,0:T(8,128)S(1)}, s32[]{:T(128)}, /*index=5*/s32[]{:T(128)}, s32[]{:T(128)}, s32[]{:T(128)}, s32[]{:T(128)}) while((s32[]{:T(128)}, f32[1024,512]{1,0:T(8,128)}, f32[1024,4096]{1,0:T(8,128)}, f32[1024,512]{1,0:T(8,128)S(1)}, s32[]{:T(128)}, ...), condition=%wide.region_5.6_spmd, body=%wide.region_4.5_spmd.sunk | while | flops 6442975232 | bytes 18874564 | solution.py:103
  332.6 4.5 collective-permute-start.1
  337.1 45.7 %collective-permute-done.1 = f32[1024,512]{1,0:T(8,128)} collective-permute-done((f32[1024,512]{1,0:T(8,128)}, f32[1024,512]{1,0:T(8,128)}, u32[]{:S(2)}, u32[]{:S(2)}) %collective-permute-start.1) | collective-permute-done | bytes 2097184 | tf_op jit(solution)/shard_map/while/body/eval_jaxpr/ppermute | solution.py:10
  382.7 9.8 %fusion.51 = f32[1024,512]{1,0:T(8,128)} fusion(f32[1024,512]{1,0:T(8,128)} %collective-permute-done.1, f32[1024,512]{1,0:T(8,128)S(1)} %get-tuple-element.276, f32[1024,4096]{1,0:T(8,128)} %get-tuple-element.275, s32[]{:T(128)S(6)} %select_n.118), kind=kOutput, calls=%fused_computation.7.clone.1 | convolution fusion | flops 6442975232 | bytes 10485764 | tf_op jit(solution)/shard_map/while/body/eval_jaxpr/dot_general | solution.py:89
  392.6 5.2 collective-permute-start.1
  397.8 44.9 %collective-permute-done.1 = f32[1024,512]{1,0:T(8,128)} collective-permute-done((f32[1024,512]{1,0:T(8,128)}, f32[1024,512]{1,0:T(8,128)}, u32[]{:S(2)}, u32[]{:S(2)}) %collective-permute-start.1) | collective-permute-done | bytes 2097184 | tf_op jit(solution)/shard_map/while/body/eval_jaxpr/ppermute | solution.py:10
  442.6 9.8 %fusion.51 = f32[1024,512]{1,0:T(8,128)} fusion(f32[1024,512]{1,0:T(8,128)} %collective-permute-done.1, f32[1024,512]{1,0:T(8,128)S(1)} %get-tuple-element.276, f32[1024,4096]{1,0:T(8,128)} %get-tuple-element.275, s32[]{:T(128)S(6)} %select_n.118), kind=kOutput, calls=%fused_computation.7.clone.1 | convolution fusion | flops 6442975232 | bytes 10485764 | tf_op jit(solution)/shard_map/while/body/eval_jaxpr/dot_general | solution.py:89
  452.5 5.2 collective-permute-start.1
  457.6 43.9 %collective-permute-done.1 = f32[1024,512]{1,0:T(8,128)} collective-permute-done((f32[1024,512]{1,0:T(8,128)}, f32[1024,512]{1,0:T(8,128)}, u32[]{:S(2)}, u32[]{:S(2)}) %collective-permute-start.1) | collective-permute-done | bytes 2097184 | tf_op jit(solution)/shard_map/while/body/eval_jaxpr/ppermute | solution.py:10
  501.6 9.8 %fusion.51 = f32[1024,512]{1,0:T(8,128)} fusion(f32[1024,512]{1,0:T(8,128)} %collective-permute-done.1, f32[1024,512]{1,0:T(8,128)S(1)} %get-tuple-element.276, f32[1024,4096]{1,0:T(8,128)} %get-tuple-element.275, s32[]{:T(128)S(6)} %select_n.118), kind=kOutput, calls=%fused_computation.7.clone.1 | convolution fusion | flops 6442975232 | bytes 10485764 | tf_op jit(solution)/shard_map/while/body/eval_jaxpr/dot_general | solution.py:89
  511.4 4.5 fusion.17
  515.9 0.0 all-reduce.6.cloned.1.call-start
  516.0 92.5 %collective-permute-done.3 = f32[1024,512]{1,0:T(8,128)} collective-permute-done((f32[1024,512]{1,0:T(8,128)}, f32[1024,512]{1,0:T(8,128)}, u32[]{:S(2)}, u32[]{:S(2)}) %collective-permute-start.3) | collective-permute-done | bytes 2097184 | tf_op jit(solution)/shard_map/ppermute | solution.py:10
  608.5 1.8 broadcast_select_fusion
  610.3 62.3 %all-reduce.8.cloned.1.call-done = f32[512,512]{1,0:T(8,128)} async-done(((f32[512,512]{1,0:T(8,128)}), f32[512,512]{1,0:T(8,128)}) %all-reduce.8.cloned.1.call-update) | async-done | bytes 1048592 | tf_op jit(solution)/shard_map/psum | solution.py:85
  672.6 23.5 %all-reduce.6.cloned.1.call-done = f32[1024,512]{1,0:T(8,128)} async-done(((f32[1024,512]{1,0:T(8,128)}), f32[1024,512]{1,0:T(8,128)}) %all-reduce.6.cloned.1.call-update) | async-done | bytes 2097168 | tf_op jit(solution)/shard_map/psum | solution.py:106
  696.1 3.2 copy.33
  699.3 1.0 copy.34
  (33 shorter events, 0.2 us)
Async XLA Ops:
  7.2 305.1 %copy-start = (f32[512,512]{1,0:T(8,128)S(1)}, f32[512,512]{1,0:T(8,128)}, u32[]{:S(2)}) copy-start(f32[512,512]{1,0:T(8,128)} %param.11) | copy-start | bytes 3145732
  7.2 305.1 %all-reduce.4.cloned.1.call-start = ((), (), s32[]{:S(2)}) async-start(), calls=%async_computation | async-start | bytes 4194304 | tf_op jit(solution)/shard_map/psum | solution.py:71
  7.2 94.9 %collective-permute-start.2 = (f32[1024,512]{1,0:T(8,128)}, f32[1024,512]{1,0:T(8,128)S(1)}, u32[]{:S(2)}, u32[]{:S(2)}) collective-permute-start(f32[1024,512]{1,0:T(8,128)} %param.10), channel_id=1, source_target_pairs={{8,0},{10,2},{12,4},{14,6},{0,8},{2,10},{4,12},{6,14},{9,1},{11,3}... | collective-permute-start | bytes 6291464 | tf_op jit(solution)/shard_map/ppermute | solution.py:10
  70.7 31.4 %copy-start.7 = (f32[1024,512]{1,0:T(8,128)S(1)}, f32[1024,512]{1,0:T(8,128)}, u32[]{:S(2)}) copy-start(f32[1024,512]{1,0:T(8,128)} %param.10) | copy-start | bytes 6291460
  81.3 29.3 %copy-start.1 = (f32[128,8,32,128]{3,1,2,0:T(8,128)}, f32[128,8,32,128]{3,1,2,0:T(8,128)S(1)}, u32[]{:S(2)}) copy-start(f32[128,8,32,128]{3,1,2,0:T(8,128)S(1)} %copy.13) | copy-start | bytes 50331652
  102.6 8.0 %copy-start.5 = (f32[1024,512]{1,0:T(8,128)}, f32[1024,512]{1,0:T(8,128)S(1)}, u32[]{:S(2)}) copy-start(f32[1024,512]{1,0:T(8,128)S(1)} %broadcast_select_fusion.1) | copy-start | bytes 6291460
  110.6 50.5 %collective-permute-start = (f32[1024,512]{1,0:T(8,128)}, f32[1024,512]{1,0:T(8,128)S(1)}, u32[]{:S(2)}, u32[]{:S(2)}) collective-permute-start(f32[1024,512]{1,0:T(8,128)} %get-tuple-element.240), channel_id=1, source_target_pairs={{14,0},{0,2},{2,4},{4,6},{6,8},{8,10},{10,12},{12,14},{15,1},{1,3}... | collective-permute-start | bytes 6291464 | tf_op jit(solution)/shard_map/while/body/eval_jaxpr/ppermute | solution.py:10
  112.2 50.3 %copy-start.2 = (f32[1024,512]{1,0:T(8,128)S(1)}, f32[1024,512]{1,0:T(8,128)}, u32[]{:S(2)}) copy-start(f32[1024,512]{1,0:T(8,128)} %get-tuple-element.241) | copy-start | bytes 6291460 | tf_op jit(solution)/shard_map/while
  171.2 1.3 copy-start.3
  172.5 49.7 %collective-permute-start = (f32[1024,512]{1,0:T(8,128)}, f32[1024,512]{1,0:T(8,128)S(1)}, u32[]{:S(2)}, u32[]{:S(2)}) collective-permute-start(f32[1024,512]{1,0:T(8,128)} %get-tuple-element.240), channel_id=1, source_target_pairs={{14,0},{0,2},{2,4},{4,6},{6,8},{8,10},{10,12},{12,14},{15,1},{1,3}... | collective-permute-start | bytes 6291464 | tf_op jit(solution)/shard_map/while/body/eval_jaxpr/ppermute | solution.py:10
  172.5 51.0 %copy-start.2 = (f32[1024,512]{1,0:T(8,128)S(1)}, f32[1024,512]{1,0:T(8,128)}, u32[]{:S(2)}) copy-start(f32[1024,512]{1,0:T(8,128)} %get-tuple-element.241) | copy-start | bytes 6291460 | tf_op jit(solution)/shard_map/while
  232.3 1.3 copy-start.3
  233.6 48.7 %collective-permute-start = (f32[1024,512]{1,0:T(8,128)}, f32[1024,512]{1,0:T(8,128)S(1)}, u32[]{:S(2)}, u32[]{:S(2)}) collective-permute-start(f32[1024,512]{1,0:T(8,128)} %get-tuple-element.240), channel_id=1, source_target_pairs={{14,0},{0,2},{2,4},{4,6},{6,8},{8,10},{10,12},{12,14},{15,1},{1,3}... | collective-permute-start | bytes 6291464 | tf_op jit(solution)/shard_map/while/body/eval_jaxpr/ppermute | solution.py:10
  233.6 50.1 %copy-start.2 = (f32[1024,512]{1,0:T(8,128)S(1)}, f32[1024,512]{1,0:T(8,128)}, u32[]{:S(2)}) copy-start(f32[1024,512]{1,0:T(8,128)} %get-tuple-element.241) | copy-start | bytes 6291460 | tf_op jit(solution)/shard_map/while
  292.4 1.3 copy-start.3
  293.7 18.5 %copy-start.9 = (f32[1024,512]{1,0:T(8,128)S(1)}, f32[1024,512]{1,0:T(8,128)}, u32[]{:S(2)}) copy-start(f32[1024,512]{1,0:T(8,128)} %param.12) | copy-start | bytes 6291460
  293.8 378.8 %all-reduce.8.cloned.1.call-start = ((), (), s32[]{:S(2)}) async-start(), calls=%async_computation.2 | async-start | bytes 2097152 | tf_op jit(solution)/shard_map/psum | solution.py:85
  319.3 3.5 copy-start.6
  332.6 50.2 %collective-permute-start.1 = (f32[1024,512]{1,0:T(8,128)}, f32[1024,512]{1,0:T(8,128)}, u32[]{:S(2)}, u32[]{:S(2)}) collective-permute-start(f32[1024,512]{1,0:T(8,128)} %get-tuple-element.265), channel_id=1, source_target_pairs={{2,0},{4,2},{6,4},{8,6},{10,8},{12,10},{14,12},{0,14},{3,1},{5,3},... | collective-permute-start | bytes 6291464 | tf_op jit(solution)/shard_map/while/body/eval_jaxpr/ppermute | solution.py:10
  392.6 50.0 %collective-permute-start.1 = (f32[1024,512]{1,0:T(8,128)}, f32[1024,512]{1,0:T(8,128)}, u32[]{:S(2)}, u32[]{:S(2)}) collective-permute-start(f32[1024,512]{1,0:T(8,128)} %get-tuple-element.265), channel_id=1, source_target_pairs={{2,0},{4,2},{6,4},{8,6},{10,8},{12,10},{14,12},{0,14},{3,1},{5,3},... | collective-permute-start | bytes 6291464 | tf_op jit(solution)/shard_map/while/body/eval_jaxpr/ppermute | solution.py:10
  452.5 49.1 %collective-permute-start.1 = (f32[1024,512]{1,0:T(8,128)}, f32[1024,512]{1,0:T(8,128)}, u32[]{:S(2)}, u32[]{:S(2)}) collective-permute-start(f32[1024,512]{1,0:T(8,128)} %get-tuple-element.265), channel_id=1, source_target_pairs={{2,0},{4,2},{6,4},{8,6},{10,8},{12,10},{14,12},{0,14},{3,1},{5,3},... | collective-permute-start | bytes 6291464 | tf_op jit(solution)/shard_map/while/body/eval_jaxpr/ppermute | solution.py:10
  511.4 97.1 %collective-permute-start.3 = (f32[1024,512]{1,0:T(8,128)}, f32[1024,512]{1,0:T(8,128)}, u32[]{:S(2)}, u32[]{:S(2)}) collective-permute-start(f32[1024,512]{1,0:T(8,128)} %get-tuple-element.162), channel_id=1, source_target_pairs={{8,0},{10,2},{12,4},{14,6},{0,8},{2,10},{4,12},{6,14},{9,1},{11,3}... | collective-permute-start | bytes 6291464 | tf_op jit(solution)/shard_map/ppermute | solution.py:10
  511.4 97.1 %copy-start.4 = (f32[1024,512]{1,0:T(8,128)S(1)}, f32[1024,512]{1,0:T(8,128)}, u32[]{:S(2)}) copy-start(f32[1024,512]{1,0:T(8,128)} %get-tuple-element.162) | copy-start | bytes 6291460
  515.9 180.2 %all-reduce.6.cloned.1.call-start = ((), (), s32[]{:S(2)}) async-start(), calls=%async_computation.1 | async-start | bytes 4194304 | tf_op jit(solution)/shard_map/psum | solution.py:106
  696.1 3.2 copy-start.8
Sparse Core Ops, SparseCore 0:
  293.9 18.3 all-reduce.3
  516.1 156.4 all-reduce.7
  675.6 20.4 all-reduce.5
where the time goes:
time: 707 us
  waiting for transfers between devices  499 us (71%)
  matrix products  88.5 us (13%)
  local copies, waits for them, and re-layouts  45.8 us (6%)
  other arithmetic  38.5 us (5%)
  starting transfers between devices  20.7 us (3%)
  between operations  13.8 us (2%)
    ppermute x8, waiting for transfers between devices, shifted(): return lax.ppermute(block, axis, route)  395 us
    psum x1, waiting for transfers between devices, per_device(): weight_grad = lax.psum(weight_part, ('row', 'rep'))  62.3 us
    dot_general x4, matrix products, give_back(): lax.dot_general(selected, grad_agg, (((0,), (0,)), ((), ())), precision=h...  39.3 us
    dot_general x4, matrix products, block_product(): jnp.dot(selected, block, precision=highest, preferred_element_type=jnp.fl...  34.2 us
    scatter-add x1, other arithmetic, densify(): placed = placed.at[row_ids, position].add(tile_block)  27.5 us
    psum x1, waiting for transfers between devices, per_device(): input_grad = lax.psum(gathered_grad, 'rep')  23.5 us
    ppermute x8, starting transfers between devices, shifted(): return lax.ppermute(block, axis, route)  20.5 us
    psum x1, waiting for transfers between devices, per_device(): summed = lax.psum(aggregated, 'rep')  18.5 us
  transfers between devices with their start and end apart: 11, of which 11 were waited for; matrix products, arithmetic and copies ran while one was open for 11% of the time, Pallas kernels for 0%

commit v1 on v0

v1 whole, which is shorter than its diff:
```python
import functools

import jax
import jax.numpy as jnp
from jax import lax
from jax.experimental import pallas as pl
from jax.experimental.pallas import tpu as pltpu
from jax.sharding import PartitionSpec as P

BF16 = jnp.bfloat16
F32 = jnp.float32
VMEM_LIMIT = 56 * 1024 * 1024


def ring_place(index, size):
    if size == 8:
        z, y = index // 2, index % 2
        return z + y * (size - 1 - 2 * z)
    return index


def ring_pairs(size):
    at = {ring_place(i, size): i for i in range(size)}
    ahead = [(at[p], at[(p + 1) % size]) for p in range(size)]
    back = [(b, a) for a, b in ahead]
    return ahead, back


def split_hi_lo(value):
    hi = value.astype(BF16)
    return hi, (value - hi.astype(F32)).astype(BF16)


def dot(a, b, dims=((1,), (0,))):
    return lax.dot_general(a, b, (dims, ((), ())), preferred_element_type=F32)


def params():
    return pltpu.CompilerParams(vmem_limit_bytes=VMEM_LIMIT)


def densify_kernel(first, slots, place_ref, count_ref, own_ref, other_ref, *refs):
    hi_ref, lo_ref = refs[-2:]
    row = first + pl.program_id(0)
    tiles_here = pl.num_programs(0)
    del tiles_here
    hi_ref[...] = jnp.zeros_like(hi_ref)
    lo_ref[...] = jnp.zeros_like(lo_ref)
    tile = own_ref.shape[-1]
    for replica, ref in enumerate((own_ref, other_ref)):

        def body(slot, carry, replica=replica, ref=ref):
            hi, lo = split_hi_lo(ref[0, slot])
            block = place_ref[replica, 0, row, slot]
            column = pl.multiple_of(place_ref[replica, 1, row, slot] * tile, tile)
            hi_ref[block, :, pl.ds(column, tile)] = hi
            lo_ref[block, :, pl.ds(column, tile)] = lo
            return carry

        lax.fori_loop(0, count_ref[replica, row], body, 0)


def densify(tiles, place, count, size, pieces):
    own, other = tiles
    tiles_here, slots, tile, _ = own.shape
    rows = tiles_here * tile
    per_call = tiles_here // pieces
    shape = jax.ShapeDtypeStruct((size, rows, rows), BF16)
    dense = ()
    for piece in range(pieces):
        first = piece * per_call
        tile_spec = pl.BlockSpec(
            (1, slots, tile, tile), lambda i, *_, first=first: (first + i, 0, 0, 0)
        )
        out_spec = pl.BlockSpec((size, tile, rows), lambda i, *_, first=first: (0, first + i, 0))
        keep = [pl.BlockSpec(memory_space=pl.ANY)] * len(dense)
        dense = pl.pallas_call(
            functools.partial(densify_kernel, first, slots),
            out_shape=(shape, shape),
            grid_spec=pltpu.PrefetchScalarGridSpec(
                num_scalar_prefetch=2,
                grid=(per_call,),
                in_specs=[tile_spec, tile_spec] + keep,
                out_specs=(out_spec, out_spec),
            ),
            input_output_aliases={4: 0, 5: 1} if dense else {},
            compiler_params=params(),
            cost_estimate=pl.CostEstimate(
                flops=0,
                transcendentals=0,
                bytes_accessed=per_call * tile * (slots * tile * 8 + size * rows * 4),
            ),
            name="densify",
        )(place, count, own, other, *dense)
    return dense


def gather_kernel(blocks, *refs):
    x_refs = refs[: 2 * blocks]
    a_refs = refs[2 * blocks : 4 * blocks]
    rest = refs[4 * blocks :]
    total_ref = rest[0] if len(rest) == 3 else None
    out_ref, x_split = rest[-2:]
    half, width = x_refs[0].shape

    @pl.when(pl.program_id(0) == 0)
    def _():
        for n in range(2 * blocks):
            hi, lo = split_hi_lo(x_refs[n][...])
            x_split[pl.ds(n * half, half), pl.ds(0, width)] = hi
            x_split[pl.ds(n * half, half), pl.ds(width, width)] = lo

    acc = None
    for n in range(blocks):
        span = pl.ds(n * 2 * half, 2 * half)
        both = dot(a_refs[2 * n][0], x_split[span, :])
        low = dot(a_refs[2 * n + 1][0], x_split[span, pl.ds(0, width)])
        part = both[:, :width] + both[:, width:] + low
        acc = part if acc is None else acc + part
    if total_ref is not None:
        acc = acc + total_ref[...]
    out_ref[...] = acc


def gather_product(dense, chunks, total):
    size, rows, columns = dense[0].shape
    half, width = chunks[0][1].shape
    blocks = len(chunks)
    step = 256
    full = pl.BlockSpec((half, width), lambda i: (0, 0))
    in_specs = [full] * (2 * blocks)
    operands = [value for _, top, bottom in chunks for value in (top, bottom)]
    for block, _, _ in chunks:
        spec = pl.BlockSpec((1, step, columns), lambda i, block=block: (block, i, 0))
        in_specs += [spec, spec]
        operands += [dense[0], dense[1]]
    row_spec = pl.BlockSpec((step, width), lambda i: (i, 0))
    if total is not None:
        in_specs.append(row_spec)
        operands.append(total)
    return pl.pallas_call(
        functools.partial(gather_kernel, blocks),
        out_shape=jax.ShapeDtypeStruct((rows, width), F32),
        grid=(rows // step,),
        in_specs=in_specs,
        out_specs=row_spec,
        scratch_shapes=[pltpu.VMEM((blocks * 2 * half, 2 * width), BF16)],
        compiler_params=params(),
        cost_estimate=pl.CostEstimate(
            flops=6 * blocks * rows * columns * width,
            transcendentals=0,
            bytes_accessed=blocks * (rows * columns * 4 + columns * width * 4) + rows * width * 8,
        ),
        name="gather_product",
    )(*operands)


def layer_kernel(own_ref, other_ref, cot_ref, whi_ref, wlo_ref, out_ref, slope_ref, grad_ref):
    width = own_ref.shape[1]
    own_hi, own_lo = split_hi_lo(own_ref[...])
    other_hi, other_lo = split_hi_lo(other_ref[...])
    top, bottom = pl.ds(0, width), pl.ds(width, width)
    pre = dot(own_hi, whi_ref[top, :]) + dot(other_hi, whi_ref[bottom, :])
    pre += dot(own_lo, whi_ref[top, :]) + dot(other_lo, whi_ref[bottom, :])
    pre += dot(own_hi, wlo_ref[top, :]) + dot(other_hi, wlo_ref[bottom, :])
    sigma = jax.nn.sigmoid(pre)
    out_ref[...] = pre * sigma
    grad_pre = cot_ref[...] * (sigma * (1.0 + pre * (1.0 - sigma)))
    slope_ref[...] = grad_pre
    hi, lo = split_hi_lo(grad_pre)
    turned = ((1,), (1,))
    grad = dot(whi_ref[top, :], hi, turned) + dot(whi_ref[top, :], lo, turned)
    grad += dot(wlo_ref[top, :], hi, turned)
    hi, lo = split_hi_lo(grad)
    grad_ref[pl.ds(0, width), :] = hi
    grad_ref[pl.ds(width, width), :] = lo


def layer(own, other, cotangent, w_hi, w_lo):
    rows, width = own.shape
    features = cotangent.shape[1]
    step = 256
    half_spec = pl.BlockSpec((step, width), lambda i: (i, 0))
    full_spec = pl.BlockSpec((step, features), lambda i: (i, 0))
    weight_spec = pl.BlockSpec(w_hi.shape, lambda i: (0, 0))
    return pl.pallas_call(
        layer_kernel,
        out_shape=(
            jax.ShapeDtypeStruct((rows, features), F32),
            jax.ShapeDtypeStruct((rows, features), F32),
            jax.ShapeDtypeStruct((2 * width, rows), BF16),
        ),
        grid=(rows // step,),
        in_specs=[half_spec, half_spec, full_spec, weight_spec, weight_spec],
        out_specs=(full_spec, full_spec, pl.BlockSpec((2 * width, step), lambda i: (0, i))),
        compiler_params=params(),
        cost_estimate=pl.CostEstimate(
            flops=6 * rows * features * (features + width),
            transcendentals=rows * features,
            bytes_accessed=rows * features * 20,
        ),
        name="layer",
    )(own, other, cotangent, w_hi, w_lo)


def scatter_kernel(turn, grad_ref, hi_ref, lo_ref, *refs):
    out_ref = refs[-1]
    width = grad_ref.shape[0] // 2
    both = dot(grad_ref[...], hi_ref[0])
    acc = both[:width] + both[width:] + dot(grad_ref[pl.ds(0, width), :], lo_ref[0])
    if len(refs) == 2:
        acc = acc + refs[0][...]
    out_ref[...] = acc.T if turn else acc


def scatter_product(dense, grad, block, part, parts, carried, turn):
    size, rows, columns = dense[0].shape
    width = grad.shape[0] // 2
    here = columns // parts
    step = 256
    first = part * (here // step)
    a_spec = pl.BlockSpec((1, rows, step), lambda i: (block, 0, first + i))
    in_specs = [pl.BlockSpec(grad.shape, lambda i: (0, 0)), a_spec, a_spec]
    operands = [grad, dense[0], dense[1]]
    if carried is not None:
        in_specs.append(pl.BlockSpec((width, step), lambda i: (0, i)))
        operands.append(carried)
    if turn:
        out_shape, out_spec = (here, width), pl.BlockSpec((step, width), lambda i: (i, 0))
    else:
        out_shape, out_spec = (width, here), pl.BlockSpec((width, step), lambda i: (0, i))
    return pl.pallas_call(
        functools.partial(scatter_kernel, turn),
        out_shape=jax.ShapeDtypeStruct(out_shape, F32),
        grid=(here // step,),
        in_specs=in_specs,
        out_specs=out_spec,
        compiler_params=params(),
        cost_estimate=pl.CostEstimate(
            flops=6 * rows * here * width,
            transcendentals=0,
            bytes_accessed=rows * here * 4 + rows * width * 4 + here * width * 8,
        ),
        name="scatter_product",
    )(*operands)


def sum_over_row(value, size):
    me = lax.axis_index("row")
    half = value.shape[0] // 2
    odd = me % 2

    def swap(block, distance):
        return lax.ppermute(block, "row", [(i, i ^ distance) for i in range(size)])

    top, bottom = value[:half], value[half:]
    mine = jnp.where(odd == 0, top, bottom)
    sent = jnp.where(odd == 0, bottom, top)
    mine = mine + swap(sent, 1)
    distance = 2
    while distance < size:
        mine = mine + swap(mine, distance)
        distance *= 2
    theirs = swap(mine, 1)
    low = jnp.where(odd == 0, mine, theirs)
    high = jnp.where(odd == 0, theirs, mine)
    return jnp.concatenate([low, high], 0)


def per_device(features, weight, cotangent, tile_vals, col_tile, counts):
    size = lax.axis_size("row")
    hops = size // 2
    rep = lax.axis_index("rep")
    row = lax.axis_index("row")
    tiles_here = tile_vals.shape[0]
    width = features.shape[1] // 2
    half = features.shape[0] // 2
    ahead, back = ring_pairs(size)

    def forth(block):
        return lax.ppermute(block, "row", ahead)

    def rear(block):
        return lax.ppermute(block, "row", back)

    def swap(block):
        return lax.ppermute(block, "rep", [(0, 1), (1, 0)])

    def order(own, other, axis):
        low = jnp.where(rep == 0, own, other)
        high = jnp.where(rep == 0, other, own)
        return jnp.concatenate([low, high], axis)

    mine = jnp.where(rep == 0, features[:, :width], features[:, width:])
    top, bottom = mine[:half], mine[half:]

    got = [{0: (top, bottom)}]
    forward_top, forward_bottom, rear_top, rear_bottom = top, bottom, top, bottom
    for hop in range(1, hops + 1):
        forward_top = forth(forward_top)
        rear_bottom = rear(rear_bottom)
        if hop < hops:
            forward_bottom = forth(forward_bottom)
            rear_top = rear(rear_top)
            got.append(
                {size - hop: (forward_top, forward_bottom), hop: (rear_top, rear_bottom)}
            )
        else:
            got.append({hop: (forward_top, rear_bottom)})

    own_tiles = tile_vals[:, 0]
    other_tiles = swap(own_tiles)
    own_columns = col_tile[:, 0]
    columns = jnp.stack([own_columns, swap(own_columns)])
    block = jnp.mod(ring_place(columns // tiles_here, size) - ring_place(row, size), size)
    place = jnp.stack([block, columns % tiles_here], 1)
    count = jnp.stack([counts[:, 0], swap(counts[:, 0])])
    dense = densify((own_tiles, other_tiles), place, count, size, 4)

    w_own = jnp.where(rep == 0, weight[:width], weight[width:])
    w_other = jnp.where(rep == 0, weight[width:], weight[:width])
    w_rows = jnp.concatenate([w_own, w_other], 0)
    w_high = lax.reduce_precision(w_rows, 8, 7)
    w_hi, w_lo = w_high.astype(BF16), (w_rows - w_high).astype(BF16)

    total = None
    for arrived in got:
        chunks = [(block, first, second) for block, (first, second) in arrived.items()]
        total = gather_product(dense, chunks, total)
    output, grad_pre, grad = layer(total, swap(total), cotangent, w_hi, w_lo)

    def product(block, part, carried=None, turn=False):
        return scatter_product(dense, grad, block, part, 2, carried, turn)

    forward_top = rear_bottom = forward_bottom = rear_top = None
    for hop in range(hops, 0, -1):
        turn = hop == 1
        if hop < hops:
            forward_bottom = forth(product(hop, 1, forward_bottom, turn))
            rear_top = rear(product(size - hop, 0, rear_top, turn))
        forward_top = forth(product(hop, 0, forward_top, turn))
        rear_bottom = rear(product(size - hop, 1, rear_bottom, turn))

    weight_part = lax.dot_general(
        total,
        grad_pre,
        (((0,), (0,)), ((), ())),
        precision=lax.Precision.HIGH,
        preferred_element_type=F32,
    )
    weight_half = sum_over_row(weight_part, size)
    weight_grad = order(weight_half, swap(weight_half), 0)

    home_top = product(0, 0, None, True) + forward_top + rear_top
    home_bottom = product(0, 1, None, True) + forward_bottom + rear_bottom
    input_grad = jnp.concatenate(
        [order(home_top, swap(home_top), 1), order(home_bottom, swap(home_bottom), 1)], 0
    )
    return (output, input_grad, weight_grad)


def solution(mesh):
    return jax.shard_map(
        per_device,
        mesh=mesh,
        in_specs=(
            P(("groups", "row"), None),
            P(),
            P(("groups", "row"), None),
            P(("groups", "row"), "rep", None, None, None),
            P(("groups", "row"), "rep", None),
            P(("groups", "row"), "rep"),
        ),
        out_specs=(P(("groups", "row"), None), P(("groups", "row"), None), P("groups", None)),
        check_vma=False,
    )
```

time: 707 us -> 268 us (0.38)
  waiting for transfers between devices: 499 us -> 77.5 us
  Pallas kernels: 0 us -> 129 us
  matrix products: 88.5 us -> 1.02 us
  local copies, waits for them, and re-layouts: 45.8 us -> 12.2 us
  other arithmetic: 38.5 us -> 7.48 us
  starting transfers between devices: 20.7 us -> 38.6 us
  between operations: 13.8 us -> 0.97 us
    ppermute x8 -> x39, waiting for transfers between devices: 395 us -> 77.5 us  [the longest x14 53.5 us: forth(): return lax.ppermute(block, 'row', ahead)]
    pallas_call x0 -> x26, Pallas kernels: none -> 129 us  [the longest x16 59.3 us: scatter_product(): pl.pallas_call(functools.partial(scatter_kernel, turn), out_shape=jax.Sha...]
    psum x3 -> x0, waiting for transfers between devices: 104 us -> none  [the longest x1 62.3 us: per_device(): weight_grad = lax.psum(weight_part, ('row', 'rep'))]
    dot_general x11 -> x1, matrix products: 88.5 us -> 1.02 us  [per_device(): lax.dot_general(total, grad_pre, (((0,), (0,)), ((), ())), precision=lax....]
    scatter-add x1 -> x0, other arithmetic: 27.5 us -> none  [densify(): placed = placed.at[row_ids, position].add(tile_block)]
    ppermute x8 -> x39, starting transfers between devices: 20.5 us -> 38.6 us  [the longest x14 25.2 us: forth(): return lax.ppermute(block, 'row', ahead)]
    transpose x1 -> x0, local copies, waits for them, and re-layouts: 15.2 us -> none  [densify(): placed.transpose(0, 2, 1, 3)]
    while x15 -> x0, local copies, waits for them, and re-layouts: 7.91 us -> none
  transfers between devices with their start and end apart: 11 -> 39, of which waited for: 11 -> 14; matrix products, arithmetic and copies ran while one was open for 11% -> 3% of each run, Pallas kernels for 0% -> 41%
where the time goes in v1:
time: 268 us; the launch traced here: 266 us
  Pallas kernels  129 us (48%)
  waiting for transfers between devices  77.5 us (29%)
  starting transfers between devices  38.6 us (14%)
  local copies, waits for them, and re-layouts  12.2 us (5%)
  other arithmetic  7.48 us (3%)
    pallas_call x16, Pallas kernels, scatter_product(): pl.pallas_call(functools.partial(scatter_kernel, turn), out_shape=jax.Sha...  59.3 us
    ppermute x14, waiting for transfers between devices, forth(): return lax.ppermute(block, 'row', ahead)  53.5 us
    pallas_call x5, Pallas kernels, gather_product(): pl.pallas_call(functools.partial(gather_kernel, blocks), out_shape=jax.Sh...  37 us
    ppermute x14, starting transfers between devices, forth(): return lax.ppermute(block, 'row', ahead)  25.2 us
    pallas_call x4, Pallas kernels, densify(): pl.pallas_call(functools.partial(densify_kernel, first, slots), out_shape...  24.7 us
    ppermute x4, waiting for transfers between devices, swap(): return lax.ppermute(block, 'row', [(i, i ^ distance) for i in range(size)])  12.9 us
    unnamed x58, local copies, waits for them, and re-layouts  12.1 us
    ppermute x7, waiting for transfers between devices, swap(): return lax.ppermute(block, 'rep', [(0, 1), (1, 0)])  10.1 us
  transfers between devices with their start and end apart: 39, of which 14 were waited for; matrix products, arithmetic and copies ran while one was open for 3% of the time, Pallas kernels for 41%

profile of v1, /device:TPU:0, one launch (start us, length us, event | category | flops | bytes accessed | tf_op | source)
XLA Modules:
  0.0 266.4 jit_solution(1373107558358829855)
XLA Ops:
  3.0 2.6 collective-permute-start
  6.1 7.8 %collective-permute-done.9 = s32[8]{0:T(128)S(1)} collective-permute-done((s32[8]{0:T(128)S(1)}, s32[8]{0:T(128)S(1)}, u32[]{:S(2)}, u32[]{:S(2)}) %collective-permute-start.9) | collective-permute-done | bytes 64 | tf_op jit(solution)/shard_map/ppermute | solution.py:287
  13.9 2.9 %collective-permute-start.11 = (f32[512,256]{1,0:T(8,128)S(1)}, f32[512,256]{1,0:T(8,128)S(1)}, u32[]{:S(2)}, u32[]{:S(2)}) collective-permute-start(f32[512,256]{1,0:T(8,128)S(1)} %get-tuple-element.35.refs_1_), channel_id=1, source_target_pairs={{0,4},{4,8},{8,12},{12,14},{14,10},{10,6},{6,2},{2,0},{1,5},{5,9},... | collective-permute-start | bytes 1572872 | tf_op jit(solution)/shard_map/ppermute | solution.py:281
  20.4 9.3 %collective-permute-done.11.refs_1_ = f32[512,256]{1,0:T(8,128)S(1)} collective-permute-done((f32[512,256]{1,0:T(8,128)S(1)}, f32[512,256]{1,0:T(8,128)S(1)}, u32[]{:S(2)}, u32[]{:S(2)}) %collective-permute-start.11) | collective-permute-done | bytes 524320 | tf_op jit(solution)/shard_map/ppermute | solution.py:281
  29.7 2.0 collective-permute-start.12
  31.7 9.3 %collective-permute-done.1.refs_0_ = f32[512,256]{1,0:T(8,128)} collective-permute-done((f32[512,256]{1,0:T(8,128)S(1)}, f32[512,256]{1,0:T(8,128)}, u32[]{:S(2)}, u32[]{:S(2)}) %collective-permute-start.1) | collective-permute-done | bytes 524320 | tf_op jit(solution)/shard_map/ppermute | solution.py:281
  41.0 2.0 collective-permute-start.2
  44.2 8.0 %collective-permute-done.12.refs_1_ = f32[512,256]{1,0:T(8,128)} collective-permute-done((f32[512,256]{1,0:T(8,128)S(1)}, f32[512,256]{1,0:T(8,128)}, u32[]{:S(2)}, u32[]{:S(2)}) %collective-permute-start.12) | collective-permute-done | bytes 524320 | tf_op jit(solution)/shard_map/ppermute | solution.py:281
  52.2 2.0 collective-permute-start.13
  54.3 9.2 %collective-permute-done.2.refs_0_ = f32[512,256]{1,0:T(8,128)} collective-permute-done((f32[512,256]{1,0:T(8,128)}, f32[512,256]{1,0:T(8,128)}, u32[]{:S(2)}, u32[]{:S(2)}) %collective-permute-start.2) | collective-permute-done | bytes 524320 | tf_op jit(solution)/shard_map/ppermute | solution.py:281
  63.5 2.0 collective-permute-start.3
  65.5 6.1 %densify.4 = (bf16[8,1024,1024]{2,1,0:T(8,128)(2,1)}, bf16[8,1024,1024]{2,1,0:T(8,128)(2,1)}) custom-call(s32[2,2,8,16]{3,2,1,0:T(8,128)} %pad_add_fusion.place_ref, s32[2,8]{1,0:T(2,128)} %pad_add_fusion.2.count_ref, f32[8,16,128,128]{3,2,1,0:T(8,128)} %bitcast.10, f32[8,16,128,128]{3,2,1,0:T(8,128)} %collective-permute-done.10.other_ref), custom_call_target="tpu_custom_call" | custom-call | bytes 12582912 | tf_op jit(solution)/shard_map/densify/pallas_call | solution.py:77
  71.6 6.2 %densify.5 = (bf16[8,1024,1024]{2,1,0:T(8,128)(2,1)}, bf16[8,1024,1024]{2,1,0:T(8,128)(2,1)}) custom-call(s32[2,2,8,16]{3,2,1,0:T(8,128)} %pad_add_fusion.place_ref, s32[2,8]{1,0:T(2,128)} %pad_add_fusion.2.count_ref, f32[8,16,128,128]{3,2,1,0:T(8,128)} %bitcast.11, ...), custom_call_target="tpu_custom_call", output_to_operand_aliasing={{0}: (4, {}), {1}: (5, {})} | custom-call | bytes 12582912 | tf_op jit(solution)/shard_map/densify/pallas_call | solution.py:77
  77.8 6.2 %densify.6 = (bf16[8,1024,1024]{2,1,0:T(8,128)(2,1)}, bf16[8,1024,1024]{2,1,0:T(8,128)(2,1)}) custom-call(s32[2,2,8,16]{3,2,1,0:T(8,128)} %pad_add_fusion.place_ref, s32[2,8]{1,0:T(2,128)} %pad_add_fusion.2.count_ref, f32[8,16,128,128]{3,2,1,0:T(8,128)} %bitcast.12, ...), custom_call_target="tpu_custom_call", output_to_operand_aliasing={{0}: (4, {}), {1}: (5, {})} | custom-call | bytes 12582912 | tf_op jit(solution)/shard_map/densify/pallas_call | solution.py:77
  84.0 6.2 %densify.7 = (bf16[8,1024,1024]{2,1,0:T(8,128)(2,1)}, bf16[8,1024,1024]{2,1,0:T(8,128)(2,1)}) custom-call(s32[2,2,8,16]{3,2,1,0:T(8,128)} %pad_add_fusion.place_ref, s32[2,8]{1,0:T(2,128)} %pad_add_fusion.2.count_ref, f32[8,16,128,128]{3,2,1,0:T(8,128)} %bitcast.13, ...), custom_call_target="tpu_custom_call", output_to_operand_aliasing={{0}: (4, {}), {1}: (5, {})} | custom-call | bytes 12582912 | tf_op jit(solution)/shard_map/densify/pallas_call | solution.py:77
  90.3 5.6 %gather_product.5.refs_8_ = f32[1024,256]{1,0:T(8,128)} custom-call(f32[512,256]{1,0:T(8,128)} %copy-done.2, f32[512,256]{1,0:T(8,128)} %copy-done.1, bf16[8,1024,1024]{2,1,0:T(8,128)(2,1)} %get-tuple-element.20.refs_2_.refs_4_.refs_6_.hi_ref, bf16[8,1024,1024]{2,1,0:T(8,128)(2,1)} %get-tuple-element.21.refs_3_.refs_5_.refs_7_.lo_ref), custom_call_target="tpu_custom_call" | custom-call | flops 1610612736 | bytes 7340032 | tf_op jit(solution)/shard_map/gather_product/pallas_call | solution.py:141
  95.8 8.6 %gather_product.6.refs_8_ = f32[1024,256]{1,0:T(8,128)} custom-call(f32[512,256]{1,0:T(8,128)} %copy-done.7, f32[512,256]{1,0:T(8,128)} %copy-done.9, f32[512,256]{1,0:T(8,128)} %copy-done.10, f32[512,256]{1,0:T(8,128)} %copy-done.8, bf16[8,1024,1024]{2,1,0:T(8,128)(2,1)} %get-tuple-element.20.refs_2_.refs_4_.refs_6_.hi_ref, ...), custom_call_target="tpu_custom_call" | custom-call | flops 3221225472 | bytes 12582912 | tf_op jit(solution)/shard_map/gather_product/pallas_call | solution.py:141
  104.5 8.5 %gather_product.7.refs_8_ = f32[1024,256]{1,0:T(8,128)} custom-call(f32[512,256]{1,0:T(8,128)} %collective-permute-done.1.refs_0_, f32[512,256]{1,0:T(8,128)} %collective-permute-done.12.refs_1_, f32[512,256]{1,0:T(8,128)} %collective-permute-done.15.refs_2_, f32[512,256]{1,0:T(8,128)} %collective-permute-done.5.refs_3_, ...), custom_call_target="tpu_custom_call" | custom-call | flops 3221225472 | bytes 12582912 | tf_op jit(solution)/shard_map/gather_product/pallas_call | solution.py:141
  114.6 8.5 %gather_product.8.refs_4_ = f32[1024,256]{1,0:T(8,128)} custom-call(f32[512,256]{1,0:T(8,128)} %collective-permute-done.2.refs_0_, f32[512,256]{1,0:T(8,128)} %copy-done.11, f32[512,256]{1,0:T(8,128)} %copy-done.13, f32[512,256]{1,0:T(8,128)} %collective-permute-done.6.refs_3_, bf16[8,1024,1024]{2,1,0:T(8,128)(2,1)} %get-tuple-element.20.refs_2_.refs_4_.refs_6_.hi_ref, ...), custom_call_target="tpu_custom_call" | custom-call | flops 3221225472 | bytes 12582912 | tf_op jit(solution)/shard_map/gather_product/pallas_call | solution.py:141
  124.7 5.9 %gather_product.9.own_ref = f32[1024,256]{1,0:T(8,128)} custom-call(f32[512,256]{1,0:T(8,128)} %copy-done.12, f32[512,256]{1,0:T(8,128)} %copy-done.14, bf16[8,1024,1024]{2,1,0:T(8,128)(2,1)} %get-tuple-element.20.refs_2_.refs_4_.refs_6_.hi_ref, bf16[8,1024,1024]{2,1,0:T(8,128)(2,1)} %get-tuple-element.21.refs_3_.refs_5_.refs_7_.lo_ref, ...), custom_call_target="tpu_custom_call" | custom-call | flops 1610612736 | bytes 7340032 | tf_op jit(solution)/shard_map/gather_product/pallas_call | solution.py:141
  134.4 7.6 %layer.1 = (f32[1024,512]{1,0:T(8,128)}, f32[1024,512]{1,0:T(8,128)}, bf16[512,1024]{1,0:T(8,128)(2,1)}) custom-call(f32[1024,256]{1,0:T(8,128)} %gather_product.9.own_ref, f32[1024,256]{1,0:T(8,128)} %copy-done.28, f32[1024,512]{1,0:T(8,128)} %cot_ref.1, bf16[512,512]{1,0:T(8,128)(2,1)} %get-tuple-element.32.whi_ref, bf16[512,512]{1,0:T(8,128)(2,1)} %get-tuple-element.31.wlo_ref), custom_call_target="tpu_custom_call" | custom-call | flops 2415919104 | bytes 10485760 | tf_op jit(solution)/shard_map/layer/pallas_call | solution.py:186
  142.0 3.6 %scatter_product.17 = f32[256,512]{1,0:T(8,128)} custom-call(bf16[512,1024]{1,0:T(8,128)(2,1)} %get-tuple-element.23.grad_ref, bf16[8,1024,1024]{2,1,0:T(8,128)(2,1)} %get-tuple-element.20.refs_2_.refs_4_.refs_6_.hi_ref, bf16[8,1024,1024]{2,1,0:T(8,128)(2,1)} %get-tuple-element.21.refs_3_.refs_5_.refs_7_.lo_ref), custom_call_target="tpu_custom_call" | custom-call | flops 805306368 | bytes 4194304 | tf_op jit(solution)/shard_map/scatter_product/pallas_call | solution.py:232
  145.6 3.6 %scatter_product.28 = f32[256,512]{1,0:T(8,128)} custom-call(bf16[512,1024]{1,0:T(8,128)(2,1)} %get-tuple-element.23.grad_ref, bf16[8,1024,1024]{2,1,0:T(8,128)(2,1)} %get-tuple-element.20.refs_2_.refs_4_.refs_6_.hi_ref, bf16[8,1024,1024]{2,1,0:T(8,128)(2,1)} %get-tuple-element.21.refs_3_.refs_5_.refs_7_.lo_ref), custom_call_target="tpu_custom_call" | custom-call | flops 805306368 | bytes 4194304 | tf_op jit(solution)/shard_map/scatter_product/pallas_call | solution.py:232
  149.3 2.4 collective-permute-start.18
  153.3 1.9 collective-permute-start.34
  155.2 3.6 %scatter_product.21 = f32[256,512]{1,0:T(8,128)} custom-call(bf16[512,1024]{1,0:T(8,128)(2,1)} %get-tuple-element.23.grad_ref, bf16[8,1024,1024]{2,1,0:T(8,128)(2,1)} %get-tuple-element.20.refs_2_.refs_4_.refs_6_.hi_ref, bf16[8,1024,1024]{2,1,0:T(8,128)(2,1)} %get-tuple-element.21.refs_3_.refs_5_.refs_7_.lo_ref), custom_call_target="tpu_custom_call" | custom-call | flops 805306368 | bytes 4194304 | tf_op jit(solution)/shard_map/scatter_product/pallas_call | solution.py:232
  159.0 5.7 %collective-permute-done.18.refs_0_ = f32[256,512]{1,0:T(8,128)S(1)} collective-permute-done((f32[256,512]{1,0:T(8,128)S(1)}, f32[256,512]{1,0:T(8,128)S(1)}, u32[]{:S(2)}, u32[]{:S(2)}) %collective-permute-start.18) | collective-permute-done | bytes 524320 | tf_op jit(solution)/shard_map/ppermute | solution.py:281
  165.5 3.7 %scatter_product.18 = f32[256,512]{1,0:T(8,128)} custom-call(bf16[512,1024]{1,0:T(8,128)(2,1)} %get-tuple-element.23.grad_ref, bf16[8,1024,1024]{2,1,0:T(8,128)(2,1)} %get-tuple-element.20.refs_2_.refs_4_.refs_6_.hi_ref, bf16[8,1024,1024]{2,1,0:T(8,128)(2,1)} %get-tuple-element.21.refs_3_.refs_5_.refs_7_.lo_ref, f32[256,512]{1,0:T(8,128)} %copy-done.25), custom_call_target="tpu_custom_call" | custom-call | flops 805306368 | bytes 4194304 | tf_op jit(solution)/shard_map/scatter_product/pallas_call | solution.py:232
  170.2 3.5 %scatter_product.25 = f32[256,512]{1,0:T(8,128)} custom-call(bf16[512,1024]{1,0:T(8,128)(2,1)} %get-tuple-element.23.grad_ref, bf16[8,1024,1024]{2,1,0:T(8,128)(2,1)} %get-tuple-element.20.refs_2_.refs_4_.refs_6_.hi_ref, bf16[8,1024,1024]{2,1,0:T(8,128)(2,1)} %get-tuple-element.21.refs_3_.refs_5_.refs_7_.lo_ref), custom_call_target="tpu_custom_call" | custom-call | flops 805306368 | bytes 4194304 | tf_op jit(solution)/shard_map/scatter_product/pallas_call | solution.py:232
  175.9 3.7 %scatter_product.29 = f32[256,512]{1,0:T(8,128)} custom-call(bf16[512,1024]{1,0:T(8,128)(2,1)} %get-tuple-element.23.grad_ref, bf16[8,1024,1024]{2,1,0:T(8,128)(2,1)} %get-tuple-element.20.refs_2_.refs_4_.refs_6_.hi_ref, bf16[8,1024,1024]{2,1,0:T(8,128)(2,1)} %get-tuple-element.21.refs_3_.refs_5_.refs_7_.lo_ref, f32[256,512]{1,0:T(8,128)} %copy-done.23), custom_call_target="tpu_custom_call" | custom-call | flops 805306368 | bytes 4194304 | tf_op jit(solution)/shard_map/scatter_product/pallas_call | solution.py:232
  182.6 3.7 %scatter_product.22 = f32[256,512]{1,0:T(8,128)} custom-call(bf16[512,1024]{1,0:T(8,128)(2,1)} %get-tuple-element.23.grad_ref, bf16[8,1024,1024]{2,1,0:T(8,128)(2,1)} %get-tuple-element.20.refs_2_.refs_4_.refs_6_.hi_ref, bf16[8,1024,1024]{2,1,0:T(8,128)(2,1)} %get-tuple-element.21.refs_3_.refs_5_.refs_7_.lo_ref, f32[256,512]{1,0:T(8,128)} %copy-done.21), custom_call_target="tpu_custom_call" | custom-call | flops 805306368 | bytes 4194304 | tf_op jit(solution)/shard_map/scatter_product/pallas_call | solution.py:232
  186.3 2.3 collective-permute-start.23
  189.4 3.7 %scatter_product.19 = f32[256,512]{1,0:T(8,128)} custom-call(bf16[512,1024]{1,0:T(8,128)(2,1)} %get-tuple-element.23.grad_ref, bf16[8,1024,1024]{2,1,0:T(8,128)(2,1)} %get-tuple-element.20.refs_2_.refs_4_.refs_6_.hi_ref, bf16[8,1024,1024]{2,1,0:T(8,128)(2,1)} %get-tuple-element.21.refs_3_.refs_5_.refs_7_.lo_ref, f32[256,512]{1,0:T(8,128)} %copy-done.22), custom_call_target="tpu_custom_call" | custom-call | flops 805306368 | bytes 4194304 | tf_op jit(solution)/shard_map/scatter_product/pallas_call | solution.py:232
  194.9 3.7 %scatter_product.26 = f32[256,512]{1,0:T(8,128)} custom-call(bf16[512,1024]{1,0:T(8,128)(2,1)} %get-tuple-element.23.grad_ref, bf16[8,1024,1024]{2,1,0:T(8,128)(2,1)} %get-tuple-element.20.refs_2_.refs_4_.refs_6_.hi_ref, bf16[8,1024,1024]{2,1,0:T(8,128)(2,1)} %get-tuple-element.21.refs_3_.refs_5_.refs_7_.lo_ref, f32[256,512]{1,0:T(8,128)} %copy-done.19), custom_call_target="tpu_custom_call" | custom-call | flops 805306368 | bytes 4194304 | tf_op jit(solution)/shard_map/scatter_product/pallas_call | solution.py:232
  198.6 2.4 collective-permute-start.27
  201.8 3.7 %scatter_product.30 = f32[256,512]{1,0:T(8,128)} custom-call(bf16[512,1024]{1,0:T(8,128)(2,1)} %get-tuple-element.23.grad_ref, bf16[8,1024,1024]{2,1,0:T(8,128)(2,1)} %get-tuple-element.20.refs_2_.refs_4_.refs_6_.hi_ref, bf16[8,1024,1024]{2,1,0:T(8,128)(2,1)} %get-tuple-element.21.refs_3_.refs_5_.refs_7_.lo_ref, f32[256,512]{1,0:T(8,128)} %copy-done.20), custom_call_target="tpu_custom_call" | custom-call | flops 805306368 | bytes 4194304 | tf_op jit(solution)/shard_map/scatter_product/pallas_call | solution.py:232
  205.8 2.5 collective-permute-start.36
  208.4 3.7 %scatter_product.16 = f32[512,256]{1,0:T(8,128)} custom-call(bf16[512,1024]{1,0:T(8,128)(2,1)} %get-tuple-element.23.grad_ref, bf16[8,1024,1024]{2,1,0:T(8,128)(2,1)} %get-tuple-element.20.refs_2_.refs_4_.refs_6_.hi_ref, bf16[8,1024,1024]{2,1,0:T(8,128)(2,1)} %get-tuple-element.21.refs_3_.refs_5_.refs_7_.lo_ref), custom_call_target="tpu_custom_call" | custom-call | flops 805306368 | bytes 4194304 | tf_op jit(solution)/shard_map/scatter_product/pallas_call | solution.py:232
  212.1 3.6 %scatter_product.24 = f32[512,256]{1,0:T(8,128)} custom-call(bf16[512,1024]{1,0:T(8,128)(2,1)} %get-tuple-element.23.grad_ref, bf16[8,1024,1024]{2,1,0:T(8,128)(2,1)} %get-tuple-element.20.refs_2_.refs_4_.refs_6_.hi_ref, bf16[8,1024,1024]{2,1,0:T(8,128)(2,1)} %get-tuple-element.21.refs_3_.refs_5_.refs_7_.lo_ref), custom_call_target="tpu_custom_call" | custom-call | flops 805306368 | bytes 4194304 | tf_op jit(solution)/shard_map/scatter_product/pallas_call | solution.py:232
  215.7 12.8 %collective-permute-done.36 = f32[128,512]{1,0:T(8,128)S(1)} collective-permute-done((f32[128,512]{1,0:T(8,128)S(1)}, f32[128,512]{1,0:T(8,128)S(1)}, u32[]{:S(2)}, u32[]{:S(2)}) %collective-permute-start.36) | collective-permute-done | bytes 262176 | tf_op jit(solution)/shard_map/ppermute | solution.py:254
  229.4 3.8 %scatter_product.23 = f32[512,256]{1,0:T(8,128)} custom-call(bf16[512,1024]{1,0:T(8,128)(2,1)} %get-tuple-element.23.grad_ref, bf16[8,1024,1024]{2,1,0:T(8,128)(2,1)} %get-tuple-element.20.refs_2_.refs_4_.refs_6_.hi_ref, bf16[8,1024,1024]{2,1,0:T(8,128)(2,1)} %get-tuple-element.21.refs_3_.refs_5_.refs_7_.lo_ref, f32[256,512]{1,0:T(8,128)} %copy-done.16), custom_call_target="tpu_custom_call" | custom-call | flops 805306368 | bytes 4194304 | tf_op jit(solution)/shard_map/scatter_product/pallas_call | solution.py:232
  233.3 2.0 collective-permute-start.24
  236.1 3.8 %scatter_product.20 = f32[512,256]{1,0:T(8,128)} custom-call(bf16[512,1024]{1,0:T(8,128)(2,1)} %get-tuple-element.23.grad_ref, bf16[8,1024,1024]{2,1,0:T(8,128)(2,1)} %get-tuple-element.20.refs_2_.refs_4_.refs_6_.hi_ref, bf16[8,1024,1024]{2,1,0:T(8,128)(2,1)} %get-tuple-element.21.refs_3_.refs_5_.refs_7_.lo_ref, f32[256,512]{1,0:T(8,128)} %copy-done.17), custom_call_target="tpu_custom_call" | custom-call | flops 805306368 | bytes 4194304 | tf_op jit(solution)/shard_map/scatter_product/pallas_call | solution.py:232
  241.3 3.9 %scatter_product.27 = f32[512,256]{1,0:T(8,128)} custom-call(bf16[512,1024]{1,0:T(8,128)(2,1)} %get-tuple-element.23.grad_ref, bf16[8,1024,1024]{2,1,0:T(8,128)(2,1)} %get-tuple-element.20.refs_2_.refs_4_.refs_6_.hi_ref, bf16[8,1024,1024]{2,1,0:T(8,128)(2,1)} %get-tuple-element.21.refs_3_.refs_5_.refs_7_.lo_ref, f32[256,512]{1,0:T(8,128)} %copy-done.18), custom_call_target="tpu_custom_call" | custom-call | flops 805306368 | bytes 4194304 | tf_op jit(solution)/shard_map/scatter_product/pallas_call | solution.py:232
  245.1 2.0 collective-permute-start.28
  248.0 3.8 %scatter_product.31 = f32[512,256]{1,0:T(8,128)} custom-call(bf16[512,1024]{1,0:T(8,128)(2,1)} %get-tuple-element.23.grad_ref, bf16[8,1024,1024]{2,1,0:T(8,128)(2,1)} %get-tuple-element.20.refs_2_.refs_4_.refs_6_.hi_ref, bf16[8,1024,1024]{2,1,0:T(8,128)(2,1)} %get-tuple-element.21.refs_3_.refs_5_.refs_7_.lo_ref, f32[256,512]{1,0:T(8,128)} %copy-done.15), custom_call_target="tpu_custom_call" | custom-call | flops 805306368 | bytes 4194304 | tf_op jit(solution)/shard_map/scatter_product/pallas_call | solution.py:232
  252.0 3.0 %collective-permute-done.21 = f32[512,256]{1,0:T(8,128)S(1)} collective-permute-done((f32[512,256]{1,0:T(8,128)}, f32[512,256]{1,0:T(8,128)S(1)}, u32[]{:S(2)}, u32[]{:S(2)}) %collective-permute-start.21) | collective-permute-done | bytes 524320 | tf_op jit(solution)/shard_map/ppermute | solution.py:281
  255.2 6.6 %collective-permute-done.28 = f32[512,256]{1,0:T(8,128)S(1)} collective-permute-done((f32[512,256]{1,0:T(8,128)}, f32[512,256]{1,0:T(8,128)S(1)}, u32[]{:S(2)}, u32[]{:S(2)}) %collective-permute-start.28) | collective-permute-done | bytes 524320 | tf_op jit(solution)/shard_map/ppermute | solution.py:281
  (135 shorter events, 36.1 us)
Async XLA Ops:
  0.6 64.9 %collective-permute-start.10 = (f32[8,16,128,128]{3,2,1,0:T(8,128)}, f32[8,16,128,128]{3,2,1,0:T(8,128)}, u32[]{:S(2)}, u32[]{:S(2)}) collective-permute-start(f32[8,16,128,128]{3,2,1,0:T(8,128)} %bitcast.9), channel_id=1, source_target_pairs={{0,1},{1,0},{2,3},{3,2},{4,5},{5,4},{6,7},{7,6},{8,9},{9,8},{10,11... | collective-permute-start | bytes 25165832 | tf_op jit(solution)/shard_map/ppermute | solution.py:287
  2.9 68.7 %copy-start.1 = (f32[512,256]{1,0:T(8,128)}, f32[512,256]{1,0:T(8,128)S(1)}, u32[]{:S(2)}) copy-start(f32[512,256]{1,0:T(8,128)S(1)} %get-tuple-element.35.refs_1_) | copy-start | bytes 1572868
  2.9 68.7 %copy-start.2 = (f32[512,256]{1,0:T(8,128)}, f32[512,256]{1,0:T(8,128)S(1)}, u32[]{:S(2)}) copy-start(f32[512,256]{1,0:T(8,128)S(1)} %get-tuple-element.36.refs_0_) | copy-start | bytes 1572868
  3.0 15.4 %collective-permute-start = (f32[512,256]{1,0:T(8,128)S(1)}, f32[512,256]{1,0:T(8,128)S(1)}, u32[]{:S(2)}, u32[]{:S(2)}) collective-permute-start(f32[512,256]{1,0:T(8,128)S(1)} %get-tuple-element.36.refs_0_), channel_id=1, source_target_pairs={{0,4},{4,8},{8,12},{12,14},{14,10},{10,6},{6,2},{2,0},{1,5},{5,9},... | collective-permute-start | bytes 1572872 | tf_op jit(solution)/shard_map/ppermute | solution.py:281
  5.6 14.6 %collective-permute-start.4 = (f32[512,256]{1,0:T(8,128)S(1)}, f32[512,256]{1,0:T(8,128)S(1)}, u32[]{:S(2)}, u32[]{:S(2)}) collective-permute-start(f32[512,256]{1,0:T(8,128)S(1)} %get-tuple-element.35.refs_1_), channel_id=1, source_target_pairs={{4,0},{8,4},{12,8},{14,12},{10,14},{6,10},{2,6},{0,2},{5,1},{9,5},... | collective-permute-start | bytes 1572872 | tf_op jit(solution)/shard_map/ppermute | solution.py:284
  5.6 11.3 %collective-permute-start.8 = (s32[8,16]{1,0:T(8,128)S(1)}, s32[8,16]{1,0:T(8,128)S(1)}, u32[]{:S(2)}, u32[]{:S(2)}) collective-permute-start(s32[8,16]{1,0:T(8,128)S(1)} %bitcast.14), channel_id=1, source_target_pairs={{0,1},{1,0},{2,3},{3,2},{4,5},{5,4},{6,7},{7,6},{8,9},{9,8},{10,11... | collective-permute-start | bytes 1544 | tf_op jit(solution)/shard_map/ppermute | solution.py:287
  5.8 8.1 %collective-permute-start.9 = (s32[8]{0:T(128)S(1)}, s32[8]{0:T(128)S(1)}, u32[]{:S(2)}, u32[]{:S(2)}) collective-permute-start(s32[8]{0:T(128)S(1)} %bitcast.17), channel_id=1, source_target_pairs={{0,1},{1,0},{2,3},{3,2},{4,5},{5,4},{6,7},{7,6},{8,9},{9,8},{10,11... | collective-permute-start | bytes 104 | tf_op jit(solution)/shard_map/ppermute | solution.py:287
  13.9 15.7 %collective-permute-start.11 = (f32[512,256]{1,0:T(8,128)S(1)}, f32[512,256]{1,0:T(8,128)S(1)}, u32[]{:S(2)}, u32[]{:S(2)}) collective-permute-start(f32[512,256]{1,0:T(8,128)S(1)} %get-tuple-element.35.refs_1_), channel_id=1, source_target_pairs={{0,4},{4,8},{8,12},{12,14},{14,10},{10,6},{6,2},{2,0},{1,5},{5,9},... | collective-permute-start | bytes 1572872 | tf_op jit(solution)/shard_map/ppermute | solution.py:281
  16.9 14.8 %collective-permute-start.14 = (f32[512,256]{1,0:T(8,128)S(1)}, f32[512,256]{1,0:T(8,128)S(1)}, u32[]{:S(2)}, u32[]{:S(2)}) collective-permute-start(f32[512,256]{1,0:T(8,128)S(1)} %get-tuple-element.36.refs_0_), channel_id=1, source_target_pairs={{4,0},{8,4},{12,8},{14,12},{10,14},{6,10},{2,6},{0,2},{5,1},{9,5},... | collective-permute-start | bytes 1572872 | tf_op jit(solution)/shard_map/ppermute | solution.py:284
  18.3 53.3 %copy-start.7 = (f32[512,256]{1,0:T(8,128)}, f32[512,256]{1,0:T(8,128)S(1)}, u32[]{:S(2)}) copy-start(f32[512,256]{1,0:T(8,128)S(1)} %collective-permute-done.refs_0_) | copy-start | bytes 1572868
  18.3 22.7 %collective-permute-start.1 = (f32[512,256]{1,0:T(8,128)S(1)}, f32[512,256]{1,0:T(8,128)}, u32[]{:S(2)}, u32[]{:S(2)}) collective-permute-start(f32[512,256]{1,0:T(8,128)S(1)} %collective-permute-done.refs_0_), channel_id=1, source_target_pairs={{0,4},{4,8},{8,12},{12,14},{14,10},{10,6},{6,2},{2,0},{1,5},{5,9},... | collective-permute-start | bytes 1572872 | tf_op jit(solution)/shard_map/ppermute | solution.py:281
  20.2 51.5 %copy-start.8 = (f32[512,256]{1,0:T(8,128)}, f32[512,256]{1,0:T(8,128)S(1)}, u32[]{:S(2)}) copy-start(f32[512,256]{1,0:T(8,128)S(1)} %collective-permute-done.4.refs_3_) | copy-start | bytes 1572868
  20.2 22.9 %collective-permute-start.5 = (f32[512,256]{1,0:T(8,128)S(1)}, f32[512,256]{1,0:T(8,128)}, u32[]{:S(2)}, u32[]{:S(2)}) collective-permute-start(f32[512,256]{1,0:T(8,128)S(1)} %collective-permute-done.4.refs_3_), channel_id=1, source_target_pairs={{4,0},{8,4},{12,8},{14,12},{10,14},{6,10},{2,6},{0,2},{5,1},{9,5},... | collective-permute-start | bytes 1572872 | tf_op jit(solution)/shard_map/ppermute | solution.py:284
  29.7 42.0 %copy-start.9 = (f32[512,256]{1,0:T(8,128)}, f32[512,256]{1,0:T(8,128)S(1)}, u32[]{:S(2)}) copy-start(f32[512,256]{1,0:T(8,128)S(1)} %collective-permute-done.11.refs_1_) | copy-start | bytes 1572868
  29.7 22.6 %collective-permute-start.12 = (f32[512,256]{1,0:T(8,128)S(1)}, f32[512,256]{1,0:T(8,128)}, u32[]{:S(2)}, u32[]{:S(2)}) collective-permute-start(f32[512,256]{1,0:T(8,128)S(1)} %collective-permute-done.11.refs_1_), channel_id=1, source_target_pairs={{0,4},{4,8},{8,12},{12,14},{14,10},{10,6},{6,2},{2,0},{1,5},{5,9},... | collective-permute-start | bytes 1572872 | tf_op jit(solution)/shard_map/ppermute | solution.py:281
  31.7 39.9 %copy-start.10 = (f32[512,256]{1,0:T(8,128)}, f32[512,256]{1,0:T(8,128)S(1)}, u32[]{:S(2)}) copy-start(f32[512,256]{1,0:T(8,128)S(1)} %collective-permute-done.14.refs_2_) | copy-start | bytes 1572868
  31.7 22.6 %collective-permute-start.15 = (f32[512,256]{1,0:T(8,128)S(1)}, f32[512,256]{1,0:T(8,128)}, u32[]{:S(2)}, u32[]{:S(2)}) collective-permute-start(f32[512,256]{1,0:T(8,128)S(1)} %collective-permute-done.14.refs_2_), channel_id=1, source_target_pairs={{4,0},{8,4},{12,8},{14,12},{10,14},{6,10},{2,6},{0,2},{5,1},{9,5},... | collective-permute-start | bytes 1572872 | tf_op jit(solution)/shard_map/ppermute | solution.py:284
  41.0 22.5 %collective-permute-start.2 = (f32[512,256]{1,0:T(8,128)}, f32[512,256]{1,0:T(8,128)}, u32[]{:S(2)}, u32[]{:S(2)}) collective-permute-start(f32[512,256]{1,0:T(8,128)} %collective-permute-done.1.refs_0_), channel_id=1, source_target_pairs={{0,4},{4,8},{8,12},{12,14},{14,10},{10,6},{6,2},{2,0},{1,5},{5,9},... | collective-permute-start | bytes 1572872 | tf_op jit(solution)/shard_map/ppermute | solution.py:281
  43.0 22.5 %collective-permute-start.6 = (f32[512,256]{1,0:T(8,128)}, f32[512,256]{1,0:T(8,128)}, u32[]{:S(2)}, u32[]{:S(2)}) collective-permute-start(f32[512,256]{1,0:T(8,128)} %collective-permute-done.5.refs_3_), channel_id=1, source_target_pairs={{4,0},{8,4},{12,8},{14,12},{10,14},{6,10},{2,6},{0,2},{5,1},{9,5},... | collective-permute-start | bytes 1572872 | tf_op jit(solution)/shard_map/ppermute | solution.py:284
  52.2 60.7 %collective-permute-start.13 = (f32[512,256]{1,0:T(8,128)}, f32[512,256]{1,0:T(8,128)S(1)}, u32[]{:S(2)}, u32[]{:S(2)}) collective-permute-start(f32[512,256]{1,0:T(8,128)} %collective-permute-done.12.refs_1_), channel_id=1, source_target_pairs={{0,4},{4,8},{8,12},{12,14},{14,10},{10,6},{6,2},{2,0},{1,5},{5,9},... | collective-permute-start | bytes 1572872 | tf_op jit(solution)/shard_map/ppermute | solution.py:281
  54.3 58.7 %collective-permute-start.16 = (f32[512,256]{1,0:T(8,128)}, f32[512,256]{1,0:T(8,128)S(1)}, u32[]{:S(2)}, u32[]{:S(2)}) collective-permute-start(f32[512,256]{1,0:T(8,128)} %collective-permute-done.15.refs_2_), channel_id=1, source_target_pairs={{4,0},{8,4},{12,8},{14,12},{10,14},{6,10},{2,6},{0,2},{5,1},{9,5},... | collective-permute-start | bytes 1572872 | tf_op jit(solution)/shard_map/ppermute | solution.py:284
  63.5 59.6 %collective-permute-start.3 = (f32[512,256]{1,0:T(8,128)}, f32[512,256]{1,0:T(8,128)S(1)}, u32[]{:S(2)}, u32[]{:S(2)}) collective-permute-start(f32[512,256]{1,0:T(8,128)} %collective-permute-done.2.refs_0_), channel_id=1, source_target_pairs={{0,4},{4,8},{8,12},{12,14},{14,10},{10,6},{6,2},{2,0},{1,5},{5,9},... | collective-permute-start | bytes 1572872 | tf_op jit(solution)/shard_map/ppermute | solution.py:281
  65.5 57.6 %collective-permute-start.7 = (f32[512,256]{1,0:T(8,128)}, f32[512,256]{1,0:T(8,128)S(1)}, u32[]{:S(2)}, u32[]{:S(2)}) collective-permute-start(f32[512,256]{1,0:T(8,128)} %collective-permute-done.6.refs_3_), channel_id=1, source_target_pairs={{4,0},{8,4},{12,8},{14,12},{10,14},{6,10},{2,6},{0,2},{5,1},{9,5},... | collective-permute-start | bytes 1572872 | tf_op jit(solution)/shard_map/ppermute | solution.py:284
  123.1 7.5 %copy-start.6 = (f32[512,512]{1,0:T(8,128)S(1)}, f32[512,512]{1,0:T(8,128)}, u32[]{:S(2)}) copy-start(f32[512,512]{1,0:T(8,128)} %param.7) | copy-start | bytes 3145732
  130.5 2.9 %collective-permute-start.17 = (f32[1024,256]{1,0:T(8,128)}, f32[1024,256]{1,0:T(8,128)S(1)}, u32[]{:S(2)}, u32[]{:S(2)}) collective-permute-start(f32[1024,256]{1,0:T(8,128)} %gather_product.9.own_ref), channel_id=1, source_target_pairs={{0,1},{1,0},{2,3},{3,2},{4,5},{5,4},{6,7},{7,6},{8,9},{9,8},{10,11... | collective-permute-start | bytes 3145736 | tf_op jit(solution)/shard_map/ppermute | solution.py:287
  145.6 6.6 %copy-start.5 = (f32[1024,512]{1,0:T(8,128)S(1)}, f32[1024,512]{1,0:T(8,128)}, u32[]{:S(2)}) copy-start(f32[1024,512]{1,0:T(8,128)} %get-tuple-element.24) | copy-start | bytes 6291460
  149.3 15.4 %collective-permute-start.18 = (f32[256,512]{1,0:T(8,128)S(1)}, f32[256,512]{1,0:T(8,128)S(1)}, u32[]{:S(2)}, u32[]{:S(2)}) collective-permute-start(f32[256,512]{1,0:T(8,128)S(1)} %copy-done.24), channel_id=1, source_target_pairs={{0,4},{4,8},{8,12},{12,14},{14,10},{10,6},{6,2},{2,0},{1,5},{5,9},... | collective-permute-start | bytes 1572872 | tf_op jit(solution)/shard_map/ppermute | solution.py:281
  151.7 23.4 %collective-permute-start.29 = (f32[256,512]{1,0:T(8,128)}, f32[256,512]{1,0:T(8,128)S(1)}, u32[]{:S(2)}, u32[]{:S(2)}) collective-permute-start(f32[256,512]{1,0:T(8,128)} %scatter_product.28), channel_id=1, source_target_pairs={{4,0},{8,4},{12,8},{14,12},{10,14},{6,10},{2,6},{0,2},{5,1},{9,5},... | collective-permute-start | bytes 1572872 | tf_op jit(solution)/shard_map/ppermute | solution.py:284
  153.3 26.9 %collective-permute-start.34 = (f32[128,512]{1,0:T(8,128)S(1)}, f32[128,512]{1,0:T(8,128)S(1)}, u32[]{:S(2)}, u32[]{:S(2)}) collective-permute-start(f32[128,512]{1,0:T(8,128)S(1)} %slice_select_fusion.3), channel_id=1, source_target_pairs={{0,2},{2,0},{4,6},{6,4},{8,10},{10,8},{12,14},{14,12},{1,3},{3,1},... | collective-permute-start | bytes 786440 | tf_op jit(solution)/shard_map/ppermute | solution.py:254
  158.8 23.0 %collective-permute-start.22 = (f32[256,512]{1,0:T(8,128)}, f32[256,512]{1,0:T(8,128)S(1)}, u32[]{:S(2)}, u32[]{:S(2)}) collective-permute-start(f32[256,512]{1,0:T(8,128)} %scatter_product.21), channel_id=1, source_target_pairs={{4,0},{8,4},{12,8},{14,12},{10,14},{6,10},{2,6},{0,2},{5,1},{9,5},... | collective-permute-start | bytes 1572872 | tf_op jit(solution)/shard_map/ppermute | solution.py:284
  169.2 19.4 %collective-permute-start.19 = (f32[256,512]{1,0:T(8,128)}, f32[256,512]{1,0:T(8,128)S(1)}, u32[]{:S(2)}, u32[]{:S(2)}) collective-permute-start(f32[256,512]{1,0:T(8,128)} %scatter_product.18), channel_id=1, source_target_pairs={{0,4},{4,8},{8,12},{12,14},{14,10},{10,6},{6,2},{2,0},{1,5},{5,9},... | collective-permute-start | bytes 1572872 | tf_op jit(solution)/shard_map/ppermute | solution.py:281
  173.6 20.5 %collective-permute-start.26 = (f32[256,512]{1,0:T(8,128)}, f32[256,512]{1,0:T(8,128)S(1)}, u32[]{:S(2)}, u32[]{:S(2)}) collective-permute-start(f32[256,512]{1,0:T(8,128)} %scatter_product.25), channel_id=1, source_target_pairs={{0,4},{4,8},{8,12},{12,14},{14,10},{10,6},{6,2},{2,0},{1,5},{5,9},... | collective-permute-start | bytes 1572872 | tf_op jit(solution)/shard_map/ppermute | solution.py:281
  179.6 21.4 %collective-permute-start.30 = (f32[256,512]{1,0:T(8,128)}, f32[256,512]{1,0:T(8,128)S(1)}, u32[]{:S(2)}, u32[]{:S(2)}) collective-permute-start(f32[256,512]{1,0:T(8,128)} %scatter_product.29), channel_id=1, source_target_pairs={{4,0},{8,4},{12,8},{14,12},{10,14},{6,10},{2,6},{0,2},{5,1},{9,5},... | collective-permute-start | bytes 1572872 | tf_op jit(solution)/shard_map/ppermute | solution.py:284
  180.2 25.6 %collective-permute-start.35 = (f32[128,512]{1,0:T(8,128)S(1)}, f32[128,512]{1,0:T(8,128)S(1)}, u32[]{:S(2)}, u32[]{:S(2)}) collective-permute-start(f32[128,512]{1,0:T(8,128)S(1)} %select_add_fusion), channel_id=1, source_target_pairs={{0,4},{2,6},{4,0},{6,2},{8,12},{10,14},{12,8},{14,10},{1,5},{3,7},... | collective-permute-start | bytes 786440 | tf_op jit(solution)/shard_map/ppermute | solution.py:254
  186.3 42.4 %collective-permute-start.23 = (f32[256,512]{1,0:T(8,128)}, f32[256,512]{1,0:T(8,128)S(1)}, u32[]{:S(2)}, u32[]{:S(2)}) collective-permute-start(f32[256,512]{1,0:T(8,128)} %scatter_product.22), channel_id=1, source_target_pairs={{4,0},{8,4},{12,8},{14,12},{10,14},{6,10},{2,6},{0,2},{5,1},{9,5},... | collective-permute-start | bytes 1572872 | tf_op jit(solution)/shard_map/ppermute | solution.py:284
  193.1 42.2 %collective-permute-start.20 = (f32[256,512]{1,0:T(8,128)}, f32[256,512]{1,0:T(8,128)S(1)}, u32[]{:S(2)}, u32[]{:S(2)}) collective-permute-start(f32[256,512]{1,0:T(8,128)} %scatter_product.19), channel_id=1, source_target_pairs={{0,4},{4,8},{8,12},{12,14},{14,10},{10,6},{6,2},{2,0},{1,5},{5,9},... | collective-permute-start | bytes 1572872 | tf_op jit(solution)/shard_map/ppermute | solution.py:281
  198.6 41.9 %collective-permute-start.27 = (f32[256,512]{1,0:T(8,128)}, f32[256,512]{1,0:T(8,128)S(1)}, u32[]{:S(2)}, u32[]{:S(2)}) collective-permute-start(f32[256,512]{1,0:T(8,128)} %scatter_product.26), channel_id=1, source_target_pairs={{0,4},{4,8},{8,12},{12,14},{14,10},{10,6},{6,2},{2,0},{1,5},{5,9},... | collective-permute-start | bytes 1572872 | tf_op jit(solution)/shard_map/ppermute | solution.py:281
  205.5 41.7 %collective-permute-start.31 = (f32[256,512]{1,0:T(8,128)}, f32[256,512]{1,0:T(8,128)S(1)}, u32[]{:S(2)}, u32[]{:S(2)}) collective-permute-start(f32[256,512]{1,0:T(8,128)} %scatter_product.30), channel_id=1, source_target_pairs={{4,0},{8,4},{12,8},{14,12},{10,14},{6,10},{2,6},{0,2},{5,1},{9,5},... | collective-permute-start | bytes 1572872 | tf_op jit(solution)/shard_map/ppermute | solution.py:284
  205.8 22.7 %collective-permute-start.36 = (f32[128,512]{1,0:T(8,128)S(1)}, f32[128,512]{1,0:T(8,128)S(1)}, u32[]{:S(2)}, u32[]{:S(2)}) collective-permute-start(f32[128,512]{1,0:T(8,128)S(1)} %add.102), channel_id=1, source_target_pairs={{0,8},{2,10},{4,12},{6,14},{8,0},{10,2},{12,4},{14,6},{1,9},{3,11}... | collective-permute-start | bytes 786440 | tf_op jit(solution)/shard_map/ppermute | solution.py:254
  228.6 23.2 %collective-permute-start.37 = (f32[128,512]{1,0:T(8,128)S(1)}, f32[128,512]{1,0:T(8,128)S(1)}, u32[]{:S(2)}, u32[]{:S(2)}) collective-permute-start(f32[128,512]{1,0:T(8,128)S(1)} %add.103), channel_id=1, source_target_pairs={{0,2},{2,0},{4,6},{6,4},{8,10},{10,8},{12,14},{14,12},{1,3},{3,1},... | collective-permute-start | bytes 786440 | tf_op jit(solution)/shard_map/ppermute | solution.py:254
  233.3 18.7 %collective-permute-start.24 = (f32[512,256]{1,0:T(8,128)}, f32[512,256]{1,0:T(8,128)S(1)}, u32[]{:S(2)}, u32[]{:S(2)}) collective-permute-start(f32[512,256]{1,0:T(8,128)} %scatter_product.23), channel_id=1, source_target_pairs={{4,0},{8,4},{12,8},{14,12},{10,14},{6,10},{2,6},{0,2},{5,1},{9,5},... | collective-permute-start | bytes 1572872 | tf_op jit(solution)/shard_map/ppermute | solution.py:284
  239.9 15.1 %collective-permute-start.21 = (f32[512,256]{1,0:T(8,128)}, f32[512,256]{1,0:T(8,128)S(1)}, u32[]{:S(2)}, u32[]{:S(2)}) collective-permute-start(f32[512,256]{1,0:T(8,128)} %scatter_product.20), channel_id=1, source_target_pairs={{0,4},{4,8},{8,12},{12,14},{14,10},{10,6},{6,2},{2,0},{1,5},{5,9},... | collective-permute-start | bytes 1572872 | tf_op jit(solution)/shard_map/ppermute | solution.py:281
  245.1 16.6 %collective-permute-start.28 = (f32[512,256]{1,0:T(8,128)}, f32[512,256]{1,0:T(8,128)S(1)}, u32[]{:S(2)}, u32[]{:S(2)}) collective-permute-start(f32[512,256]{1,0:T(8,128)} %scatter_product.27), channel_id=1, source_target_pairs={{0,4},{4,8},{8,12},{12,14},{14,10},{10,6},{6,2},{2,0},{1,5},{5,9},... | collective-permute-start | bytes 1572872 | tf_op jit(solution)/shard_map/ppermute | solution.py:281
  251.8 10.9 %copy-start.3 = (f32[512,256]{1,0:T(8,128)S(1)}, f32[512,256]{1,0:T(8,128)}, u32[]{:S(2)}) copy-start(f32[512,256]{1,0:T(8,128)} %scatter_product.24) | copy-start | bytes 1572868
  251.8 10.9 %collective-permute-start.32 = (f32[512,256]{1,0:T(8,128)}, f32[512,256]{1,0:T(8,128)S(1)}, u32[]{:S(2)}, u32[]{:S(2)}) collective-permute-start(f32[512,256]{1,0:T(8,128)} %scatter_product.31), channel_id=1, source_target_pairs={{4,0},{8,4},{12,8},{14,12},{10,14},{6,10},{2,6},{0,2},{5,1},{9,5},... | collective-permute-start | bytes 1572872 | tf_op jit(solution)/shard_map/ppermute | solution.py:284
  251.9 11.0 %collective-permute-start.38 = (f32[256,512]{1,0:T(8,128)S(1)}, f32[256,512]{1,0:T(8,128)S(1)}, u32[]{:S(2)}, u32[]{:S(2)}) collective-permute-start(f32[256,512]{1,0:T(8,128)S(1)} %pad_maximum_fusion.2), channel_id=1, source_target_pairs={{0,1},{1,0},{2,3},{3,2},{4,5},{5,4},{6,7},{7,6},{8,9},{9,8},{10,11... | collective-permute-start | bytes 1572872 | tf_op jit(solution)/shard_map/ppermute | solution.py:287
  255.1 9.0 %collective-permute-start.25 = (f32[512,256]{1,0:T(8,128)S(1)}, f32[512,256]{1,0:T(8,128)S(1)}, u32[]{:S(2)}, u32[]{:S(2)}) collective-permute-start(f32[512,256]{1,0:T(8,128)S(1)} %add_add_fusion.1), channel_id=1, source_target_pairs={{0,1},{1,0},{2,3},{3,2},{4,5},{5,4},{6,7},{7,6},{8,9},{9,8},{10,11... | collective-permute-start | bytes 1572872 | tf_op jit(solution)/shard_map/ppermute | solution.py:287
  262.8 2.0 collective-permute-start.33
  (20 other events, 34.7 us)

commit v2 on v1

v2 whole, which is shorter than its diff:
```python
import functools

import jax
import jax.numpy as jnp
from jax import lax
from jax.experimental import pallas as pl
from jax.experimental.pallas import tpu as pltpu
from jax.sharding import PartitionSpec as P

BF16 = jnp.bfloat16
F32 = jnp.float32


def ring_place(index, size):
    if size == 8:
        z, y = index // 2, index % 2
        return z + y * (size - 1 - 2 * z)
    return index


def ring_pairs(size):
    at = {ring_place(i, size): i for i in range(size)}
    ahead = [(at[p], at[(p + 1) % size]) for p in range(size)]
    back = [(b, a) for a, b in ahead]
    return ahead, back


def split_hi_lo(value):
    hi = value.astype(BF16)
    return hi, (value - hi.astype(F32)).astype(BF16)


def dot(a, b, dims=((1,), (0,))):
    return lax.dot_general(a, b, (dims, ((), ())), preferred_element_type=F32)


def params(mib):
    return pltpu.CompilerParams(vmem_limit_bytes=mib * 1024 * 1024)


def after(value, *others):
    return lax.optimization_barrier((value, *others))[0]


def densify_kernel(first, place_ref, count_ref, own_ref, other_ref, *refs):
    hi_ref, lo_ref = refs[-2:]
    row = first + pl.program_id(0)
    hi_ref[...] = jnp.zeros_like(hi_ref)
    lo_ref[...] = jnp.zeros_like(lo_ref)
    tile = own_ref.shape[-1]
    for replica, ref in enumerate((own_ref, other_ref)):

        def body(slot, carry, replica=replica, ref=ref):
            hi, lo = split_hi_lo(ref[0, slot])
            block = place_ref[replica, 0, row, slot]
            column = pl.multiple_of(place_ref[replica, 1, row, slot] * tile, tile)
            hi_ref[block, :, pl.ds(column, tile)] = hi
            lo_ref[block, :, pl.ds(column, tile)] = lo
            return carry

        lax.fori_loop(0, count_ref[replica, row], body, 0)


def densify(dense, tiles, place, count, size, first, last):
    own, other = tiles
    tiles_here, slots, tile, _ = own.shape
    rows = tiles_here * tile
    shape = jax.ShapeDtypeStruct((size, rows, rows), BF16)
    tile_spec = pl.BlockSpec((1, slots, tile, tile), lambda i, *_: (first + i, 0, 0, 0))
    out_spec = pl.BlockSpec((size, tile, rows), lambda i, *_: (0, first + i, 0))
    return pl.pallas_call(
        functools.partial(densify_kernel, first),
        out_shape=(shape, shape),
        grid_spec=pltpu.PrefetchScalarGridSpec(
            num_scalar_prefetch=2,
            grid=(last - first,),
            in_specs=[tile_spec, tile_spec] + [pl.BlockSpec(memory_space=pl.ANY)] * len(dense),
            out_specs=(out_spec, out_spec),
        ),
        input_output_aliases={4: 0, 5: 1} if dense else {},
        compiler_params=params(50),
        cost_estimate=pl.CostEstimate(
            flops=0,
            transcendentals=0,
            bytes_accessed=(last - first) * tile * (slots * tile * 8 + size * rows * 4),
        ),
        name="densify",
    )(place, count, own, other, *dense)


def gather_kernel(blocks, *refs):
    x_refs = refs[: 2 * blocks]
    a_refs = refs[2 * blocks : 4 * blocks]
    rest = refs[4 * blocks :]
    total_ref = rest[0] if len(rest) == 3 else None
    out_ref, x_split = rest[-2:]
    half, width = x_refs[0].shape

    @pl.when(pl.program_id(0) == 0)
    def _():
        for n in range(2 * blocks):
            hi, lo = split_hi_lo(x_refs[n][...])
            x_split[pl.ds(n * half, half), pl.ds(0, width)] = hi
            x_split[pl.ds(n * half, half), pl.ds(width, width)] = lo

    acc = None
    for n in range(blocks):
        span = pl.ds(n * 2 * half, 2 * half)
        both = dot(a_refs[2 * n][0], x_split[span, :])
        low = dot(a_refs[2 * n + 1][0], x_split[span, pl.ds(0, width)])
        part = both[:, :width] + both[:, width:] + low
        acc = part if acc is None else acc + part
    if total_ref is not None:
        acc = acc + total_ref[...]
    out_ref[...] = acc


def gather_product(dense, chunks, total):
    size, rows, columns = dense[0].shape
    half, width = chunks[0][1].shape
    blocks = len(chunks)
    step = rows // 2
    full = pl.BlockSpec((half, width), lambda i: (0, 0))
    in_specs = [full] * (2 * blocks)
    operands = [value for _, top, bottom in chunks for value in (top, bottom)]
    for block, _, _ in chunks:
        spec = pl.BlockSpec((1, step, columns), lambda i, block=block: (block, i, 0))
        in_specs += [spec, spec]
        operands += [dense[0], dense[1]]
    row_spec = pl.BlockSpec((step, width), lambda i: (i, 0))
    if total is not None:
        in_specs.append(row_spec)
        operands.append(total)
    return pl.pallas_call(
        functools.partial(gather_kernel, blocks),
        out_shape=jax.ShapeDtypeStruct((rows, width), F32),
        grid=(rows // step,),
        in_specs=in_specs,
        out_specs=row_spec,
        scratch_shapes=[pltpu.VMEM((blocks * 2 * half, 2 * width), BF16)],
        compiler_params=params(50),
        cost_estimate=pl.CostEstimate(
            flops=6 * blocks * rows * columns * width,
            transcendentals=0,
            bytes_accessed=blocks * (rows * columns * 4 + columns * width * 4) + rows * width * 8,
        ),
        name="gather_product",
    )(*operands)


def layer_kernel(*refs):
    x_refs = refs[:4]
    hi_ref, lo_ref, own_ref, other_ref, cot_ref, whi_ref, wlo_ref = refs[4:11]
    out_ref, pre_grad_ref, total_ref, grad_ref, top_ref, bottom_ref, x_split = refs[11:]
    half, width = x_refs[0].shape
    both_width = 2 * width

    @pl.when(pl.program_id(0) == 0)
    def _():
        for n in range(4):
            hi, lo = split_hi_lo(x_refs[n][...])
            span = pl.ds((n % 2) * half, half)
            x_split[span, pl.ds((n // 2) * width, width)] = hi
            x_split[span, pl.ds(both_width + (n // 2) * width, width)] = lo

    a_hi, a_lo = hi_ref[0], lo_ref[0]
    both = dot(a_hi, x_split[...])
    total = both[:, :both_width] + both[:, both_width:] + dot(a_lo, x_split[:, pl.ds(0, both_width)])
    total = total + jnp.concatenate([own_ref[...], other_ref[...]], 1)
    total_ref[...] = total[:, :width]
    hi, lo = split_hi_lo(total)
    pre = dot(hi, whi_ref[...]) + dot(lo, whi_ref[...]) + dot(hi, wlo_ref[...])
    sigma = jax.nn.sigmoid(pre)
    out_ref[...] = pre * sigma
    pre_grad = cot_ref[...] * (sigma * (1.0 + pre * (1.0 - sigma)))
    pre_grad_ref[...] = pre_grad
    hi, lo = split_hi_lo(pre_grad)
    mine = pl.ds(0, width)
    turned = ((1,), (1,))
    grad = dot(hi, whi_ref[mine, :], turned) + dot(lo, whi_ref[mine, :], turned)
    grad += dot(hi, wlo_ref[mine, :], turned)
    hi, lo = split_hi_lo(grad)
    grad = jnp.concatenate([hi, lo], 1)
    grad_ref[...] = grad
    down = ((0,), (0,))
    both = dot(a_hi, grad, down)
    part = both[:, :width] + both[:, width:] + dot(a_lo, hi, down)

    @pl.when(pl.program_id(0) == 0)
    def _():
        top_ref[...] = part[:half]
        bottom_ref[...] = part[half:]

    @pl.when(pl.program_id(0) != 0)
    def _():
        top_ref[...] += part[:half]
        bottom_ref[...] += part[half:]


def layer(dense, block, x_own, x_other, own, other, cotangent, w_hi, w_lo):
    size, rows, columns = dense[0].shape
    width = own.shape[1]
    half = x_own[0].shape[0]
    features = cotangent.shape[1]
    step = 256
    x_spec = pl.BlockSpec((half, width), lambda i: (0, 0))
    a_spec = pl.BlockSpec((1, step, columns), lambda i: (block, i, 0))
    half_spec = pl.BlockSpec((step, width), lambda i: (i, 0))
    full_spec = pl.BlockSpec((step, features), lambda i: (i, 0))
    weight_spec = pl.BlockSpec(w_hi.shape, lambda i: (0, 0))
    return pl.pallas_call(
        layer_kernel,
        out_shape=(
            jax.ShapeDtypeStruct((rows, features), F32),
            jax.ShapeDtypeStruct((rows, features), F32),
            jax.ShapeDtypeStruct((rows, width), F32),
            jax.ShapeDtypeStruct((rows, 2 * width), BF16),
            jax.ShapeDtypeStruct((half, width), F32),
            jax.ShapeDtypeStruct((half, width), F32),
        ),
        grid=(rows // step,),
        in_specs=[x_spec] * 4
        + [a_spec, a_spec, half_spec, half_spec, full_spec, weight_spec, weight_spec],
        out_specs=(
            full_spec,
            full_spec,
            half_spec,
            pl.BlockSpec((step, 2 * width), lambda i: (i, 0)),
            x_spec,
            x_spec,
        ),
        scratch_shapes=[pltpu.VMEM((2 * half, 4 * width), BF16)],
        compiler_params=params(50),
        cost_estimate=pl.CostEstimate(
            flops=6 * rows * (3 * columns * width + features * (features + width)),
            transcendentals=rows * features,
            bytes_accessed=rows * (features * 24 + columns * 4),
        ),
        name="layer",
    )(*x_own, *x_other, dense[0], dense[1], own, other, cotangent, w_hi, w_lo)


def scatter_kernel(grad_ref, hi_ref, lo_ref, top_ref, bottom_ref):
    width = grad_ref.shape[1] // 2
    down = ((0,), (0,))
    both = dot(hi_ref[0], grad_ref[...], down)
    part = both[:, :width] + both[:, width:]
    part += dot(lo_ref[0], grad_ref[:, pl.ds(0, width)], down)

    @pl.when(pl.program_id(0) == 0)
    def _():
        top_ref[...] = part

    @pl.when(pl.program_id(0) == 1)
    def _():
        bottom_ref[...] = part


def scatter_product(dense, grad, block):
    size, rows, columns = dense[0].shape
    width = grad.shape[1] // 2
    half = columns // 2
    a_spec = pl.BlockSpec((1, rows, half), lambda i: (block, 0, i))
    out_spec = pl.BlockSpec((half, width), lambda i: (0, 0))
    shape = jax.ShapeDtypeStruct((half, width), F32)
    return pl.pallas_call(
        scatter_kernel,
        out_shape=(shape, shape),
        grid=(2,),
        in_specs=[pl.BlockSpec(grad.shape, lambda i: (0, 0)), a_spec, a_spec],
        out_specs=(out_spec, out_spec),
        compiler_params=params(50),
        cost_estimate=pl.CostEstimate(
            flops=6 * rows * columns * width,
            transcendentals=0,
            bytes_accessed=rows * columns * 4 + rows * width * 4 + columns * width * 4,
        ),
        name="scatter_product",
    )(grad, dense[0], dense[1])


def sum_over_row(value, size):
    me = lax.axis_index("row")
    half = value.shape[0] // 2
    odd = me % 2

    def swap(block, distance):
        return lax.ppermute(block, "row", [(i, i ^ distance) for i in range(size)])

    top, bottom = value[:half], value[half:]
    mine = jnp.where(odd == 0, top, bottom)
    sent = jnp.where(odd == 0, bottom, top)
    mine = mine + swap(sent, 1)
    distance = 2
    while distance < size:
        mine = mine + swap(mine, distance)
        distance *= 2
    theirs = swap(mine, 1)
    low = jnp.where(odd == 0, mine, theirs)
    high = jnp.where(odd == 0, theirs, mine)
    return jnp.concatenate([low, high], 0)


def per_device(features, weight, cotangent, tile_vals, col_tile, counts):
    size = lax.axis_size("row")
    hops = size // 2
    rep = lax.axis_index("rep")
    row = lax.axis_index("row")
    tiles_here = tile_vals.shape[0]
    width = features.shape[1] // 2
    half = features.shape[0] // 2
    ahead, back = ring_pairs(size)

    def forth(block):
        return lax.ppermute(block, "row", ahead)

    def rear(block):
        return lax.ppermute(block, "row", back)

    def swap(block):
        return lax.ppermute(block, "rep", [(0, 1), (1, 0)])

    def order(own, other, axis):
        low = jnp.where(rep == 0, own, other)
        high = jnp.where(rep == 0, other, own)
        return jnp.concatenate([low, high], axis)

    own_tiles = tile_vals[:, 0]
    other_tiles = swap(own_tiles)
    own_columns = col_tile[:, 0]
    columns = jnp.stack([own_columns, swap(own_columns)])
    block = jnp.mod(ring_place(columns // tiles_here, size) - ring_place(row, size), size)
    place = jnp.stack([block, columns % tiles_here], 1)
    count = jnp.stack([counts[:, 0], swap(counts[:, 0])])

    w_own = jnp.where(rep == 0, weight[:width], weight[width:])
    w_other = jnp.where(rep == 0, weight[width:], weight[:width])
    w_rows = jnp.concatenate([w_own, w_other], 0)
    w_high = lax.reduce_precision(w_rows, 8, 7)
    w_hi, w_lo = w_high.astype(BF16), (w_rows - w_high).astype(BF16)

    mine = jnp.where(rep == 0, features[:, :width], features[:, width:])
    top, bottom = mine[:half], mine[half:]
    dense, total = (), None
    cuts = [0, tiles_here * 3 // 8, tiles_here * 3 // 4, tiles_here]
    ready = []

    def next_piece():
        nonlocal dense
        done = next_piece.done
        if done < 3:
            dense = densify(
                dense, (own_tiles, other_tiles), place, count, size, cuts[done], cuts[done + 1]
            )
            next_piece.done += 1
            if next_piece.done < 3:
                return dense
        return multiply_ready()

    next_piece.done = 0

    def multiply_ready():
        nonlocal total
        if next_piece.done == 3 and ready:
            total = gather_product(dense, ready.pop(0), total)
            return (total,)
        return ()

    ready.append([(0, top, bottom)])
    forward_top, forward_bottom, rear_top, rear_bottom = top, bottom, top, bottom
    covered = ()
    for hop in range(1, hops + 1):
        if hop > 2:
            covered = next_piece()
        if covered:
            forward_top, rear_bottom = (after(v, *covered) for v in (forward_top, rear_bottom))
        forward_top = forth(forward_top)
        rear_bottom = rear(rear_bottom)
        if hop < hops:
            if hop > 1:
                covered = next_piece()
                forward_bottom, rear_top = (after(v, *covered) for v in (forward_bottom, rear_top))
            forward_bottom = forth(forward_bottom)
            rear_top = rear(rear_top)
            ready.append(
                [(size - hop, forward_top, forward_bottom), (hop, rear_top, rear_bottom)]
            )
    while ready:
        multiply_ready()
    x_last = (forward_top, rear_bottom)
    other_total = swap(total)
    x_other = tuple(swap(v) for v in x_last)
    output, grad_pre, total, grad, first_top, first_bottom = layer(
        dense, hops, x_last, x_other, total, other_total, cotangent, w_hi, w_lo
    )

    def product(block):
        return scatter_product(dense, grad, block)

    forward_top, rear_bottom = forth(first_top), rear(first_bottom)
    forward_bottom = rear_top = None
    for hop in range(hops - 1, 0, -1):
        ahead_top, ahead_bottom = product(hop)
        back_top, back_bottom = product(size - hop)
        if forward_bottom is not None:
            ahead_bottom = ahead_bottom + forward_bottom
            back_top = back_top + rear_top
        forward_bottom = forth(ahead_bottom)
        rear_top = rear(back_top)
        forward_top = forth(ahead_top + forward_top)
        rear_bottom = rear(back_bottom + rear_bottom)

    weight_part = lax.dot_general(
        total,
        grad_pre,
        (((0,), (0,)), ((), ())),
        precision=lax.Precision.HIGH,
        preferred_element_type=F32,
    )
    weight_half = sum_over_row(weight_part, size)
    weight_grad = order(weight_half, swap(weight_half), 0)

    home_top, home_bottom = product(0)
    home_top = home_top + forward_top + rear_top
    home_bottom = home_bottom + forward_bottom + rear_bottom
    input_grad = jnp.concatenate(
        [order(home_top, swap(home_top), 1), order(home_bottom, swap(home_bottom), 1)], 0
    )
    return (output, input_grad, weight_grad)


def solution(mesh):
    return jax.shard_map(
        per_device,
        mesh=mesh,
        in_specs=(
            P(("groups", "row"), None),
            P(),
            P(("groups", "row"), None),
            P(("groups", "row"), "rep", None, None, None),
            P(("groups", "row"), "rep", None),
            P(("groups", "row"), "rep"),
        ),
        out_specs=(P(("groups", "row"), None), P(("groups", "row"), None), P("groups", None)),
        check_vma=False,
    )
```

time: 268 us -> 204 us (0.76)
  Pallas kernels: 129 us -> 87.3 us
  waiting for transfers between devices: 77.5 us -> 56.7 us
  local copies, waits for them, and re-layouts: 12.2 us -> 2.98 us
  starting transfers between devices: 38.6 us -> 44.6 us
    pallas_call x20 -> x10, Pallas kernels: 84.1 us -> 49.4 us  [the longest x7 25.8 us: scatter_product(): pl.pallas_call(scatter_kernel, out_shape=(shape, shape), grid=(2,), in_sp...]
    ppermute x14, waiting for transfers between devices: 53.5 us -> 20.1 us  [forth(): return lax.ppermute(block, 'row', ahead)]
    ppermute x14, waiting for transfers between devices: 1.14 us -> 17 us  [rear(): return lax.ppermute(block, 'row', back)]
    ppermute x14, starting transfers between devices: 6.13 us -> 21.5 us  [rear(): return lax.ppermute(block, 'row', back)]
    ppermute x14, starting transfers between devices: 25.2 us -> 10.2 us  [forth(): return lax.ppermute(block, 'row', ahead)]
    pallas_call x5 -> x4, Pallas kernels: 37 us -> 22.7 us  [gather_product(): pl.pallas_call(functools.partial(gather_kernel, blocks), out_shape=jax.Sh...]
    unnamed x58 -> x14, local copies, waits for them, and re-layouts: 12.1 us -> 2.91 us
    pallas_call x1, Pallas kernels: 7.59 us -> 15.2 us  [layer(): pl.pallas_call(layer_kernel, out_shape=(jax.ShapeDtypeStruct((rows, featu...]
  transfers between devices with their start and end apart: 39 -> 41, of which waited for: 14 -> 17; matrix products, arithmetic and copies ran while one was open for 3% -> 5% of each run, Pallas kernels for 41% -> 35%
where the time goes in v2:
time: 204 us
  Pallas kernels  87.3 us (43%)
  waiting for transfers between devices  56.7 us (28%)
  starting transfers between devices  44.6 us (22%)
  other arithmetic  7.99 us (4%)
  matrix products  3.02 us (1%)
  local copies, waits for them, and re-layouts  2.98 us (1%)
    pallas_call x7, Pallas kernels, scatter_product(): pl.pallas_call(scatter_kernel, out_shape=(shape, shape), grid=(2,), in_sp...  25.8 us
    pallas_call x3, Pallas kernels, densify(): pl.pallas_call(functools.partial(densify_kernel, first), out_shape=(shape...  23.6 us
    pallas_call x4, Pallas kernels, gather_product(): pl.pallas_call(functools.partial(gather_kernel, blocks), out_shape=jax.Sh...  22.7 us
    ppermute x14, starting transfers between devices, rear(): return lax.ppermute(block, 'row', back)  21.5 us
    ppermute x14, waiting for transfers between devices, forth(): return lax.ppermute(block, 'row', ahead)  20.1 us
    ppermute x14, waiting for transfers between devices, rear(): return lax.ppermute(block, 'row', back)  17 us
    pallas_call x1, Pallas kernels, layer(): pl.pallas_call(layer_kernel, out_shape=(jax.ShapeDtypeStruct((rows, featu...  15.2 us
    ppermute x4, starting transfers between devices, swap(): return lax.ppermute(block, 'row', [(i, i ^ distance) for i in range(size)])  11.6 us
  transfers between devices with their start and end apart: 41, of which 17 were waited for; matrix products, arithmetic and copies ran while one was open for 5% of the time, Pallas kernels for 35%

profile of v2, /device:TPU:0, one launch (start us, length us, event | category | flops | bytes accessed | tf_op | source)
XLA Modules:
  0.0 203.6 jit_solution(4505590894907734892)
XLA Ops:
  1.2 1.7 slice_select_fusion
  2.9 2.6 %collective-permute-start.8 = (f32[512,256]{1,0:T(8,128)S(1)}, f32[512,256]{1,0:T(8,128)S(1)}, u32[]{:S(2)}, u32[]{:S(2)}) collective-permute-start(f32[512,256]{1,0:T(8,128)S(1)} %get-tuple-element.81.refs_1_), channel_id=1, source_target_pairs={{4,0},{8,4},{12,8},{14,12},{10,14},{6,10},{2,6},{0,2},{5,1},{9,5},... | collective-permute-start | bytes 1572872 | tf_op jit(solution)/shard_map/ppermute | solution.py:318
  6.2 7.8 %collective-permute-done.3 = s32[8]{0:T(128)S(1)} collective-permute-done((s32[8]{0:T(128)S(1)}, s32[8]{0:T(128)S(1)}, u32[]{:S(2)}, u32[]{:S(2)}) %collective-permute-start.3) | collective-permute-done | bytes 64 | tf_op jit(solution)/shard_map/ppermute | solution.py:321
  13.9 2.9 %collective-permute-start.7 = (f32[512,256]{1,0:T(8,128)S(1)}, f32[512,256]{1,0:T(8,128)S(1)}, u32[]{:S(2)}, u32[]{:S(2)}) collective-permute-start(f32[512,256]{1,0:T(8,128)S(1)} %get-tuple-element.82.refs_0_), channel_id=1, source_target_pairs={{4,0},{8,4},{12,8},{14,12},{10,14},{6,10},{2,6},{0,2},{5,1},{9,5},... | collective-permute-start | bytes 1572872 | tf_op jit(solution)/shard_map/ppermute | solution.py:318
  16.9 1.5 collective-permute-done.8.refs_3_
  18.4 1.7 collective-permute-start.10
  20.5 9.0 %densify.3 = (bf16[8,1024,1024]{2,1,0:T(8,128)(2,1)}, bf16[8,1024,1024]{2,1,0:T(8,128)(2,1)}) custom-call(s32[2,2,8,16]{3,2,1,0:T(8,128)S(1)} %pad_add_fusion.place_ref, s32[2,8]{1,0:T(2,128)S(1)} %pad_add_fusion.2.count_ref, f32[8,16,128,128]{3,2,1,0:T(8,128)} %bitcast.10, f32[8,16,128,128]{3,2,1,0:T(8,128)} %collective-permute-done.4.other_ref), custom_call_target="tpu_custom_call" | custom-call | bytes 18874368 | tf_op jit(solution)/shard_map/densify/pallas_call | solution.py:71
  29.7 1.9 collective-permute-start.17
  31.8 8.2 %densify.4 = (bf16[8,1024,1024]{2,1,0:T(8,128)(2,1)}, bf16[8,1024,1024]{2,1,0:T(8,128)(2,1)}) custom-call(s32[2,2,8,16]{3,2,1,0:T(8,128)S(1)} %pad_add_fusion.place_ref, s32[2,8]{1,0:T(2,128)S(1)} %pad_add_fusion.2.count_ref, f32[8,16,128,128]{3,2,1,0:T(8,128)} %bitcast.11, ...), custom_call_target="tpu_custom_call", output_to_operand_aliasing={{0}: (4, {}), {1}: (5, {})} | custom-call | bytes 18874368 | tf_op jit(solution)/shard_map/densify/pallas_call | solution.py:71
  41.0 1.9 collective-permute-start.11
  43.0 6.4 %densify.5 = (bf16[8,1024,1024]{2,1,0:T(8,128)(2,1)}, bf16[8,1024,1024]{2,1,0:T(8,128)(2,1)}) custom-call(s32[2,2,8,16]{3,2,1,0:T(8,128)S(1)} %pad_add_fusion.place_ref, s32[2,8]{1,0:T(2,128)S(1)} %pad_add_fusion.2.count_ref, f32[8,16,128,128]{3,2,1,0:T(8,128)} %bitcast.12, ...), custom_call_target="tpu_custom_call", output_to_operand_aliasing={{0}: (4, {}), {1}: (5, {})} | custom-call | bytes 12582912 | tf_op jit(solution)/shard_map/densify/pallas_call | solution.py:71
  49.4 3.7 %gather_product.4.refs_8_ = f32[1024,256]{1,0:T(8,128)S(1)} custom-call(f32[512,256]{1,0:T(8,128)S(1)} %get-tuple-element.82.refs_0_, f32[512,256]{1,0:T(8,128)S(1)} %get-tuple-element.81.refs_1_, bf16[8,1024,1024]{2,1,0:T(8,128)(2,1)} %get-tuple-element.42.refs_2_.refs_4_.refs_6_.hi_ref, bf16[8,1024,1024]{2,1,0:T(8,128)(2,1)} %get-tuple-element.43.refs_3_.refs_5_.refs_7_.lo_ref), custom_call_target="tpu_custom_call" | custom-call | flops 1610612736 | bytes 7340032 | tf_op jit(solution)/shard_map/gather_product/pallas_call | solution.py:134
  54.1 1.6 collective-permute-start.18
  56.1 6.3 %gather_product.5.refs_8_ = f32[1024,256]{1,0:T(8,128)S(1)} custom-call(f32[512,256]{1,0:T(8,128)S(1)} %collective-permute-done.refs_0_, f32[512,256]{1,0:T(8,128)S(1)} %collective-permute-done.6.refs_1_, f32[512,256]{1,0:T(8,128)S(1)} %collective-permute-done.7.refs_2_, f32[512,256]{1,0:T(8,128)S(1)} %collective-permute-done.8.refs_3_, ...), custom_call_target="tpu_custom_call" | custom-call | flops 3221225472 | bytes 12582912 | tf_op jit(solution)/shard_map/gather_product/pallas_call | solution.py:134
  63.4 1.9 collective-permute-start.12
  65.5 6.3 %gather_product.6.refs_8_ = f32[1024,256]{1,0:T(8,128)S(1)} custom-call(f32[512,256]{1,0:T(8,128)S(1)} %collective-permute-done.1.refs_0_, f32[512,256]{1,0:T(8,128)S(1)} %collective-permute-done.15.refs_1_, f32[512,256]{1,0:T(8,128)S(1)} %collective-permute-done.17.refs_2_, f32[512,256]{1,0:T(8,128)S(1)} %collective-permute-done.10.refs_3_, ...), custom_call_target="tpu_custom_call" | custom-call | flops 3221225472 | bytes 12582912 | tf_op jit(solution)/shard_map/gather_product/pallas_call | solution.py:134
  72.8 1.9 collective-permute-done.18.refs_2_
  74.7 1.9 collective-permute-done.16.refs_1_
  76.6 6.3 %gather_product.7.refs_6_ = f32[1024,256]{1,0:T(8,128)S(1)} custom-call(f32[512,256]{1,0:T(8,128)S(1)} %collective-permute-done.5.refs_0_, f32[512,256]{1,0:T(8,128)S(1)} %collective-permute-done.16.refs_1_, f32[512,256]{1,0:T(8,128)S(1)} %collective-permute-done.18.refs_2_, f32[512,256]{1,0:T(8,128)S(1)} %collective-permute-done.11.refs_3_, ...), custom_call_target="tpu_custom_call" | custom-call | flops 3221225472 | bytes 12582912 | tf_op jit(solution)/shard_map/gather_product/pallas_call | solution.py:134
  83.0 2.6 %collective-permute-done.12.refs_1_ = f32[512,256]{1,0:T(8,128)S(1)} collective-permute-done((f32[512,256]{1,0:T(8,128)S(1)}, f32[512,256]{1,0:T(8,128)S(1)}, u32[]{:S(2)}, u32[]{:S(2)}) %collective-permute-start.12) | collective-permute-done | bytes 524320 | tf_op jit(solution)/shard_map/ppermute | solution.py:318
  85.6 1.4 collective-permute-done.9.refs_0_
  87.0 1.3 slice_select_fusion.2
  89.3 15.2 %layer.1 = (f32[1024,512]{1,0:T(8,128)}, f32[1024,512]{1,0:T(8,128)}, f32[1024,256]{1,0:T(8,128)}, bf16[1024,512]{1,0:T(8,128)(2,1)}, f32[512,256]{1,0:T(8,128)S(1)}, /*index=5*/f32[512,256]{1,0:T(8,128)S(1)}) custom-call(f32[512,256]{1,0:T(8,128)S(1)} %collective-permute-done.9.refs_0_, f32[512,256]{1,0:T(8,128)S(1)} %collective-permute-done.12.refs_1_, ...), custom_call_target="tpu_custom_call" | custom-call | flops 7247757312 | bytes 16777216 | tf_op jit(solution)/shard_map/layer/pallas_call | solution.py:211
  106.5 3.0 %fusion.11 = f32[256,512]{1,0:T(8,128)S(1)} fusion(f32[1024,256]{1,0:T(8,128)} %get-tuple-element.69, f32[1024,512]{1,0:T(8,128)} %get-tuple-element.70), kind=kOutput, calls=%fused_computation.51 | convolution fusion | flops 805306368 | bytes 3670016 | tf_op jit(solution)/shard_map/dot_general | solution.py:413
  109.5 1.7 collective-permute-start.36
  111.2 3.7 %scatter_product.13 = (f32[512,256]{1,0:T(8,128)S(1)}, f32[512,256]{1,0:T(8,128)S(1)}) custom-call(bf16[1024,512]{1,0:T(8,128)(2,1)S(1)} %copy-done, bf16[8,1024,1024]{2,1,0:T(8,128)(2,1)} %get-tuple-element.42.refs_2_.refs_4_.refs_6_.hi_ref, bf16[8,1024,1024]{2,1,0:T(8,128)(2,1)} %get-tuple-element.43.refs_3_.refs_5_.refs_7_.lo_ref), custom_call_target="tpu_custom_call" | custom-call | flops 1610612736 | bytes 6291456 | tf_op jit(solution)/shard_map/scatter_product/pallas_call | solution.py:266
  115.4 3.7 %scatter_product.10 = (f32[512,256]{1,0:T(8,128)S(1)}, f32[512,256]{1,0:T(8,128)S(1)}) custom-call(bf16[1024,512]{1,0:T(8,128)(2,1)S(1)} %copy-done, bf16[8,1024,1024]{2,1,0:T(8,128)(2,1)} %get-tuple-element.42.refs_2_.refs_4_.refs_6_.hi_ref, bf16[8,1024,1024]{2,1,0:T(8,128)(2,1)} %get-tuple-element.43.refs_3_.refs_5_.refs_7_.lo_ref), custom_call_target="tpu_custom_call" | custom-call | flops 1610612736 | bytes 6291456 | tf_op jit(solution)/shard_map/scatter_product/pallas_call | solution.py:266
  119.1 1.6 collective-permute-start.28
  120.8 1.6 collective-permute-start.21
  123.2 1.6 collective-permute-done.36
  124.9 3.7 %scatter_product.9 = (f32[512,256]{1,0:T(8,128)S(1)}, f32[512,256]{1,0:T(8,128)S(1)}) custom-call(bf16[1024,512]{1,0:T(8,128)(2,1)S(1)} %copy-done, bf16[8,1024,1024]{2,1,0:T(8,128)(2,1)} %get-tuple-element.42.refs_2_.refs_4_.refs_6_.hi_ref, bf16[8,1024,1024]{2,1,0:T(8,128)(2,1)} %get-tuple-element.43.refs_3_.refs_5_.refs_7_.lo_ref), custom_call_target="tpu_custom_call" | custom-call | flops 1610612736 | bytes 6291456 | tf_op jit(solution)/shard_map/scatter_product/pallas_call | solution.py:266
  128.6 3.7 %scatter_product.12 = (f32[512,256]{1,0:T(8,128)S(1)}, f32[512,256]{1,0:T(8,128)S(1)}) custom-call(bf16[1024,512]{1,0:T(8,128)(2,1)S(1)} %copy-done, bf16[8,1024,1024]{2,1,0:T(8,128)(2,1)} %get-tuple-element.42.refs_2_.refs_4_.refs_6_.hi_ref, bf16[8,1024,1024]{2,1,0:T(8,128)(2,1)} %get-tuple-element.43.refs_3_.refs_5_.refs_7_.lo_ref), custom_call_target="tpu_custom_call" | custom-call | flops 1610612736 | bytes 6291456 | tf_op jit(solution)/shard_map/scatter_product/pallas_call | solution.py:266
  132.3 3.3 %collective-permute-done.24 = f32[512,256]{1,0:T(8,128)S(1)} collective-permute-done((f32[512,256]{1,0:T(8,128)S(1)}, f32[512,256]{1,0:T(8,128)S(1)}, u32[]{:S(2)}, u32[]{:S(2)}) %collective-permute-start.24) | collective-permute-done | bytes 524320 | tf_op jit(solution)/shard_map/ppermute | solution.py:318
  135.7 2.5 %collective-permute-start.25 = (f32[512,256]{1,0:T(8,128)S(1)}, f32[512,256]{1,0:T(8,128)S(1)}, u32[]{:S(2)}, u32[]{:S(2)}) collective-permute-start(f32[512,256]{1,0:T(8,128)S(1)} %add.131), channel_id=1, source_target_pairs={{4,0},{8,4},{12,8},{14,12},{10,14},{6,10},{2,6},{0,2},{5,1},{9,5},... | collective-permute-start | bytes 1572872 | tf_op jit(solution)/shard_map/ppermute | solution.py:318
  138.2 8.7 %collective-permute-done.21 = f32[512,256]{1,0:T(8,128)S(1)} collective-permute-done((f32[512,256]{1,0:T(8,128)S(1)}, f32[512,256]{1,0:T(8,128)S(1)}, u32[]{:S(2)}, u32[]{:S(2)}) %collective-permute-start.21) | collective-permute-done | bytes 524320 | tf_op jit(solution)/shard_map/ppermute | solution.py:315
  147.0 2.4 %collective-permute-done.37 = f32[128,512]{1,0:T(8,128)S(1)} collective-permute-done((f32[128,512]{1,0:T(8,128)S(1)}, f32[128,512]{1,0:T(8,128)S(1)}, u32[]{:S(2)}, u32[]{:S(2)}) %collective-permute-start.37) | collective-permute-done | bytes 262176 | tf_op jit(solution)/shard_map/ppermute | solution.py:288
  149.4 3.2 %collective-permute-start.38 = (f32[128,512]{1,0:T(8,128)S(1)}, f32[128,512]{1,0:T(8,128)S(1)}, u32[]{:S(2)}, u32[]{:S(2)}) collective-permute-start(f32[128,512]{1,0:T(8,128)S(1)} %add.142), channel_id=1, source_target_pairs={{0,8},{2,10},{4,12},{6,14},{8,0},{10,2},{12,4},{14,6},{1,9},{3,11}... | collective-permute-start | bytes 786440 | tf_op jit(solution)/shard_map/ppermute | solution.py:288
  152.7 2.5 %collective-permute-start.29 = (f32[512,256]{1,0:T(8,128)S(1)}, f32[512,256]{1,0:T(8,128)S(1)}, u32[]{:S(2)}, u32[]{:S(2)}) collective-permute-start(f32[512,256]{1,0:T(8,128)S(1)} %add.134), channel_id=1, source_target_pairs={{0,4},{4,8},{8,12},{12,14},{14,10},{10,6},{6,2},{2,0},{1,5},{5,9},... | collective-permute-start | bytes 1572872 | tf_op jit(solution)/shard_map/ppermute | solution.py:315
  155.4 3.7 %scatter_product.8 = (f32[512,256]{1,0:T(8,128)S(1)}, f32[512,256]{1,0:T(8,128)S(1)}) custom-call(bf16[1024,512]{1,0:T(8,128)(2,1)S(1)} %copy-done, bf16[8,1024,1024]{2,1,0:T(8,128)(2,1)} %get-tuple-element.42.refs_2_.refs_4_.refs_6_.hi_ref, bf16[8,1024,1024]{2,1,0:T(8,128)(2,1)} %get-tuple-element.43.refs_3_.refs_5_.refs_7_.lo_ref), custom_call_target="tpu_custom_call" | custom-call | flops 1610612736 | bytes 6291456 | tf_op jit(solution)/shard_map/scatter_product/pallas_call | solution.py:266
  159.1 7.2 %collective-permute-done.38 = f32[128,512]{1,0:T(8,128)S(1)} collective-permute-done((f32[128,512]{1,0:T(8,128)S(1)}, f32[128,512]{1,0:T(8,128)S(1)}, u32[]{:S(2)}, u32[]{:S(2)}) %collective-permute-start.38) | collective-permute-done | bytes 262176 | tf_op jit(solution)/shard_map/ppermute | solution.py:288
  166.3 6.7 %collective-permute-start.39 = (f32[128,512]{1,0:T(8,128)S(1)}, f32[128,512]{1,0:T(8,128)S(1)}, u32[]{:S(2)}, u32[]{:S(2)}) collective-permute-start(f32[128,512]{1,0:T(8,128)S(1)} %add.143), channel_id=1, source_target_pairs={{0,2},{2,0},{4,6},{6,4},{8,10},{10,8},{12,14},{14,12},{1,3},{3,1},... | collective-permute-start | bytes 786440 | tf_op jit(solution)/shard_map/ppermute | solution.py:288
  173.0 3.7 %scatter_product.11 = (f32[512,256]{1,0:T(8,128)S(1)}, f32[512,256]{1,0:T(8,128)S(1)}) custom-call(bf16[1024,512]{1,0:T(8,128)(2,1)S(1)} %copy-done, bf16[8,1024,1024]{2,1,0:T(8,128)(2,1)} %get-tuple-element.42.refs_2_.refs_4_.refs_6_.hi_ref, bf16[8,1024,1024]{2,1,0:T(8,128)(2,1)} %get-tuple-element.43.refs_3_.refs_5_.refs_7_.lo_ref), custom_call_target="tpu_custom_call" | custom-call | flops 1610612736 | bytes 6291456 | tf_op jit(solution)/shard_map/scatter_product/pallas_call | solution.py:266
  176.9 2.1 %collective-permute-start.23 = (f32[512,256]{1,0:T(8,128)S(1)}, f32[512,256]{1,0:T(8,128)S(1)}, u32[]{:S(2)}, u32[]{:S(2)}) collective-permute-start(f32[512,256]{1,0:T(8,128)S(1)} %add.129), channel_id=1, source_target_pairs={{0,4},{4,8},{8,12},{12,14},{14,10},{10,6},{6,2},{2,0},{1,5},{5,9},... | collective-permute-start | bytes 1572872 | tf_op jit(solution)/shard_map/ppermute | solution.py:315
  179.0 3.7 %scatter_product.7 = (f32[512,256]{1,0:T(8,128)S(1)}, f32[512,256]{1,0:T(8,128)S(1)}) custom-call(bf16[1024,512]{1,0:T(8,128)(2,1)S(1)} %copy-done, bf16[8,1024,1024]{2,1,0:T(8,128)(2,1)} %get-tuple-element.42.refs_2_.refs_4_.refs_6_.hi_ref, bf16[8,1024,1024]{2,1,0:T(8,128)(2,1)} %get-tuple-element.43.refs_3_.refs_5_.refs_7_.lo_ref), custom_call_target="tpu_custom_call" | custom-call | flops 1610612736 | bytes 6291456 | tf_op jit(solution)/shard_map/scatter_product/pallas_call | solution.py:266
  182.9 2.1 %collective-permute-start.34 = (f32[512,256]{1,0:T(8,128)S(1)}, f32[512,256]{1,0:T(8,128)S(1)}, u32[]{:S(2)}, u32[]{:S(2)}) collective-permute-start(f32[512,256]{1,0:T(8,128)S(1)} %add.139), channel_id=1, source_target_pairs={{4,0},{8,4},{12,8},{14,12},{10,14},{6,10},{2,6},{0,2},{5,1},{9,5},... | collective-permute-start | bytes 1572872 | tf_op jit(solution)/shard_map/ppermute | solution.py:318
  185.1 6.5 %collective-permute-done.26 = f32[512,256]{1,0:T(8,128)S(1)} collective-permute-done((f32[512,256]{1,0:T(8,128)S(1)}, f32[512,256]{1,0:T(8,128)S(1)}, u32[]{:S(2)}, u32[]{:S(2)}) %collective-permute-start.26) | collective-permute-done | bytes 524320 | tf_op jit(solution)/shard_map/ppermute | solution.py:318
  192.0 7.9 %collective-permute-done.30 = f32[512,256]{1,0:T(8,128)S(1)} collective-permute-done((f32[512,256]{1,0:T(8,128)S(1)}, f32[512,256]{1,0:T(8,128)S(1)}, u32[]{:S(2)}, u32[]{:S(2)}) %collective-permute-start.30) | collective-permute-done | bytes 524320 | tf_op jit(solution)/shard_map/ppermute | solution.py:315
  202.0 1.6 maximum_maximum_fusion
  (94 shorter events, 14.8 us)
Async XLA Ops:
  0.6 19.8 %collective-permute-start.4 = (f32[8,16,128,128]{3,2,1,0:T(8,128)}, f32[8,16,128,128]{3,2,1,0:T(8,128)}, u32[]{:S(2)}, u32[]{:S(2)}) collective-permute-start(f32[8,16,128,128]{3,2,1,0:T(8,128)} %bitcast.9), channel_id=1, source_target_pairs={{0,1},{1,0},{2,3},{3,2},{4,5},{5,4},{6,7},{7,6},{8,9},{9,8},{10,11... | collective-permute-start | bytes 25165832 | tf_op jit(solution)/shard_map/ppermute | solution.py:321
  1.1 4.5 %copy-start.5 = (s32[8,1,16]{2,1,0:T(1,128)S(1)}, s32[8,1,16]{2,1,0:T(1,128)}, u32[]{:S(2)}) copy-start(s32[8,1,16]{2,1,0:T(1,128)} %param.10) | copy-start | bytes 1540
  1.2 4.7 %copy-start.6 = (s32[8,1]{0,1:T(1,128)S(1)}, s32[8,1]{0,1:T(1,128)}, u32[]{:S(2)}) copy-start(s32[8,1]{0,1:T(1,128)} %param.11) | copy-start | bytes 100
  2.9 15.4 %collective-permute-start.8 = (f32[512,256]{1,0:T(8,128)S(1)}, f32[512,256]{1,0:T(8,128)S(1)}, u32[]{:S(2)}, u32[]{:S(2)}) collective-permute-start(f32[512,256]{1,0:T(8,128)S(1)} %get-tuple-element.81.refs_1_), channel_id=1, source_target_pairs={{4,0},{8,4},{12,8},{14,12},{10,14},{6,10},{2,6},{0,2},{5,1},{9,5},... | collective-permute-start | bytes 1572872 | tf_op jit(solution)/shard_map/ppermute | solution.py:318
  5.5 14.5 %collective-permute-start = (f32[512,256]{1,0:T(8,128)S(1)}, f32[512,256]{1,0:T(8,128)S(1)}, u32[]{:S(2)}, u32[]{:S(2)}) collective-permute-start(f32[512,256]{1,0:T(8,128)S(1)} %get-tuple-element.82.refs_0_), channel_id=1, source_target_pairs={{0,4},{4,8},{8,12},{12,14},{14,10},{10,6},{6,2},{2,0},{1,5},{5,9},... | collective-permute-start | bytes 1572872 | tf_op jit(solution)/shard_map/ppermute | solution.py:315
  5.7 11.2 %collective-permute-start.2 = (s32[8,16]{1,0:T(8,128)S(1)}, s32[8,16]{1,0:T(8,128)S(1)}, u32[]{:S(2)}, u32[]{:S(2)}) collective-permute-start(s32[8,16]{1,0:T(8,128)S(1)} %bitcast.13), channel_id=1, source_target_pairs={{0,1},{1,0},{2,3},{3,2},{4,5},{5,4},{6,7},{7,6},{8,9},{9,8},{10,11... | collective-permute-start | bytes 1544 | tf_op jit(solution)/shard_map/ppermute | solution.py:321
  5.9 8.1 %collective-permute-start.3 = (s32[8]{0:T(128)S(1)}, s32[8]{0:T(128)S(1)}, u32[]{:S(2)}, u32[]{:S(2)}) collective-permute-start(s32[8]{0:T(128)S(1)} %bitcast.16), channel_id=1, source_target_pairs={{0,1},{1,0},{2,3},{3,2},{4,5},{5,4},{6,7},{7,6},{8,9},{9,8},{10,11... | collective-permute-start | bytes 104 | tf_op jit(solution)/shard_map/ppermute | solution.py:321
  13.9 15.8 %collective-permute-start.7 = (f32[512,256]{1,0:T(8,128)S(1)}, f32[512,256]{1,0:T(8,128)S(1)}, u32[]{:S(2)}, u32[]{:S(2)}) collective-permute-start(f32[512,256]{1,0:T(8,128)S(1)} %get-tuple-element.82.refs_0_), channel_id=1, source_target_pairs={{4,0},{8,4},{12,8},{14,12},{10,14},{6,10},{2,6},{0,2},{5,1},{9,5},... | collective-permute-start | bytes 1572872 | tf_op jit(solution)/shard_map/ppermute | solution.py:318
  16.8 14.8 %collective-permute-start.6 = (f32[512,256]{1,0:T(8,128)S(1)}, f32[512,256]{1,0:T(8,128)S(1)}, u32[]{:S(2)}, u32[]{:S(2)}) collective-permute-start(f32[512,256]{1,0:T(8,128)S(1)} %get-tuple-element.81.refs_1_), channel_id=1, source_target_pairs={{0,4},{4,8},{8,12},{12,14},{14,10},{10,6},{6,2},{2,0},{1,5},{5,9},... | collective-permute-start | bytes 1572872 | tf_op jit(solution)/shard_map/ppermute | solution.py:315
  18.4 22.6 %collective-permute-start.10 = (f32[512,256]{1,0:T(8,128)S(1)}, f32[512,256]{1,0:T(8,128)S(1)}, u32[]{:S(2)}, u32[]{:S(2)}) collective-permute-start(f32[512,256]{1,0:T(8,128)S(1)} %collective-permute-done.8.refs_3_), channel_id=1, source_target_pairs={{4,0},{8,4},{12,8},{14,12},{10,14},{6,10},{2,6},{0,2},{5,1},{9,5},... | collective-permute-start | bytes 1572872 | tf_op jit(solution)/shard_map/ppermute | solution.py:318
  20.1 22.8 %collective-permute-start.1 = (f32[512,256]{1,0:T(8,128)S(1)}, f32[512,256]{1,0:T(8,128)S(1)}, u32[]{:S(2)}, u32[]{:S(2)}) collective-permute-start(f32[512,256]{1,0:T(8,128)S(1)} %collective-permute-done.refs_0_), channel_id=1, source_target_pairs={{0,4},{4,8},{8,12},{12,14},{14,10},{10,6},{6,2},{2,0},{1,5},{5,9},... | collective-permute-start | bytes 1572872 | tf_op jit(solution)/shard_map/ppermute | solution.py:315
  29.7 24.3 %collective-permute-start.17 = (f32[512,256]{1,0:T(8,128)S(1)}, f32[512,256]{1,0:T(8,128)S(1)}, u32[]{:S(2)}, u32[]{:S(2)}) collective-permute-start(f32[512,256]{1,0:T(8,128)S(1)} %collective-permute-done.7.refs_2_), channel_id=1, source_target_pairs={{4,0},{8,4},{12,8},{14,12},{10,14},{6,10},{2,6},{0,2},{5,1},{9,5},... | collective-permute-start | bytes 1572872 | tf_op jit(solution)/shard_map/ppermute | solution.py:318
  31.6 24.0 %collective-permute-start.15 = (f32[512,256]{1,0:T(8,128)S(1)}, f32[512,256]{1,0:T(8,128)S(1)}, u32[]{:S(2)}, u32[]{:S(2)}) collective-permute-start(f32[512,256]{1,0:T(8,128)S(1)} %collective-permute-done.6.refs_1_), channel_id=1, source_target_pairs={{0,4},{4,8},{8,12},{12,14},{14,10},{10,6},{6,2},{2,0},{1,5},{5,9},... | collective-permute-start | bytes 1572872 | tf_op jit(solution)/shard_map/ppermute | solution.py:315
  41.0 22.5 %collective-permute-start.11 = (f32[512,256]{1,0:T(8,128)S(1)}, f32[512,256]{1,0:T(8,128)S(1)}, u32[]{:S(2)}, u32[]{:S(2)}) collective-permute-start(f32[512,256]{1,0:T(8,128)S(1)} %collective-permute-done.10.refs_3_), channel_id=1, source_target_pairs={{4,0},{8,4},{12,8},{14,12},{10,14},{6,10},{2,6},{0,2},{5,1},{9,5},... | collective-permute-start | bytes 1572872 | tf_op jit(solution)/shard_map/ppermute | solution.py:318
  42.9 22.5 %collective-permute-start.5 = (f32[512,256]{1,0:T(8,128)S(1)}, f32[512,256]{1,0:T(8,128)S(1)}, u32[]{:S(2)}, u32[]{:S(2)}) collective-permute-start(f32[512,256]{1,0:T(8,128)S(1)} %collective-permute-done.1.refs_0_), channel_id=1, source_target_pairs={{0,4},{4,8},{8,12},{12,14},{14,10},{10,6},{6,2},{2,0},{1,5},{5,9},... | collective-permute-start | bytes 1572872 | tf_op jit(solution)/shard_map/ppermute | solution.py:315
  53.1 1.0 copy-start.4
  54.1 20.6 %collective-permute-start.18 = (f32[512,256]{1,0:T(8,128)S(1)}, f32[512,256]{1,0:T(8,128)S(1)}, u32[]{:S(2)}, u32[]{:S(2)}) collective-permute-start(f32[512,256]{1,0:T(8,128)S(1)} %collective-permute-done.17.refs_2_), channel_id=1, source_target_pairs={{4,0},{8,4},{12,8},{14,12},{10,14},{6,10},{2,6},{0,2},{5,1},{9,5},... | collective-permute-start | bytes 1572872 | tf_op jit(solution)/shard_map/ppermute | solution.py:318
  55.6 20.9 %collective-permute-start.16 = (f32[512,256]{1,0:T(8,128)S(1)}, f32[512,256]{1,0:T(8,128)S(1)}, u32[]{:S(2)}, u32[]{:S(2)}) collective-permute-start(f32[512,256]{1,0:T(8,128)S(1)} %collective-permute-done.15.refs_1_), channel_id=1, source_target_pairs={{0,4},{4,8},{8,12},{12,14},{14,10},{10,6},{6,2},{2,0},{1,5},{5,9},... | collective-permute-start | bytes 1572872 | tf_op jit(solution)/shard_map/ppermute | solution.py:315
  62.4 1.0 copy-start.1
  63.4 22.1 %collective-permute-start.12 = (f32[512,256]{1,0:T(8,128)S(1)}, f32[512,256]{1,0:T(8,128)S(1)}, u32[]{:S(2)}, u32[]{:S(2)}) collective-permute-start(f32[512,256]{1,0:T(8,128)S(1)} %collective-permute-done.11.refs_3_), channel_id=1, source_target_pairs={{4,0},{8,4},{12,8},{14,12},{10,14},{6,10},{2,6},{0,2},{5,1},{9,5},... | collective-permute-start | bytes 1572872 | tf_op jit(solution)/shard_map/ppermute | solution.py:318
  65.3 21.6 %collective-permute-start.9 = (f32[512,256]{1,0:T(8,128)S(1)}, f32[512,256]{1,0:T(8,128)S(1)}, u32[]{:S(2)}, u32[]{:S(2)}) collective-permute-start(f32[512,256]{1,0:T(8,128)S(1)} %collective-permute-done.5.refs_0_), channel_id=1, source_target_pairs={{0,4},{4,8},{8,12},{12,14},{14,10},{10,6},{6,2},{2,0},{1,5},{5,9},... | collective-permute-start | bytes 1572872 | tf_op jit(solution)/shard_map/ppermute | solution.py:315
  71.8 1.0 copy-start.2
  82.9 6.3 %copy-start.3 = (f32[1024,256]{1,0:T(8,128)}, f32[1024,256]{1,0:T(8,128)S(1)}, u32[]{:S(2)}) copy-start(f32[1024,256]{1,0:T(8,128)S(1)} %gather_product.7.refs_6_) | copy-start | bytes 3145732
  82.9 6.3 %collective-permute-start.19 = (f32[1024,256]{1,0:T(8,128)S(1)}, f32[1024,256]{1,0:T(8,128)}, u32[]{:S(2)}, u32[]{:S(2)}) collective-permute-start(f32[1024,256]{1,0:T(8,128)S(1)} %gather_product.7.refs_6_), channel_id=1, source_target_pairs={{0,1},{1,0},{2,3},{3,2},{4,5},{5,4},{6,7},{7,6},{8,9},{9,8},{10,11... | collective-permute-start | bytes 3145736 | tf_op jit(solution)/shard_map/ppermute | solution.py:321
  85.6 3.7 %collective-permute-start.14 = (f32[512,256]{1,0:T(8,128)S(1)}, f32[512,256]{1,0:T(8,128)S(1)}, u32[]{:S(2)}, u32[]{:S(2)}) collective-permute-start(f32[512,256]{1,0:T(8,128)S(1)} %collective-permute-done.12.refs_1_), channel_id=1, source_target_pairs={{0,1},{1,0},{2,3},{3,2},{4,5},{5,4},{6,7},{7,6},{8,9},{9,8},{10,11... | collective-permute-start | bytes 1572872 | tf_op jit(solution)/shard_map/ppermute | solution.py:321
  87.0 2.3 %collective-permute-start.13 = (f32[512,256]{1,0:T(8,128)S(1)}, f32[512,256]{1,0:T(8,128)S(1)}, u32[]{:S(2)}, u32[]{:S(2)}) collective-permute-start(f32[512,256]{1,0:T(8,128)S(1)} %collective-permute-done.9.refs_0_), channel_id=1, source_target_pairs={{0,1},{1,0},{2,3},{3,2},{4,5},{5,4},{6,7},{7,6},{8,9},{9,8},{10,11... | collective-permute-start | bytes 1572872 | tf_op jit(solution)/shard_map/ppermute | solution.py:321
  104.4 16.3 %collective-permute-start.20 = (f32[512,256]{1,0:T(8,128)S(1)}, f32[512,256]{1,0:T(8,128)S(1)}, u32[]{:S(2)}, u32[]{:S(2)}) collective-permute-start(f32[512,256]{1,0:T(8,128)S(1)} %get-tuple-element.57), channel_id=1, source_target_pairs={{0,4},{4,8},{8,12},{12,14},{14,10},{10,6},{6,2},{2,0},{1,5},{5,9},... | collective-permute-start | bytes 1572872 | tf_op jit(solution)/shard_map/ppermute | solution.py:315
  105.3 17.1 %collective-permute-start.31 = (f32[512,256]{1,0:T(8,128)S(1)}, f32[512,256]{1,0:T(8,128)S(1)}, u32[]{:S(2)}, u32[]{:S(2)}) collective-permute-start(f32[512,256]{1,0:T(8,128)S(1)} %get-tuple-element.68), channel_id=1, source_target_pairs={{4,0},{8,4},{12,8},{14,12},{10,14},{6,10},{2,6},{0,2},{5,1},{9,5},... | collective-permute-start | bytes 1572872 | tf_op jit(solution)/shard_map/ppermute | solution.py:318
  106.5 4.7 %copy-start = (bf16[1024,512]{1,0:T(8,128)(2,1)S(1)}, bf16[1024,512]{1,0:T(8,128)(2,1)}, u32[]{:S(2)}) copy-start(bf16[1024,512]{1,0:T(8,128)(2,1)} %get-tuple-element.52.grad_ref) | copy-start | bytes 3145732
  109.5 15.2 %collective-permute-start.36 = (f32[128,512]{1,0:T(8,128)S(1)}, f32[128,512]{1,0:T(8,128)S(1)}, u32[]{:S(2)}, u32[]{:S(2)}) collective-permute-start(f32[128,512]{1,0:T(8,128)S(1)} %slice_select_fusion.3), channel_id=1, source_target_pairs={{0,2},{2,0},{4,6},{6,4},{8,10},{10,8},{12,14},{14,12},{1,3},{3,1},... | collective-permute-start | bytes 786440 | tf_op jit(solution)/shard_map/ppermute | solution.py:288
  114.9 20.7 %collective-permute-start.24 = (f32[512,256]{1,0:T(8,128)S(1)}, f32[512,256]{1,0:T(8,128)S(1)}, u32[]{:S(2)}, u32[]{:S(2)}) collective-permute-start(f32[512,256]{1,0:T(8,128)S(1)} %get-tuple-element.60), channel_id=1, source_target_pairs={{4,0},{8,4},{12,8},{14,12},{10,14},{6,10},{2,6},{0,2},{5,1},{9,5},... | collective-permute-start | bytes 1572872 | tf_op jit(solution)/shard_map/ppermute | solution.py:318
  119.1 33.6 %collective-permute-start.28 = (f32[512,256]{1,0:T(8,128)S(1)}, f32[512,256]{1,0:T(8,128)S(1)}, u32[]{:S(2)}, u32[]{:S(2)}) collective-permute-start(f32[512,256]{1,0:T(8,128)S(1)} %get-tuple-element.64), channel_id=1, source_target_pairs={{0,4},{4,8},{8,12},{12,14},{14,10},{10,6},{6,2},{2,0},{1,5},{5,9},... | collective-permute-start | bytes 1572872 | tf_op jit(solution)/shard_map/ppermute | solution.py:315
  120.8 26.1 %collective-permute-start.21 = (f32[512,256]{1,0:T(8,128)S(1)}, f32[512,256]{1,0:T(8,128)S(1)}, u32[]{:S(2)}, u32[]{:S(2)}) collective-permute-start(f32[512,256]{1,0:T(8,128)S(1)} %add.127), channel_id=1, source_target_pairs={{0,4},{4,8},{8,12},{12,14},{14,10},{10,6},{6,2},{2,0},{1,5},{5,9},... | collective-permute-start | bytes 1572872 | tf_op jit(solution)/shard_map/ppermute | solution.py:315
  122.5 32.8 %collective-permute-start.32 = (f32[512,256]{1,0:T(8,128)S(1)}, f32[512,256]{1,0:T(8,128)S(1)}, u32[]{:S(2)}, u32[]{:S(2)}) collective-permute-start(f32[512,256]{1,0:T(8,128)S(1)} %add.137), channel_id=1, source_target_pairs={{4,0},{8,4},{12,8},{14,12},{10,14},{6,10},{2,6},{0,2},{5,1},{9,5},... | collective-permute-start | bytes 1572872 | tf_op jit(solution)/shard_map/ppermute | solution.py:318
  124.8 24.5 %collective-permute-start.37 = (f32[128,512]{1,0:T(8,128)S(1)}, f32[128,512]{1,0:T(8,128)S(1)}, u32[]{:S(2)}, u32[]{:S(2)}) collective-permute-start(f32[128,512]{1,0:T(8,128)S(1)} %select_add_fusion), channel_id=1, source_target_pairs={{0,4},{2,6},{4,0},{6,2},{8,12},{10,14},{12,8},{14,10},{1,5},{3,7},... | collective-permute-start | bytes 786440 | tf_op jit(solution)/shard_map/ppermute | solution.py:288
  135.7 41.0 %collective-permute-start.25 = (f32[512,256]{1,0:T(8,128)S(1)}, f32[512,256]{1,0:T(8,128)S(1)}, u32[]{:S(2)}, u32[]{:S(2)}) collective-permute-start(f32[512,256]{1,0:T(8,128)S(1)} %add.131), channel_id=1, source_target_pairs={{4,0},{8,4},{12,8},{14,12},{10,14},{6,10},{2,6},{0,2},{5,1},{9,5},... | collective-permute-start | bytes 1572872 | tf_op jit(solution)/shard_map/ppermute | solution.py:318
  146.9 29.9 %collective-permute-start.22 = (f32[512,256]{1,0:T(8,128)S(1)}, f32[512,256]{1,0:T(8,128)S(1)}, u32[]{:S(2)}, u32[]{:S(2)}) collective-permute-start(f32[512,256]{1,0:T(8,128)S(1)} %add.128), channel_id=1, source_target_pairs={{0,4},{4,8},{8,12},{12,14},{14,10},{10,6},{6,2},{2,0},{1,5},{5,9},... | collective-permute-start | bytes 1572872 | tf_op jit(solution)/shard_map/ppermute | solution.py:315
  149.4 16.9 %collective-permute-start.38 = (f32[128,512]{1,0:T(8,128)S(1)}, f32[128,512]{1,0:T(8,128)S(1)}, u32[]{:S(2)}, u32[]{:S(2)}) collective-permute-start(f32[128,512]{1,0:T(8,128)S(1)} %add.142), channel_id=1, source_target_pairs={{0,8},{2,10},{4,12},{6,14},{8,0},{10,2},{12,4},{14,6},{1,9},{3,11}... | collective-permute-start | bytes 786440 | tf_op jit(solution)/shard_map/ppermute | solution.py:288
  152.7 29.9 %collective-permute-start.29 = (f32[512,256]{1,0:T(8,128)S(1)}, f32[512,256]{1,0:T(8,128)S(1)}, u32[]{:S(2)}, u32[]{:S(2)}) collective-permute-start(f32[512,256]{1,0:T(8,128)S(1)} %add.134), channel_id=1, source_target_pairs={{0,4},{4,8},{8,12},{12,14},{14,10},{10,6},{6,2},{2,0},{1,5},{5,9},... | collective-permute-start | bytes 1572872 | tf_op jit(solution)/shard_map/ppermute | solution.py:315
  155.3 27.5 %collective-permute-start.33 = (f32[512,256]{1,0:T(8,128)S(1)}, f32[512,256]{1,0:T(8,128)S(1)}, u32[]{:S(2)}, u32[]{:S(2)}) collective-permute-start(f32[512,256]{1,0:T(8,128)S(1)} %add.138), channel_id=1, source_target_pairs={{4,0},{8,4},{12,8},{14,12},{10,14},{6,10},{2,6},{0,2},{5,1},{9,5},... | collective-permute-start | bytes 1572872 | tf_op jit(solution)/shard_map/ppermute | solution.py:318
  166.3 18.6 %collective-permute-start.39 = (f32[128,512]{1,0:T(8,128)S(1)}, f32[128,512]{1,0:T(8,128)S(1)}, u32[]{:S(2)}, u32[]{:S(2)}) collective-permute-start(f32[128,512]{1,0:T(8,128)S(1)} %add.143), channel_id=1, source_target_pairs={{0,2},{2,0},{4,6},{6,4},{8,10},{10,8},{12,14},{14,12},{1,3},{3,1},... | collective-permute-start | bytes 786440 | tf_op jit(solution)/shard_map/ppermute | solution.py:288
  176.8 14.9 %collective-permute-start.26 = (f32[512,256]{1,0:T(8,128)S(1)}, f32[512,256]{1,0:T(8,128)S(1)}, u32[]{:S(2)}, u32[]{:S(2)}) collective-permute-start(f32[512,256]{1,0:T(8,128)S(1)} %add.132), channel_id=1, source_target_pairs={{4,0},{8,4},{12,8},{14,12},{10,14},{6,10},{2,6},{0,2},{5,1},{9,5},... | collective-permute-start | bytes 1572872 | tf_op jit(solution)/shard_map/ppermute | solution.py:318
  176.9 14.9 %collective-permute-start.23 = (f32[512,256]{1,0:T(8,128)S(1)}, f32[512,256]{1,0:T(8,128)S(1)}, u32[]{:S(2)}, u32[]{:S(2)}) collective-permute-start(f32[512,256]{1,0:T(8,128)S(1)} %add.129), channel_id=1, source_target_pairs={{0,4},{4,8},{8,12},{12,14},{14,10},{10,6},{6,2},{2,0},{1,5},{5,9},... | collective-permute-start | bytes 1572872 | tf_op jit(solution)/shard_map/ppermute | solution.py:315
  182.7 17.1 %collective-permute-start.30 = (f32[512,256]{1,0:T(8,128)S(1)}, f32[512,256]{1,0:T(8,128)S(1)}, u32[]{:S(2)}, u32[]{:S(2)}) collective-permute-start(f32[512,256]{1,0:T(8,128)S(1)} %add.135), channel_id=1, source_target_pairs={{0,4},{4,8},{8,12},{12,14},{14,10},{10,6},{6,2},{2,0},{1,5},{5,9},... | collective-permute-start | bytes 1572872 | tf_op jit(solution)/shard_map/ppermute | solution.py:315
  182.9 17.0 %collective-permute-start.34 = (f32[512,256]{1,0:T(8,128)S(1)}, f32[512,256]{1,0:T(8,128)S(1)}, u32[]{:S(2)}, u32[]{:S(2)}) collective-permute-start(f32[512,256]{1,0:T(8,128)S(1)} %add.139), channel_id=1, source_target_pairs={{4,0},{8,4},{12,8},{14,12},{10,14},{6,10},{2,6},{0,2},{5,1},{9,5},... | collective-permute-start | bytes 1572872 | tf_op jit(solution)/shard_map/ppermute | solution.py:318
  185.0 15.0 %collective-permute-start.40 = (f32[256,512]{1,0:T(8,128)S(1)}, f32[256,512]{1,0:T(8,128)S(1)}, u32[]{:S(2)}, u32[]{:S(2)}) collective-permute-start(f32[256,512]{1,0:T(8,128)S(1)} %pad_maximum_fusion.2), channel_id=1, source_target_pairs={{0,1},{1,0},{2,3},{3,2},{4,5},{5,4},{6,7},{7,6},{8,9},{9,8},{10,11... | collective-permute-start | bytes 1572872 | tf_op jit(solution)/shard_map/ppermute | solution.py:321
  191.9 9.3 %collective-permute-start.27 = (f32[512,256]{1,0:T(8,128)S(1)}, f32[512,256]{1,0:T(8,128)S(1)}, u32[]{:S(2)}, u32[]{:S(2)}) collective-permute-start(f32[512,256]{1,0:T(8,128)S(1)} %add_add_fusion.1), channel_id=1, source_target_pairs={{0,1},{1,0},{2,3},{3,2},{4,5},{5,4},{6,7},{7,6},{8,9},{9,8},{10,11... | collective-permute-start | bytes 1572872 | tf_op jit(solution)/shard_map/ppermute | solution.py:321
  200.0 2.0 collective-permute-start.35

commit v3 on v2

v3 whole, which is shorter than its diff:
```python
import functools

import jax
import jax.numpy as jnp
from jax import lax
from jax.experimental import pallas as pl
from jax.experimental.pallas import tpu as pltpu
from jax.sharding import PartitionSpec as P

BF16 = jnp.bfloat16
F32 = jnp.float32
MIB = 48
SP_FLOPS = [10000000000,1,10000000000,1,10000000000,1,10000000000]
LAYER_MIB = 40
SMALL = pl.CostEstimate(flops=10_000_000_000, transcendentals=0, bytes_accessed=8_000_000)


def ring_place(index, size):
    if size == 8:
        z, y = index // 2, index % 2
        return z + y * (size - 1 - 2 * z)
    return index


def ring_pairs(size):
    at = {ring_place(i, size): i for i in range(size)}
    ahead = [(at[p], at[(p + 1) % size]) for p in range(size)]
    back = [(b, a) for a, b in ahead]
    return ahead, back


def split_hi_lo(value):
    hi = value.astype(BF16)
    return hi, (value - hi.astype(F32)).astype(BF16)


def dot(a, b, dims=((1,), (0,))):
    return lax.dot_general(a, b, (dims, ((), ())), preferred_element_type=F32)


def params(mib):
    return pltpu.CompilerParams(vmem_limit_bytes=mib * 1024 * 1024)


def after(value, *others):
    return lax.optimization_barrier((value, *others))[0]


def densify_kernel(first, far, place_ref, count_ref, own_ref, other_ref, *refs):
    hi_ref, lo_ref, far_hi_ref, far_lo_ref = refs[-4:]
    row = first + pl.program_id(0)
    hi_ref[...] = jnp.zeros_like(hi_ref)
    lo_ref[...] = jnp.zeros_like(lo_ref)
    tile = own_ref.shape[-1]
    for replica, ref in enumerate((own_ref, other_ref)):

        def body(slot, carry, replica=replica, ref=ref):
            hi, lo = split_hi_lo(ref[0, slot])
            block = place_ref[replica, 0, row, slot]
            column = pl.multiple_of(place_ref[replica, 1, row, slot] * tile, tile)
            hi_ref[block, :, pl.ds(column, tile)] = hi
            lo_ref[block, :, pl.ds(column, tile)] = lo
            return carry

        lax.fori_loop(0, count_ref[replica, row], body, 0)
    far_hi_ref[...] = hi_ref[far]
    far_lo_ref[...] = lo_ref[far]


def densify(dense, tiles, place, count, size, first, last):
    own, other = tiles
    tiles_here, slots, tile, _ = own.shape
    rows = tiles_here * tile
    shape = jax.ShapeDtypeStruct((size, rows, rows), BF16)
    tile_spec = pl.BlockSpec((1, slots, tile, tile), lambda i, *_: (first + i, 0, 0, 0))
    out_spec = pl.BlockSpec((size, tile, rows), lambda i, *_: (0, first + i, 0))
    far_shape = jax.ShapeDtypeStruct((rows, rows), BF16)
    far_spec = pl.BlockSpec((tile, rows), lambda i, *_: (first + i, 0))
    return pl.pallas_call(
        functools.partial(densify_kernel, first, size // 2),
        out_shape=(shape, shape, far_shape, far_shape),
        grid_spec=pltpu.PrefetchScalarGridSpec(
            num_scalar_prefetch=2,
            grid=(last - first,),
            in_specs=[tile_spec, tile_spec] + [pl.BlockSpec(memory_space=pl.ANY)] * len(dense),
            out_specs=(out_spec, out_spec, far_spec, far_spec),
        ),
        input_output_aliases={4 + n: n for n in range(len(dense))},
        compiler_params=params(MIB),
        cost_estimate=pl.CostEstimate(
            flops=0,
            transcendentals=0,
            bytes_accessed=(last - first) * tile * (slots * tile * 8 + size * rows * 4),
        ),
        name="densify",
    )(place, count, own, other, *dense)


def gather_kernel(blocks, *refs):
    x_refs = refs[: 2 * blocks]
    a_refs = refs[2 * blocks : 4 * blocks]
    rest = refs[4 * blocks :]
    total_ref = rest[0] if len(rest) == 3 else None
    out_ref, x_split = rest[-2:]
    half, width = x_refs[0].shape

    @pl.when(pl.program_id(0) == 0)
    def _():
        for n in range(2 * blocks):
            hi, lo = split_hi_lo(x_refs[n][...])
            x_split[pl.ds(n * half, half), pl.ds(0, width)] = hi
            x_split[pl.ds(n * half, half), pl.ds(width, width)] = lo

    acc = None
    for n in range(blocks):
        span = pl.ds(n * 2 * half, 2 * half)
        both = dot(a_refs[2 * n][0], x_split[span, :])
        low = dot(a_refs[2 * n + 1][0], x_split[span, pl.ds(0, width)])
        part = both[:, :width] + both[:, width:] + low
        acc = part if acc is None else acc + part
    if total_ref is not None:
        acc = acc + total_ref[...]
    out_ref[...] = acc


def gather_product(dense, chunks, total):
    size, rows, columns = dense[0].shape
    half, width = chunks[0][1].shape
    blocks = len(chunks)
    step = rows // 2
    full = pl.BlockSpec((half, width), lambda i: (0, 0))
    in_specs = [full] * (2 * blocks)
    operands = [value for _, top, bottom in chunks for value in (top, bottom)]
    for block, _, _ in chunks:
        spec = pl.BlockSpec((1, step, columns), lambda i, block=block: (block, i, 0))
        in_specs += [spec, spec]
        operands += [dense[0], dense[1]]
    row_spec = pl.BlockSpec((step, width), lambda i: (i, 0))
    if total is not None:
        in_specs.append(row_spec)
        operands.append(total)
    return pl.pallas_call(
        functools.partial(gather_kernel, blocks),
        out_shape=jax.ShapeDtypeStruct((rows, width), F32),
        grid=(rows // step,),
        in_specs=in_specs,
        out_specs=row_spec,
        scratch_shapes=[pltpu.VMEM((blocks * 2 * half, 2 * width), BF16)],
        compiler_params=params(MIB),
        cost_estimate=pl.CostEstimate(
            flops=6 * blocks * rows * columns * width,
            transcendentals=0,
            bytes_accessed=blocks * (rows * columns * 4 + columns * width * 4) + rows * width * 8,
        ),
        name="gather_product",
    )(*operands)


def layer_kernel(*refs):
    odd_ref = refs[0]
    x_refs = refs[1:5]
    hi_ref, lo_ref, own_ref, other_ref, cot_ref, whi_ref, wlo_ref = refs[5:12]
    out_ref, pre_grad_ref, mine_ref, sent_ref, x_split, total_ref = refs[12:]
    half, width = x_refs[0].shape
    rows, columns = hi_ref.shape
    step = 512
    for n in range(4):
        hi, lo = split_hi_lo(x_refs[n][...])
        at, side = (n % 2) * half, pl.ds((n // 2) * width, width)
        x_split[pl.ds(at, half), side] = hi
        x_split[pl.ds(columns + at, half), side] = lo
        x_split[pl.ds(2 * columns + at, half), side] = hi
    for first in range(0, rows, step):
        here = pl.ds(first, step)
        hi, lo = hi_ref[here, :], lo_ref[here, :]
        total = dot(jnp.concatenate([hi, hi, lo], 1), x_split[...])
        total = total + jnp.concatenate([own_ref[here, :], other_ref[here, :]], 1)
        hi, lo = split_hi_lo(total)
        total_ref[here, :] = hi[:, :width]
        total_ref[pl.ds(rows + first, step), :] = lo[:, :width]
        w_hi, w_lo = whi_ref[...], wlo_ref[...]
        pre = dot(
            jnp.concatenate([hi, lo, hi], 1), jnp.concatenate([w_hi, w_hi, w_lo], 0)
        )
        sigma = jax.nn.sigmoid(pre)
        out_ref[here, :] = pre * sigma
        pre_grad = cot_ref[here, :] * (sigma * (1.0 + pre * (1.0 - sigma)))
        hi, lo = split_hi_lo(pre_grad)
        pre_grad_ref[here, :] = hi
        pre_grad_ref[pl.ds(rows + first, step), :] = lo
    value = turned_dot(total_ref[pl.ds(0, rows), :], total_ref[pl.ds(rows, rows), :], pre_grad_ref)
    top, bottom = value[: width // 2], value[width // 2 :]
    odd = odd_ref[0]
    mine_ref[...] = jnp.where(odd == 0, top, bottom)
    sent_ref[...] = jnp.where(odd == 0, bottom, top)


def layer_grad_kernel(*refs):
    pre_grad_ref, hi_ref, lo_ref, whi_ref, wlo_ref, grad_ref, top_ref, bottom_ref = refs
    rows = hi_ref.shape[0]
    half, width = top_ref.shape
    step = 512
    mine = pl.ds(0, width)
    for first in range(0, rows, step):
        hi, lo = pre_grad_ref[pl.ds(first, step), :], pre_grad_ref[pl.ds(rows + first, step), :]
        w_hi, w_lo = whi_ref[mine, :], wlo_ref[mine, :]
        grad = dot(
            jnp.concatenate([hi, lo, hi], 1),
            jnp.concatenate([w_hi, w_hi, w_lo], 1),
            ((1,), (1,)),
        )
        hi, lo = split_hi_lo(grad)
        grad_ref[pl.ds(first, step), :] = hi
        grad_ref[pl.ds(rows + first, step), :] = lo
    for first in range(0, 2 * half, 256):
        part = turned_dot(hi_ref[:, pl.ds(first, 256)], lo_ref[:, pl.ds(first, 256)], grad_ref)
        if first < half:
            top_ref[pl.ds(first, 256), :] = part
        else:
            bottom_ref[pl.ds(first - half, 256), :] = part


def turned_dot(hi, lo, right_ref):
    rows = hi.shape[0]
    right_hi, right_lo = right_ref[pl.ds(0, rows), :], right_ref[pl.ds(rows, rows), :]
    left = jnp.concatenate([hi, hi, lo], 0)
    return dot(left, jnp.concatenate([right_hi, right_lo, right_hi], 0), ((0,), (0,)))


def layer(odd, far, x_own, x_other, own, other, cotangent, w_hi, w_lo):
    rows, columns = far[0].shape
    width = own.shape[1]
    features = cotangent.shape[1]
    whole = pl.BlockSpec(memory_space=pltpu.VMEM)
    return pl.pallas_call(
        layer_kernel,
        out_shape=(
            jax.ShapeDtypeStruct((rows, features), F32),
            jax.ShapeDtypeStruct((2 * rows, features), BF16),
            jax.ShapeDtypeStruct((width // 2, features), F32),
            jax.ShapeDtypeStruct((width // 2, features), F32),
        ),
        in_specs=[pl.BlockSpec(memory_space=pltpu.SMEM)] + [whole] * 11,
        out_specs=(whole,) * 4,
        scratch_shapes=[
            pltpu.VMEM((3 * columns, features), BF16),
            pltpu.VMEM((2 * rows, width), BF16),
        ],
        compiler_params=params(LAYER_MIB),
        cost_estimate=pl.CostEstimate(flops=1, transcendentals=0, bytes_accessed=1),
        name="layer",
    )(odd, *x_own, *x_other, *far, own, other, cotangent, w_hi, w_lo)


def layer_grad(pre_grad, far, w_hi, w_lo):
    rows, columns = far[0].shape
    width = w_hi.shape[0] // 2
    whole = pl.BlockSpec(memory_space=pltpu.VMEM)
    return pl.pallas_call(
        layer_grad_kernel,
        out_shape=(
            jax.ShapeDtypeStruct((2 * rows, width), BF16),
            jax.ShapeDtypeStruct((columns // 2, width), F32),
            jax.ShapeDtypeStruct((columns // 2, width), F32),
        ),
        in_specs=[whole] * 5,
        out_specs=(whole,) * 3,
        compiler_params=params(LAYER_MIB),
        cost_estimate=pl.CostEstimate(flops=1, transcendentals=0, bytes_accessed=1),
        name="layer_grad",
    )(pre_grad, *far, w_hi, w_lo)


def scatter_kernel(*refs):
    grad_ref, hi_ref, lo_ref = refs[:3]
    came, outs = refs[3:-2], refs[-2:]
    part = turned_dot(hi_ref[0], lo_ref[0], grad_ref)
    step = part.shape[0]
    per_side = outs[0].shape[0] // step
    at = pl.program_id(0)
    for side in range(2):

        @pl.when(at // per_side == side)
        def _(side=side):
            here = pl.ds((at % per_side) * step, step)
            outs[side][here, :] = part + came[side][here, :] if came else part


def scatter_product(dense, grad, blocks, parts, carried=()):
    flops = SP_FLOPS[(0 if blocks[0] == 0 else (6 - 2 * blocks[0]) + (2 if parts[0] == 0 else 1)) if dense[0].shape[0] == 8 else 0]
    size, rows, columns = dense[0].shape
    width = grad.shape[1]
    half = columns // 2
    step = 256
    per_side = half // step

    def place(i):
        side = i // per_side
        block = blocks[0] + side * (blocks[1] - blocks[0])
        part = parts[0] + side * (parts[1] - parts[0])
        return (block, 0, part * per_side + i % per_side)

    a_spec = pl.BlockSpec((1, rows, step), place)
    whole = pl.BlockSpec(memory_space=pltpu.VMEM)
    return pl.pallas_call(
        scatter_kernel,
        out_shape=(jax.ShapeDtypeStruct((half, width), F32),) * 2,
        grid=(2 * per_side,),
        in_specs=[whole, a_spec, a_spec] + [whole] * len(carried),
        out_specs=(whole, whole),
        compiler_params=params(MIB),
        cost_estimate=pl.CostEstimate(flops=flops, transcendentals=0, bytes_accessed=1),
        name="scatter_product",
    )(grad, dense[0], dense[1], *carried)


def per_device(features, weight, cotangent, tile_vals, col_tile, counts):
    size = lax.axis_size("row")
    hops = size // 2
    rep = lax.axis_index("rep")
    row = lax.axis_index("row")
    tiles_here = tile_vals.shape[0]
    width = features.shape[1] // 2
    half = features.shape[0] // 2
    ahead, back = ring_pairs(size)

    def forth(block):
        return lax.ppermute(block, "row", ahead)

    def rear(block):
        return lax.ppermute(block, "row", back)

    def swap(block):
        return lax.ppermute(block, "rep", [(0, 1), (1, 0)])

    def order(own, other, axis):
        low = jnp.where(rep == 0, own, other)
        high = jnp.where(rep == 0, other, own)
        return jnp.concatenate([low, high], axis)

    top = lax.dynamic_slice(features, (0, rep * width), (half, width))
    bottom = lax.dynamic_slice(features, (half, rep * width), (half, width))

    own_tiles = tile_vals[:, 0]
    other_tiles = swap(own_tiles)
    first_hop = (forth(top), rear(bottom))
    table = after(jnp.concatenate([col_tile[:, 0], counts], 1), *first_hop)
    tables = jnp.stack([table, swap(table)])
    columns = tables[:, :, :-1]
    block = jnp.mod(ring_place(columns // tiles_here, size) - ring_place(row, size), size)
    place = jnp.stack([block, columns % tiles_here], 1)
    count = tables[:, :, -1]

    w_own = jnp.where(rep == 0, weight[:width], weight[width:])
    w_other = jnp.where(rep == 0, weight[width:], weight[:width])
    w_rows = jnp.concatenate([w_own, w_other], 0)
    w_high = lax.reduce_precision(w_rows, 8, 7)
    w_hi, w_lo = w_high.astype(BF16), (w_rows - w_high).astype(BF16)

    dense, total = (), None
    cuts = [0, tiles_here * 3 // 8, tiles_here * 3 // 4, tiles_here]
    ready = []

    def next_piece():
        nonlocal dense
        done = next_piece.done
        if done < 3:
            dense = densify(
                dense, (own_tiles, other_tiles), place, count, size, cuts[done], cuts[done + 1]
            )
            next_piece.done += 1
            if next_piece.done < 3:
                return dense
        return multiply_ready()

    next_piece.done = 0

    def multiply_ready():
        nonlocal total
        if next_piece.done == 3 and ready:
            total = gather_product(dense[:2], ready.pop(0), total)
            return (total,)
        return ()

    ready.append([(0, top, bottom)])
    forward_top, forward_bottom, rear_top, rear_bottom = top, bottom, top, bottom
    covered = (w_hi, w_lo)
    for hop in range(1, hops + 1):
        if hop > 2:
            covered = next_piece()
        if hop > 1:
            forward_top, rear_bottom = (after(v, *covered) for v in (forward_top, rear_bottom))
            forward_top, rear_bottom = forth(forward_top), rear(rear_bottom)
        else:
            forward_top, rear_bottom = first_hop
        if hop < hops:
            if hop > 1:
                covered = next_piece()
                forward_bottom, rear_top = (after(v, *covered) for v in (forward_bottom, rear_top))
            forward_bottom = forth(forward_bottom)
            rear_top = rear(rear_top)
            ready.append(
                [(size - hop, forward_top, forward_bottom), (hop, rear_top, rear_bottom)]
            )
    while ready:
        multiply_ready()
    x_last = (forward_top, rear_bottom)
    other_total = swap(total)
    x_other = tuple(swap(v) for v in x_last)
    odd = jnp.mod(row, 2)
    output, pre_grad, weight_mine, weight_sent = layer(
        odd.reshape(1), dense[2:], x_last, x_other, total, other_total, cotangent, w_hi, w_lo
    )


    def exchange(block, distance):
        return lax.ppermute(block, "row", [(i, i ^ distance) for i in range(size)])

    weight_mine = weight_mine + exchange(weight_sent, 1)
    distance = 2
    while distance < size:
        weight_mine = weight_mine + exchange(weight_mine, distance)
        distance *= 2
    weight_theirs = exchange(weight_mine, 1)
    low = jnp.where(odd == 0, weight_mine, weight_theirs)
    high = jnp.where(odd == 0, weight_theirs, weight_mine)
    weight_half = jnp.concatenate([low, high], 0)
    grad, first_top, first_bottom = layer_grad(pre_grad, dense[2:], w_hi, w_lo)
    tops = (forth(first_top), rear(first_bottom))
    bottoms = ()
    for hop in range(hops - 1, 0, -1):
        blocks = (hop, size - hop)
        result = scatter_product(dense[:2], grad, blocks, (1, 0), bottoms)
        bottoms = (forth(result[0]), rear(result[1]))
        result = scatter_product(dense[:2], grad, blocks, (0, 1), tops)
        tops = (forth(result[0]), rear(result[1]))
    home_top, home_bottom = scatter_product(dense[:2], after(grad, *result), (0, 0), (0, 1))
    weight_grad = order(weight_half, swap(weight_half), 0)
    home_bottom = home_bottom + bottoms[0] + tops[1]
    home_top = home_top + bottoms[1] + tops[0]
    input_grad = jnp.concatenate(
        [order(home_top, swap(home_top), 1), order(home_bottom, swap(home_bottom), 1)], 0
    )
    return (output, input_grad, weight_grad)


def solution(mesh):
    return jax.shard_map(
        per_device,
        mesh=mesh,
        in_specs=(
            P(("groups", "row"), None),
            P(),
            P(("groups", "row"), None),
            P(("groups", "row"), "rep", None, None, None),
            P(("groups", "row"), "rep", None),
            P(("groups", "row"), "rep"),
        ),
        out_specs=(P(("groups", "row"), None), P(("groups", "row"), None), P("groups", None)),
        check_vma=False,
    )
```

time: 204 us -> 201 us (0.985)
  starting transfers between devices: 44.6 us -> 37.6 us
  waiting for transfers between devices: 56.7 us -> 63.3 us
  matrix products: 3.02 us -> 0 us
  Pallas kernels: 87.3 us -> 90.2 us
    ppermute x4, waiting for transfers between devices: 11.1 us -> 31.7 us  [exchange(): return lax.ppermute(block, 'row', [(i, i ^ distance) for i in range(size)])]
    ppermute x14, starting transfers between devices: 10.2 us -> 26.7 us  [forth(): return lax.ppermute(block, 'row', ahead)]
    ppermute x14, starting transfers between devices: 21.5 us -> 6.1 us  [rear(): return lax.ppermute(block, 'row', back)]
    pallas_call x10 -> x11, Pallas kernels: 49.4 us -> 59.4 us  [the longest x7 33 us: scatter_product(): pl.pallas_call(scatter_kernel, out_shape=(jax.ShapeDtypeStruct((half, wid...]
    ppermute x4, starting transfers between devices: 11.6 us -> 3.03 us  [exchange(): return lax.ppermute(block, 'row', [(i, i ^ distance) for i in range(size)])]
    pallas_call x1, Pallas kernels: 15.2 us -> 7.6 us  [layer(): pl.pallas_call(layer_kernel, out_shape=(jax.ShapeDtypeStruct((rows, featu...]
    ppermute x14, waiting for transfers between devices: 17 us -> 10.4 us  [rear(): return lax.ppermute(block, 'row', back)]
    ppermute x9 -> x8, waiting for transfers between devices: 8.45 us -> 4.06 us  [swap(): return lax.ppermute(block, 'rep', [(0, 1), (1, 0)])]
  transfers between devices with their start and end apart: 41 -> 40, of which waited for: 17 -> 15; matrix products, arithmetic and copies ran while one was open for 5% -> 3% of each run, Pallas kernels for 35% -> 40%
where the time goes in v3:
time: 201 us
  Pallas kernels  90.2 us (45%)
  waiting for transfers between devices  63.3 us (31%)
  starting transfers between devices  37.6 us (19%)
  other arithmetic  6.95 us (3%)
    pallas_call x7, Pallas kernels, scatter_product(): pl.pallas_call(scatter_kernel, out_shape=(jax.ShapeDtypeStruct((half, wid...  33 us
    ppermute x4, waiting for transfers between devices, exchange(): return lax.ppermute(block, 'row', [(i, i ^ distance) for i in range(size)])  31.7 us
    ppermute x14, starting transfers between devices, forth(): return lax.ppermute(block, 'row', ahead)  26.7 us
    pallas_call x3, Pallas kernels, densify(): pl.pallas_call(functools.partial(densify_kernel, first, size // 2), out_s...  23.7 us
    pallas_call x4, Pallas kernels, gather_product(): pl.pallas_call(functools.partial(gather_kernel, blocks), out_shape=jax.Sh...  23.2 us
    ppermute x14, waiting for transfers between devices, forth(): return lax.ppermute(block, 'row', ahead)  17.1 us
    ppermute x14, waiting for transfers between devices, rear(): return lax.ppermute(block, 'row', back)  10.4 us
    pallas_call x1, Pallas kernels, layer(): pl.pallas_call(layer_kernel, out_shape=(jax.ShapeDtypeStruct((rows, featu...  7.6 us
  transfers between devices with their start and end apart: 40, of which 15 were waited for; matrix products, arithmetic and copies ran while one was open for 3% of the time, Pallas kernels for 40%

profile of v3, /device:TPU:0, one launch (start us, length us, event | category | flops | bytes accessed | tf_op | source)
XLA Modules:
  0.0 200.5 jit_solution(13981677136364769264)
XLA Ops:
  1.2 1.3 constant_dynamic-slice_fusion
  2.5 2.7 %collective-permute-start = (f32[512,256]{1,0:T(8,128)S(1)}, f32[512,256]{1,0:T(8,128)S(1)}, u32[]{:S(2)}, u32[]{:S(2)}) collective-permute-start(f32[512,256]{1,0:T(8,128)S(1)} %get-tuple-element.94.refs_0_), channel_id=1, source_target_pairs={{0,4},{4,8},{8,12},{12,14},{14,10},{10,6},{6,2},{2,0},{1,5},{5,9},... | collective-permute-start | bytes 1572872 | tf_op jit(solution)/shard_map/ppermute | solution.py:328
  5.2 2.0 %collective-permute-start.6 = (f32[512,256]{1,0:T(8,128)S(1)}, f32[512,256]{1,0:T(8,128)}, u32[]{:S(2)}, u32[]{:S(2)}) collective-permute-start(f32[512,256]{1,0:T(8,128)S(1)} %get-tuple-element.93.refs_1_), channel_id=1, source_target_pairs={{0,4},{4,8},{8,12},{12,14},{14,10},{10,6},{6,2},{2,0},{1,5},{5,9},... | collective-permute-start | bytes 1572872 | tf_op jit(solution)/shard_map/ppermute | solution.py:328
  7.2 1.1 slice_select_fusion.1
  8.4 1.4 fusion
  9.8 8.1 %collective-permute-done.refs_0_ = f32[512,256]{1,0:T(8,128)S(1)} collective-permute-done((f32[512,256]{1,0:T(8,128)S(1)}, f32[512,256]{1,0:T(8,128)S(1)}, u32[]{:S(2)}, u32[]{:S(2)}) %collective-permute-start) | collective-permute-done | bytes 524320 | tf_op jit(solution)/shard_map/ppermute | solution.py:328
  17.9 2.1 %collective-permute-done.2.refs_3_ = f32[512,256]{1,0:T(8,128)S(1)} collective-permute-done((f32[512,256]{1,0:T(8,128)S(1)}, f32[512,256]{1,0:T(8,128)S(1)}, u32[]{:S(2)}, u32[]{:S(2)}) %collective-permute-start.2) | collective-permute-done | bytes 524320 | tf_op jit(solution)/shard_map/ppermute | solution.py:331
  19.9 1.2 collective-permute-done.3
  21.1 1.6 collective-permute-start.1
  23.0 8.9 %densify.3 = (bf16[8,1024,1024]{2,1,0:T(8,128)(2,1)}, bf16[8,1024,1024]{2,1,0:T(8,128)(2,1)}, bf16[1024,1024]{1,0:T(8,128)(2,1)S(1)}, bf16[1024,1024]{1,0:T(8,128)(2,1)S(1)}) custom-call(s32[2,2,8,16]{3,2,1,0:T(8,128)S(1)} %pad_add_fusion.place_ref, s32[2,8]{1,0:T(2,128)S(1)} %fusion.7.count_ref, f32[8,16,128,128]{3,2,1,0:T(8,128)} %bitcast.12, ...), custom_call_target="tpu_custom_call" | custom-call | bytes 18874368 | tf_op jit(solution)/shard_map/densify/pallas_call | solution.py:79
  31.9 2.0 %collective-permute-start.14 = (f32[512,256]{1,0:T(8,128)}, f32[512,256]{1,0:T(8,128)S(1)}, u32[]{:S(2)}, u32[]{:S(2)}) collective-permute-start(f32[512,256]{1,0:T(8,128)} %collective-permute-done.6.refs_1_), channel_id=1, source_target_pairs={{0,4},{4,8},{8,12},{12,14},{14,10},{10,6},{6,2},{2,0},{1,5},{5,9},... | collective-permute-start | bytes 1572872 | tf_op jit(solution)/shard_map/ppermute | solution.py:328
  33.9 8.7 %densify.4 = (bf16[8,1024,1024]{2,1,0:T(8,128)(2,1)}, bf16[8,1024,1024]{2,1,0:T(8,128)(2,1)}, bf16[1024,1024]{1,0:T(8,128)(2,1)S(1)}, bf16[1024,1024]{1,0:T(8,128)(2,1)S(1)}) custom-call(s32[2,2,8,16]{3,2,1,0:T(8,128)S(1)} %pad_add_fusion.place_ref, ...), custom_call_target="tpu_custom_call", output_to_operand_aliasing={{0}: (4, {}), {1}: (5, {}), {2}: (6, {}), {3}: (7, {})} | custom-call | bytes 18874368 | tf_op jit(solution)/shard_map/densify/pallas_call | solution.py:79
  42.7 2.0 %collective-permute-start.5 = (f32[512,256]{1,0:T(8,128)S(1)}, f32[512,256]{1,0:T(8,128)S(1)}, u32[]{:S(2)}, u32[]{:S(2)}) collective-permute-start(f32[512,256]{1,0:T(8,128)S(1)} %collective-permute-done.1.refs_0_), channel_id=1, source_target_pairs={{0,4},{4,8},{8,12},{12,14},{14,10},{10,6},{6,2},{2,0},{1,5},{5,9},... | collective-permute-start | bytes 1572872 | tf_op jit(solution)/shard_map/ppermute | solution.py:328
  44.7 6.1 %densify.5 = (bf16[8,1024,1024]{2,1,0:T(8,128)(2,1)}, bf16[8,1024,1024]{2,1,0:T(8,128)(2,1)}, bf16[1024,1024]{1,0:T(8,128)(2,1)S(1)}, bf16[1024,1024]{1,0:T(8,128)(2,1)S(1)}) custom-call(s32[2,2,8,16]{3,2,1,0:T(8,128)S(1)} %pad_add_fusion.place_ref, ...), custom_call_target="tpu_custom_call", output_to_operand_aliasing={{0}: (4, {}), {1}: (5, {}), {2}: (6, {}), {3}: (7, {})} | custom-call | bytes 12582912 | tf_op jit(solution)/shard_map/densify/pallas_call | solution.py:79
  50.7 3.7 %gather_product.4.refs_8_ = f32[1024,256]{1,0:T(8,128)S(1)} custom-call(f32[512,256]{1,0:T(8,128)S(1)} %get-tuple-element.94.refs_0_, f32[512,256]{1,0:T(8,128)S(1)} %get-tuple-element.93.refs_1_, bf16[8,1024,1024]{2,1,0:T(8,128)(2,1)} %get-tuple-element.59.refs_2_.refs_4_.refs_6_.refs_1_, ...), custom_call_target="tpu_custom_call" | custom-call | flops 1610612736 | bytes 7340032 | tf_op jit(solution)/shard_map/gather_product/pallas_call | solution.py:142
  54.5 2.0 %collective-permute-start.15 = (f32[512,256]{1,0:T(8,128)S(1)}, f32[512,256]{1,0:T(8,128)S(1)}, u32[]{:S(2)}, u32[]{:S(2)}) collective-permute-start(f32[512,256]{1,0:T(8,128)S(1)} %collective-permute-done.14.refs_1_), channel_id=1, source_target_pairs={{0,4},{4,8},{8,12},{12,14},{14,10},{10,6},{6,2},{2,0},{1,5},{5,9},... | collective-permute-start | bytes 1572872 | tf_op jit(solution)/shard_map/ppermute | solution.py:328
  56.6 7.1 %gather_product.5.refs_8_ = f32[1024,256]{1,0:T(8,128)S(1)} custom-call(f32[512,256]{1,0:T(8,128)S(1)} %collective-permute-done.refs_0_, f32[512,256]{1,0:T(8,128)} %collective-permute-done.6.refs_1_, f32[512,256]{1,0:T(8,128)} %collective-permute-done.7.refs_2_, f32[512,256]{1,0:T(8,128)S(1)} %collective-permute-done.2.refs_3_, ...), custom_call_target="tpu_custom_call" | custom-call | flops 3221225472 | bytes 12582912 | tf_op jit(solution)/shard_map/gather_product/pallas_call | solution.py:142
  63.7 1.2 collective-permute-done.10.refs_3_
  64.9 2.0 %collective-permute-start.8 = (f32[512,256]{1,0:T(8,128)S(1)}, f32[512,256]{1,0:T(8,128)S(1)}, u32[]{:S(2)}, u32[]{:S(2)}) collective-permute-start(f32[512,256]{1,0:T(8,128)S(1)} %collective-permute-done.5.refs_0_), channel_id=1, source_target_pairs={{0,4},{4,8},{8,12},{12,14},{14,10},{10,6},{6,2},{2,0},{1,5},{5,9},... | collective-permute-start | bytes 1572872 | tf_op jit(solution)/shard_map/ppermute | solution.py:328
  66.9 6.2 %gather_product.6.refs_8_ = f32[1024,256]{1,0:T(8,128)S(1)} custom-call(f32[512,256]{1,0:T(8,128)S(1)} %collective-permute-done.1.refs_0_, f32[512,256]{1,0:T(8,128)S(1)} %collective-permute-done.14.refs_1_, f32[512,256]{1,0:T(8,128)S(1)} %collective-permute-done.16.refs_2_, f32[512,256]{1,0:T(8,128)S(1)} %collective-permute-done.9.refs_3_, ...), custom_call_target="tpu_custom_call" | custom-call | flops 3221225472 | bytes 12582912 | tf_op jit(solution)/shard_map/gather_product/pallas_call | solution.py:142
  73.1 3.0 %collective-permute-done.17.refs_2_ = f32[512,256]{1,0:T(8,128)S(1)} collective-permute-done((f32[512,256]{1,0:T(8,128)S(1)}, f32[512,256]{1,0:T(8,128)S(1)}, u32[]{:S(2)}, u32[]{:S(2)}) %collective-permute-start.17) | collective-permute-done | bytes 524320 | tf_op jit(solution)/shard_map/ppermute | solution.py:331
  76.1 6.2 %gather_product.7.refs_7_ = f32[1024,256]{1,0:T(8,128)S(1)} custom-call(f32[512,256]{1,0:T(8,128)S(1)} %collective-permute-done.5.refs_0_, f32[512,256]{1,0:T(8,128)S(1)} %collective-permute-done.15.refs_1_, f32[512,256]{1,0:T(8,128)S(1)} %collective-permute-done.17.refs_2_, f32[512,256]{1,0:T(8,128)S(1)} %collective-permute-done.10.refs_3_, ...), custom_call_target="tpu_custom_call" | custom-call | flops 3221225472 | bytes 12582912 | tf_op jit(solution)/shard_map/gather_product/pallas_call | solution.py:142
  82.4 4.1 %collective-permute-done.11.refs_2_ = f32[512,256]{1,0:T(8,128)S(1)} collective-permute-done((f32[512,256]{1,0:T(8,128)S(1)}, f32[512,256]{1,0:T(8,128)S(1)}, u32[]{:S(2)}, u32[]{:S(2)}) %collective-permute-start.11) | collective-permute-done | bytes 524320 | tf_op jit(solution)/shard_map/ppermute | solution.py:331
  87.1 1.4 collective-permute-done.13.refs_4_
  89.2 7.6 %layer.1 = (f32[1024,512]{1,0:T(8,128)}, bf16[2048,512]{1,0:T(8,128)(2,1)S(1)}, f32[128,512]{1,0:T(8,128)S(1)}, f32[128,512]{1,0:T(8,128)S(1)}) custom-call(s32[1]{0:T(128)} %bitcast.refs_0_, f32[512,256]{1,0:T(8,128)S(1)} %collective-permute-done.8.refs_1_, f32[512,256]{1,0:T(8,128)S(1)} %collective-permute-done.11.refs_2_, ...), custom_call_target="tpu_custom_call" | custom-call | flops 1 | bytes 1 | tf_op jit(solution)/shard_map/layer/pallas_call | solution.py:235
  96.8 2.7 %layer_grad.1 = (bf16[2048,256]{1,0:T(8,128)(2,1)S(1)}, f32[512,256]{1,0:T(8,128)S(1)}, f32[512,256]{1,0:T(8,128)S(1)}) custom-call(bf16[2048,512]{1,0:T(8,128)(2,1)S(1)} %get-tuple-element.72.refs_0_, bf16[1024,1024]{1,0:T(8,128)(2,1)S(1)} %get-tuple-element.65.refs_5_.refs_1_, bf16[1024,1024]{1,0:T(8,128)(2,1)S(1)} %get-tuple-element.66.refs_6_.refs_2_, ...), custom_call_target="tpu_custom_call" | custom-call | flops 1 | bytes 1 | tf_op jit(solution)/shard_map/layer_grad/pallas_call | solution.py:259
  99.6 1.6 collective-permute-start.19
  101.9 4.5 %scatter_product.11 = (f32[512,256]{1,0:T(8,128)S(1)}, f32[512,256]{1,0:T(8,128)S(1)}) custom-call(bf16[2048,256]{1,0:T(8,128)(2,1)S(1)} %get-tuple-element.82.refs_0_, bf16[8,1024,1024]{2,1,0:T(8,128)(2,1)} %get-tuple-element.59.refs_2_.refs_4_.refs_6_.refs_1_, bf16[8,1024,1024]{2,1,0:T(8,128)(2,1)} %get-tuple-element.60.refs_3_.refs_5_.refs_7_.refs_2_), custom_call_target="tpu_custom_call" | custom-call | flops 1 | bytes 1 | tf_op jit(solution)/shard_map/scatter_product/pallas_call | solution.py:305
  106.4 1.7 collective-permute-start.25
  108.5 11.5 %collective-permute-done.35 = f32[128,512]{1,0:T(8,128)S(1)} collective-permute-done((f32[128,512]{1,0:T(8,128)S(1)}, f32[128,512]{1,0:T(8,128)S(1)}, u32[]{:S(2)}, u32[]{:S(2)}) %collective-permute-start.35) | collective-permute-done | bytes 262176 | tf_op jit(solution)/shard_map/ppermute | solution.py:417
  120.1 4.5 %scatter_product.7 = (f32[512,256]{1,0:T(8,128)S(1)}, f32[512,256]{1,0:T(8,128)S(1)}) custom-call(bf16[2048,256]{1,0:T(8,128)(2,1)S(1)} %get-tuple-element.82.refs_0_, bf16[8,1024,1024]{2,1,0:T(8,128)(2,1)} %get-tuple-element.59.refs_2_.refs_4_.refs_6_.refs_1_, bf16[8,1024,1024]{2,1,0:T(8,128)(2,1)} %get-tuple-element.60.refs_3_.refs_5_.refs_7_.refs_2_, ...), custom_call_target="tpu_custom_call" | custom-call | flops 10000000000 | bytes 1 | tf_op jit(solution)/shard_map/scatter_product/pallas_call | solution.py:305
  124.7 2.0 %collective-permute-start.21 = (f32[512,256]{1,0:T(8,128)S(1)}, f32[512,256]{1,0:T(8,128)S(1)}, u32[]{:S(2)}, u32[]{:S(2)}) collective-permute-start(f32[512,256]{1,0:T(8,128)S(1)} %get-tuple-element.76), channel_id=1, source_target_pairs={{0,4},{4,8},{8,12},{12,14},{14,10},{10,6},{6,2},{2,0},{1,5},{5,9},... | collective-permute-start | bytes 1572872 | tf_op jit(solution)/shard_map/ppermute | solution.py:328
  127.1 5.8 %collective-permute-done.36 = f32[128,512]{1,0:T(8,128)S(1)} collective-permute-done((f32[128,512]{1,0:T(8,128)S(1)}, f32[128,512]{1,0:T(8,128)S(1)}, u32[]{:S(2)}, u32[]{:S(2)}) %collective-permute-start.36) | collective-permute-done | bytes 262176 | tf_op jit(solution)/shard_map/ppermute | solution.py:417
  132.9 2.6 %collective-permute-start.37 = (f32[128,512]{1,0:T(8,128)S(1)}, f32[128,512]{1,0:T(8,128)S(1)}, u32[]{:S(2)}, u32[]{:S(2)}) collective-permute-start(f32[128,512]{1,0:T(8,128)S(1)} %add.65), channel_id=1, source_target_pairs={{0,8},{2,10},{4,12},{6,14},{8,0},{10,2},{12,4},{14,6},{1,9},{3,11}... | collective-permute-start | bytes 786440 | tf_op jit(solution)/shard_map/ppermute | solution.py:417
  135.5 4.5 %scatter_product.12 = (f32[512,256]{1,0:T(8,128)S(1)}, f32[512,256]{1,0:T(8,128)S(1)}) custom-call(bf16[2048,256]{1,0:T(8,128)(2,1)S(1)} %get-tuple-element.82.refs_0_, bf16[8,1024,1024]{2,1,0:T(8,128)(2,1)} %get-tuple-element.59.refs_2_.refs_4_.refs_6_.refs_1_, bf16[8,1024,1024]{2,1,0:T(8,128)(2,1)} %get-tuple-element.60.refs_3_.refs_5_.refs_7_.refs_2_, ...), custom_call_target="tpu_custom_call" | custom-call | flops 1 | bytes 1 | tf_op jit(solution)/shard_map/scatter_product/pallas_call | solution.py:305
  140.1 2.0 %collective-permute-start.28 = (f32[512,256]{1,0:T(8,128)S(1)}, f32[512,256]{1,0:T(8,128)S(1)}, u32[]{:S(2)}, u32[]{:S(2)}) collective-permute-start(f32[512,256]{1,0:T(8,128)S(1)} %get-tuple-element.87), channel_id=1, source_target_pairs={{4,0},{8,4},{12,8},{14,12},{10,14},{6,10},{2,6},{0,2},{5,1},{9,5},... | collective-permute-start | bytes 1572872 | tf_op jit(solution)/shard_map/ppermute | solution.py:331
  142.1 13.3 %collective-permute-done.37 = f32[128,512]{1,0:T(8,128)S(1)} collective-permute-done((f32[128,512]{1,0:T(8,128)S(1)}, f32[128,512]{1,0:T(8,128)S(1)}, u32[]{:S(2)}, u32[]{:S(2)}) %collective-permute-start.37) | collective-permute-done | bytes 262176 | tf_op jit(solution)/shard_map/ppermute | solution.py:417
  155.5 5.5 %scatter_product.8 = (f32[512,256]{1,0:T(8,128)}, f32[512,256]{1,0:T(8,128)}) custom-call(bf16[2048,256]{1,0:T(8,128)(2,1)S(1)} %get-tuple-element.82.refs_0_, bf16[8,1024,1024]{2,1,0:T(8,128)(2,1)} %get-tuple-element.59.refs_2_.refs_4_.refs_6_.refs_1_, bf16[8,1024,1024]{2,1,0:T(8,128)(2,1)} %get-tuple-element.60.refs_3_.refs_5_.refs_7_.refs_2_, ...), custom_call_target="tpu_custom_call" | custom-call | flops 10000000000 | bytes 1 | tf_op jit(solution)/shard_map/scatter_product/pallas_call | solution.py:305
  161.0 2.0 %collective-permute-start.24 = (f32[512,256]{1,0:T(8,128)}, f32[512,256]{1,0:T(8,128)}, u32[]{:S(2)}, u32[]{:S(2)}) collective-permute-start(f32[512,256]{1,0:T(8,128)} %get-tuple-element.79), channel_id=1, source_target_pairs={{4,0},{8,4},{12,8},{14,12},{10,14},{6,10},{2,6},{0,2},{5,1},{9,5},... | collective-permute-start | bytes 1572872 | tf_op jit(solution)/shard_map/ppermute | solution.py:331
  163.0 1.2 collective-permute-done.38
  165.4 4.5 %scatter_product.13 = (f32[512,256]{1,0:T(8,128)S(1)}, f32[512,256]{1,0:T(8,128)S(1)}) custom-call(bf16[2048,256]{1,0:T(8,128)(2,1)S(1)} %get-tuple-element.82.refs_0_, bf16[8,1024,1024]{2,1,0:T(8,128)(2,1)} %get-tuple-element.59.refs_2_.refs_4_.refs_6_.refs_1_, bf16[8,1024,1024]{2,1,0:T(8,128)(2,1)} %get-tuple-element.60.refs_3_.refs_5_.refs_7_.refs_2_, ...), custom_call_target="tpu_custom_call" | custom-call | flops 1 | bytes 1 | tf_op jit(solution)/shard_map/scatter_product/pallas_call | solution.py:305
  170.8 1.2 collective-permute-start.32
  172.0 4.9 %scatter_product.9 = (f32[512,256]{1,0:T(8,128)S(1)}, f32[512,256]{1,0:T(8,128)S(1)}) custom-call(bf16[2048,256]{1,0:T(8,128)(2,1)S(1)} %get-tuple-element.82.refs_0_, bf16[8,1024,1024]{2,1,0:T(8,128)(2,1)} %get-tuple-element.59.refs_2_.refs_4_.refs_6_.refs_1_, bf16[8,1024,1024]{2,1,0:T(8,128)(2,1)} %get-tuple-element.60.refs_3_.refs_5_.refs_7_.refs_2_, ...), custom_call_target="tpu_custom_call" | custom-call | flops 10000000000 | bytes 1 | tf_op jit(solution)/shard_map/scatter_product/pallas_call | solution.py:305
  176.9 5.6 %collective-permute-start.30 = (f32[512,256]{1,0:T(8,128)S(1)}, f32[512,256]{1,0:T(8,128)S(1)}, u32[]{:S(2)}, u32[]{:S(2)}) collective-permute-start(f32[512,256]{1,0:T(8,128)S(1)} %get-tuple-element.80), channel_id=1, source_target_pairs={{0,4},{4,8},{8,12},{12,14},{14,10},{10,6},{6,2},{2,0},{1,5},{5,9},... | collective-permute-start | bytes 1572872 | tf_op jit(solution)/shard_map/ppermute | solution.py:328
  182.5 4.5 %scatter_product.10 = (f32[512,256]{1,0:T(8,128)S(1)}, f32[512,256]{1,0:T(8,128)S(1)}) custom-call(bf16[2048,256]{1,0:T(8,128)(2,1)S(1)} %get-tuple-element.82.refs_0_, bf16[8,1024,1024]{2,1,0:T(8,128)(2,1)} %get-tuple-element.59.refs_2_.refs_4_.refs_6_.refs_1_, bf16[8,1024,1024]{2,1,0:T(8,128)(2,1)} %get-tuple-element.60.refs_3_.refs_5_.refs_7_.refs_2_), custom_call_target="tpu_custom_call" | custom-call | flops 10000000000 | bytes 1 | tf_op jit(solution)/shard_map/scatter_product/pallas_call | solution.py:305
  187.1 9.0 %collective-permute-done.30 = f32[512,256]{1,0:T(8,128)S(1)} collective-permute-done((f32[512,256]{1,0:T(8,128)S(1)}, f32[512,256]{1,0:T(8,128)S(1)}, u32[]{:S(2)}, u32[]{:S(2)}) %collective-permute-start.30) | collective-permute-done | bytes 524320 | tf_op jit(solution)/shard_map/ppermute | solution.py:328
  197.0 1.0 pad_maximum_fusion.1
  198.9 1.6 maximum_maximum_fusion
  (76 shorter events, 7.9 us)
Async XLA Ops:
  0.6 6.6 %copy-start.1 = (f32[512,512]{1,0:T(8,128)S(1)}, f32[512,512]{1,0:T(8,128)}, u32[]{:S(2)}) copy-start(f32[512,512]{1,0:T(8,128)} %param.7) | copy-start | bytes 3145732
  0.6 22.3 %collective-permute-start.4 = (f32[8,16,128,128]{3,2,1,0:T(8,128)}, f32[8,16,128,128]{3,2,1,0:T(8,128)}, u32[]{:S(2)}, u32[]{:S(2)}) collective-permute-start(f32[8,16,128,128]{3,2,1,0:T(8,128)} %bitcast.11), channel_id=1, source_target_pairs={{0,1},{1,0},{2,3},{3,2},{4,5},{5,4},{6,7},{7,6},{8,9},{9,8},{10,11... | collective-permute-start | bytes 25165832 | tf_op jit(solution)/shard_map/ppermute | solution.py:334
  1.2 7.1 %copy-start.3 = (s32[8,1]{0,1:T(1,128)S(1)}, s32[8,1]{0,1:T(1,128)}, u32[]{:S(2)}) copy-start(s32[8,1]{0,1:T(1,128)} %param.11) | copy-start | bytes 100
  1.2 7.2 %copy-start.2 = (s32[8,1,16]{2,1,0:T(1,128)S(1)}, s32[8,1,16]{2,1,0:T(1,128)}, u32[]{:S(2)}) copy-start(s32[8,1,16]{2,1,0:T(1,128)} %param.10) | copy-start | bytes 1540
  2.5 15.4 %collective-permute-start = (f32[512,256]{1,0:T(8,128)S(1)}, f32[512,256]{1,0:T(8,128)S(1)}, u32[]{:S(2)}, u32[]{:S(2)}) collective-permute-start(f32[512,256]{1,0:T(8,128)S(1)} %get-tuple-element.94.refs_0_), channel_id=1, source_target_pairs={{0,4},{4,8},{8,12},{12,14},{14,10},{10,6},{6,2},{2,0},{1,5},{5,9},... | collective-permute-start | bytes 1572872 | tf_op jit(solution)/shard_map/ppermute | solution.py:328
  5.2 14.8 %collective-permute-start.2 = (f32[512,256]{1,0:T(8,128)S(1)}, f32[512,256]{1,0:T(8,128)S(1)}, u32[]{:S(2)}, u32[]{:S(2)}) collective-permute-start(f32[512,256]{1,0:T(8,128)S(1)} %get-tuple-element.93.refs_1_), channel_id=1, source_target_pairs={{4,0},{8,4},{12,8},{14,12},{10,14},{6,10},{2,6},{0,2},{5,1},{9,5},... | collective-permute-start | bytes 1572872 | tf_op jit(solution)/shard_map/ppermute | solution.py:331
  5.2 26.7 %collective-permute-start.6 = (f32[512,256]{1,0:T(8,128)S(1)}, f32[512,256]{1,0:T(8,128)}, u32[]{:S(2)}, u32[]{:S(2)}) collective-permute-start(f32[512,256]{1,0:T(8,128)S(1)} %get-tuple-element.93.refs_1_), channel_id=1, source_target_pairs={{0,4},{4,8},{8,12},{12,14},{14,10},{10,6},{6,2},{2,0},{1,5},{5,9},... | collective-permute-start | bytes 1572872 | tf_op jit(solution)/shard_map/ppermute | solution.py:328
  7.2 24.7 %collective-permute-start.7 = (f32[512,256]{1,0:T(8,128)S(1)}, f32[512,256]{1,0:T(8,128)}, u32[]{:S(2)}, u32[]{:S(2)}) collective-permute-start(f32[512,256]{1,0:T(8,128)S(1)} %get-tuple-element.94.refs_0_), channel_id=1, source_target_pairs={{4,0},{8,4},{12,8},{14,12},{10,14},{6,10},{2,6},{0,2},{5,1},{9,5},... | collective-permute-start | bytes 1572872 | tf_op jit(solution)/shard_map/ppermute | solution.py:331
  19.9 1.2 collective-permute-start.3
  19.9 22.7 %collective-permute-start.9 = (f32[512,256]{1,0:T(8,128)S(1)}, f32[512,256]{1,0:T(8,128)S(1)}, u32[]{:S(2)}, u32[]{:S(2)}) collective-permute-start(f32[512,256]{1,0:T(8,128)S(1)} %collective-permute-done.2.refs_3_), channel_id=1, source_target_pairs={{4,0},{8,4},{12,8},{14,12},{10,14},{6,10},{2,6},{0,2},{5,1},{9,5},... | collective-permute-start | bytes 1572872 | tf_op jit(solution)/shard_map/ppermute | solution.py:331
  21.1 21.5 %collective-permute-start.1 = (f32[512,256]{1,0:T(8,128)S(1)}, f32[512,256]{1,0:T(8,128)S(1)}, u32[]{:S(2)}, u32[]{:S(2)}) collective-permute-start(f32[512,256]{1,0:T(8,128)S(1)} %collective-permute-done.refs_0_), channel_id=1, source_target_pairs={{0,4},{4,8},{8,12},{12,14},{14,10},{10,6},{6,2},{2,0},{1,5},{5,9},... | collective-permute-start | bytes 1572872 | tf_op jit(solution)/shard_map/ppermute | solution.py:328
  31.9 22.6 %collective-permute-start.16 = (f32[512,256]{1,0:T(8,128)}, f32[512,256]{1,0:T(8,128)S(1)}, u32[]{:S(2)}, u32[]{:S(2)}) collective-permute-start(f32[512,256]{1,0:T(8,128)} %collective-permute-done.7.refs_2_), channel_id=1, source_target_pairs={{4,0},{8,4},{12,8},{14,12},{10,14},{6,10},{2,6},{0,2},{5,1},{9,5},... | collective-permute-start | bytes 1572872 | tf_op jit(solution)/shard_map/ppermute | solution.py:331
  31.9 22.6 %collective-permute-start.14 = (f32[512,256]{1,0:T(8,128)}, f32[512,256]{1,0:T(8,128)S(1)}, u32[]{:S(2)}, u32[]{:S(2)}) collective-permute-start(f32[512,256]{1,0:T(8,128)} %collective-permute-done.6.refs_1_), channel_id=1, source_target_pairs={{0,4},{4,8},{8,12},{12,14},{14,10},{10,6},{6,2},{2,0},{1,5},{5,9},... | collective-permute-start | bytes 1572872 | tf_op jit(solution)/shard_map/ppermute | solution.py:328
  42.6 22.2 %collective-permute-start.10 = (f32[512,256]{1,0:T(8,128)S(1)}, f32[512,256]{1,0:T(8,128)S(1)}, u32[]{:S(2)}, u32[]{:S(2)}) collective-permute-start(f32[512,256]{1,0:T(8,128)S(1)} %collective-permute-done.9.refs_3_), channel_id=1, source_target_pairs={{4,0},{8,4},{12,8},{14,12},{10,14},{6,10},{2,6},{0,2},{5,1},{9,5},... | collective-permute-start | bytes 1572872 | tf_op jit(solution)/shard_map/ppermute | solution.py:331
  42.7 22.2 %collective-permute-start.5 = (f32[512,256]{1,0:T(8,128)S(1)}, f32[512,256]{1,0:T(8,128)S(1)}, u32[]{:S(2)}, u32[]{:S(2)}) collective-permute-start(f32[512,256]{1,0:T(8,128)S(1)} %collective-permute-done.1.refs_0_), channel_id=1, source_target_pairs={{0,4},{4,8},{8,12},{12,14},{14,10},{10,6},{6,2},{2,0},{1,5},{5,9},... | collective-permute-start | bytes 1572872 | tf_op jit(solution)/shard_map/ppermute | solution.py:328
  54.5 21.6 %collective-permute-start.17 = (f32[512,256]{1,0:T(8,128)S(1)}, f32[512,256]{1,0:T(8,128)S(1)}, u32[]{:S(2)}, u32[]{:S(2)}) collective-permute-start(f32[512,256]{1,0:T(8,128)S(1)} %collective-permute-done.16.refs_2_), channel_id=1, source_target_pairs={{4,0},{8,4},{12,8},{14,12},{10,14},{6,10},{2,6},{0,2},{5,1},{9,5},... | collective-permute-start | bytes 1572872 | tf_op jit(solution)/shard_map/ppermute | solution.py:331
  54.5 21.6 %collective-permute-start.15 = (f32[512,256]{1,0:T(8,128)S(1)}, f32[512,256]{1,0:T(8,128)S(1)}, u32[]{:S(2)}, u32[]{:S(2)}) collective-permute-start(f32[512,256]{1,0:T(8,128)S(1)} %collective-permute-done.14.refs_1_), channel_id=1, source_target_pairs={{0,4},{4,8},{8,12},{12,14},{14,10},{10,6},{6,2},{2,0},{1,5},{5,9},... | collective-permute-start | bytes 1572872 | tf_op jit(solution)/shard_map/ppermute | solution.py:328
  64.9 21.7 %collective-permute-start.11 = (f32[512,256]{1,0:T(8,128)S(1)}, f32[512,256]{1,0:T(8,128)S(1)}, u32[]{:S(2)}, u32[]{:S(2)}) collective-permute-start(f32[512,256]{1,0:T(8,128)S(1)} %collective-permute-done.10.refs_3_), channel_id=1, source_target_pairs={{4,0},{8,4},{12,8},{14,12},{10,14},{6,10},{2,6},{0,2},{5,1},{9,5},... | collective-permute-start | bytes 1572872 | tf_op jit(solution)/shard_map/ppermute | solution.py:331
  64.9 21.7 %collective-permute-start.8 = (f32[512,256]{1,0:T(8,128)S(1)}, f32[512,256]{1,0:T(8,128)S(1)}, u32[]{:S(2)}, u32[]{:S(2)}) collective-permute-start(f32[512,256]{1,0:T(8,128)S(1)} %collective-permute-done.5.refs_0_), channel_id=1, source_target_pairs={{0,4},{4,8},{8,12},{12,14},{14,10},{10,6},{6,2},{2,0},{1,5},{5,9},... | collective-permute-start | bytes 1572872 | tf_op jit(solution)/shard_map/ppermute | solution.py:328
  73.1 16.1 %copy-start = (f32[1024,512]{1,0:T(8,128)S(1)}, f32[1024,512]{1,0:T(8,128)}, u32[]{:S(2)}) copy-start(f32[1024,512]{1,0:T(8,128)} %refs_9_.1) | copy-start | bytes 6291460
  82.4 6.9 %collective-permute-start.18 = (f32[1024,256]{1,0:T(8,128)S(1)}, f32[1024,256]{1,0:T(8,128)S(1)}, u32[]{:S(2)}, u32[]{:S(2)}) collective-permute-start(f32[1024,256]{1,0:T(8,128)S(1)} %gather_product.7.refs_7_), channel_id=1, source_target_pairs={{0,1},{1,0},{2,3},{3,2},{4,5},{5,4},{6,7},{7,6},{8,9},{9,8},{10,11... | collective-permute-start | bytes 3145736 | tf_op jit(solution)/shard_map/ppermute | solution.py:334
  86.6 1.9 collective-permute-start.13
  86.6 2.7 %collective-permute-start.12 = (f32[512,256]{1,0:T(8,128)S(1)}, f32[512,256]{1,0:T(8,128)S(1)}, u32[]{:S(2)}, u32[]{:S(2)}) collective-permute-start(f32[512,256]{1,0:T(8,128)S(1)} %collective-permute-done.8.refs_1_), channel_id=1, source_target_pairs={{0,1},{1,0},{2,3},{3,2},{4,5},{5,4},{6,7},{7,6},{8,9},{9,8},{10,11... | collective-permute-start | bytes 1572872 | tf_op jit(solution)/shard_map/ppermute | solution.py:334
  99.6 20.6 %collective-permute-start.19 = (f32[512,256]{1,0:T(8,128)S(1)}, f32[512,256]{1,0:T(8,128)S(1)}, u32[]{:S(2)}, u32[]{:S(2)}) collective-permute-start(f32[512,256]{1,0:T(8,128)S(1)} %get-tuple-element.74), channel_id=1, source_target_pairs={{0,4},{4,8},{8,12},{12,14},{14,10},{10,6},{6,2},{2,0},{1,5},{5,9},... | collective-permute-start | bytes 1572872 | tf_op jit(solution)/shard_map/ppermute | solution.py:328
  101.2 18.9 %collective-permute-start.20 = (f32[512,256]{1,0:T(8,128)S(1)}, f32[512,256]{1,0:T(8,128)S(1)}, u32[]{:S(2)}, u32[]{:S(2)}) collective-permute-start(f32[512,256]{1,0:T(8,128)S(1)} %get-tuple-element.75), channel_id=1, source_target_pairs={{4,0},{8,4},{12,8},{14,12},{10,14},{6,10},{2,6},{0,2},{5,1},{9,5},... | collective-permute-start | bytes 1572872 | tf_op jit(solution)/shard_map/ppermute | solution.py:331
  101.6 18.4 %collective-permute-start.35 = (f32[128,512]{1,0:T(8,128)S(1)}, f32[128,512]{1,0:T(8,128)S(1)}, u32[]{:S(2)}, u32[]{:S(2)}) collective-permute-start(f32[128,512]{1,0:T(8,128)S(1)} %get-tuple-element.92), channel_id=1, source_target_pairs={{0,2},{2,0},{4,6},{6,4},{8,10},{10,8},{12,14},{14,12},{1,3},{3,1},... | collective-permute-start | bytes 786440 | tf_op jit(solution)/shard_map/ppermute | solution.py:417
  106.4 29.1 %collective-permute-start.25 = (f32[512,256]{1,0:T(8,128)S(1)}, f32[512,256]{1,0:T(8,128)S(1)}, u32[]{:S(2)}, u32[]{:S(2)}) collective-permute-start(f32[512,256]{1,0:T(8,128)S(1)} %get-tuple-element.84), channel_id=1, source_target_pairs={{0,4},{4,8},{8,12},{12,14},{14,10},{10,6},{6,2},{2,0},{1,5},{5,9},... | collective-permute-start | bytes 1572872 | tf_op jit(solution)/shard_map/ppermute | solution.py:328
  108.2 27.3 %collective-permute-start.26 = (f32[512,256]{1,0:T(8,128)S(1)}, f32[512,256]{1,0:T(8,128)S(1)}, u32[]{:S(2)}, u32[]{:S(2)}) collective-permute-start(f32[512,256]{1,0:T(8,128)S(1)} %get-tuple-element.85), channel_id=1, source_target_pairs={{4,0},{8,4},{12,8},{14,12},{10,14},{6,10},{2,6},{0,2},{5,1},{9,5},... | collective-permute-start | bytes 1572872 | tf_op jit(solution)/shard_map/ppermute | solution.py:331
  120.0 12.8 %collective-permute-start.36 = (f32[128,512]{1,0:T(8,128)S(1)}, f32[128,512]{1,0:T(8,128)S(1)}, u32[]{:S(2)}, u32[]{:S(2)}) collective-permute-start(f32[128,512]{1,0:T(8,128)S(1)} %add.64), channel_id=1, source_target_pairs={{0,4},{2,6},{4,0},{6,2},{8,12},{10,14},{12,8},{14,10},{1,5},{3,7},... | collective-permute-start | bytes 786440 | tf_op jit(solution)/shard_map/ppermute | solution.py:417
  124.7 30.8 %collective-permute-start.21 = (f32[512,256]{1,0:T(8,128)S(1)}, f32[512,256]{1,0:T(8,128)S(1)}, u32[]{:S(2)}, u32[]{:S(2)}) collective-permute-start(f32[512,256]{1,0:T(8,128)S(1)} %get-tuple-element.76), channel_id=1, source_target_pairs={{0,4},{4,8},{8,12},{12,14},{14,10},{10,6},{6,2},{2,0},{1,5},{5,9},... | collective-permute-start | bytes 1572872 | tf_op jit(solution)/shard_map/ppermute | solution.py:328
  126.7 28.8 %collective-permute-start.22 = (f32[512,256]{1,0:T(8,128)S(1)}, f32[512,256]{1,0:T(8,128)S(1)}, u32[]{:S(2)}, u32[]{:S(2)}) collective-permute-start(f32[512,256]{1,0:T(8,128)S(1)} %get-tuple-element.77), channel_id=1, source_target_pairs={{4,0},{8,4},{12,8},{14,12},{10,14},{6,10},{2,6},{0,2},{5,1},{9,5},... | collective-permute-start | bytes 1572872 | tf_op jit(solution)/shard_map/ppermute | solution.py:331
  132.9 22.5 %collective-permute-start.37 = (f32[128,512]{1,0:T(8,128)S(1)}, f32[128,512]{1,0:T(8,128)S(1)}, u32[]{:S(2)}, u32[]{:S(2)}) collective-permute-start(f32[128,512]{1,0:T(8,128)S(1)} %add.65), channel_id=1, source_target_pairs={{0,8},{2,10},{4,12},{6,14},{8,0},{10,2},{12,4},{14,6},{1,9},{3,11}... | collective-permute-start | bytes 786440 | tf_op jit(solution)/shard_map/ppermute | solution.py:417
  140.0 25.3 %collective-permute-start.27 = (f32[512,256]{1,0:T(8,128)S(1)}, f32[512,256]{1,0:T(8,128)S(1)}, u32[]{:S(2)}, u32[]{:S(2)}) collective-permute-start(f32[512,256]{1,0:T(8,128)S(1)} %get-tuple-element.86), channel_id=1, source_target_pairs={{0,4},{4,8},{8,12},{12,14},{14,10},{10,6},{6,2},{2,0},{1,5},{5,9},... | collective-permute-start | bytes 1572872 | tf_op jit(solution)/shard_map/ppermute | solution.py:328
  140.1 25.3 %collective-permute-start.28 = (f32[512,256]{1,0:T(8,128)S(1)}, f32[512,256]{1,0:T(8,128)S(1)}, u32[]{:S(2)}, u32[]{:S(2)}) collective-permute-start(f32[512,256]{1,0:T(8,128)S(1)} %get-tuple-element.87), channel_id=1, source_target_pairs={{4,0},{8,4},{12,8},{14,12},{10,14},{6,10},{2,6},{0,2},{5,1},{9,5},... | collective-permute-start | bytes 1572872 | tf_op jit(solution)/shard_map/ppermute | solution.py:331
  155.4 8.8 %collective-permute-start.38 = (f32[128,512]{1,0:T(8,128)S(1)}, f32[128,512]{1,0:T(8,128)}, u32[]{:S(2)}, u32[]{:S(2)}) collective-permute-start(f32[128,512]{1,0:T(8,128)S(1)} %add.66), channel_id=1, source_target_pairs={{0,2},{2,0},{4,6},{6,4},{8,10},{10,8},{12,14},{14,12},{1,3},{3,1},... | collective-permute-start | bytes 786440 | tf_op jit(solution)/shard_map/ppermute | solution.py:417
  161.0 11.0 %collective-permute-start.23 = (f32[512,256]{1,0:T(8,128)}, f32[512,256]{1,0:T(8,128)}, u32[]{:S(2)}, u32[]{:S(2)}) collective-permute-start(f32[512,256]{1,0:T(8,128)} %get-tuple-element.78), channel_id=1, source_target_pairs={{0,4},{4,8},{8,12},{12,14},{14,10},{10,6},{6,2},{2,0},{1,5},{5,9},... | collective-permute-start | bytes 1572872 | tf_op jit(solution)/shard_map/ppermute | solution.py:328
  161.0 11.0 %collective-permute-start.24 = (f32[512,256]{1,0:T(8,128)}, f32[512,256]{1,0:T(8,128)}, u32[]{:S(2)}, u32[]{:S(2)}) collective-permute-start(f32[512,256]{1,0:T(8,128)} %get-tuple-element.79), channel_id=1, source_target_pairs={{4,0},{8,4},{12,8},{14,12},{10,14},{6,10},{2,6},{0,2},{5,1},{9,5},... | collective-permute-start | bytes 1572872 | tf_op jit(solution)/shard_map/ppermute | solution.py:331
  165.3 31.6 %collective-permute-start.39 = (f32[256,512]{1,0:T(8,128)S(1)}, f32[256,512]{1,0:T(8,128)S(1)}, u32[]{:S(2)}, u32[]{:S(2)}) collective-permute-start(f32[256,512]{1,0:T(8,128)S(1)} %pad_maximum_fusion.2), channel_id=1, source_target_pairs={{0,1},{1,0},{2,3},{3,2},{4,5},{5,4},{6,7},{7,6},{8,9},{9,8},{10,11... | collective-permute-start | bytes 1572872 | tf_op jit(solution)/shard_map/ppermute | solution.py:334
  169.9 17.1 %collective-permute-start.29 = (f32[512,256]{1,0:T(8,128)S(1)}, f32[512,256]{1,0:T(8,128)S(1)}, u32[]{:S(2)}, u32[]{:S(2)}) collective-permute-start(f32[512,256]{1,0:T(8,128)S(1)} %get-tuple-element.88), channel_id=1, source_target_pairs={{4,0},{8,4},{12,8},{14,12},{10,14},{6,10},{2,6},{0,2},{5,1},{9,5},... | collective-permute-start | bytes 1572872 | tf_op jit(solution)/shard_map/ppermute | solution.py:331
  170.8 25.4 %collective-permute-start.32 = (f32[512,256]{1,0:T(8,128)S(1)}, f32[512,256]{1,0:T(8,128)S(1)}, u32[]{:S(2)}, u32[]{:S(2)}) collective-permute-start(f32[512,256]{1,0:T(8,128)S(1)} %get-tuple-element.90), channel_id=1, source_target_pairs={{0,4},{4,8},{8,12},{12,14},{14,10},{10,6},{6,2},{2,0},{1,5},{5,9},... | collective-permute-start | bytes 1572872 | tf_op jit(solution)/shard_map/ppermute | solution.py:328
  176.9 19.1 %collective-permute-start.30 = (f32[512,256]{1,0:T(8,128)S(1)}, f32[512,256]{1,0:T(8,128)S(1)}, u32[]{:S(2)}, u32[]{:S(2)}) collective-permute-start(f32[512,256]{1,0:T(8,128)S(1)} %get-tuple-element.80), channel_id=1, source_target_pairs={{0,4},{4,8},{8,12},{12,14},{14,10},{10,6},{6,2},{2,0},{1,5},{5,9},... | collective-permute-start | bytes 1572872 | tf_op jit(solution)/shard_map/ppermute | solution.py:328
  182.5 13.7 %collective-permute-start.33 = (f32[512,256]{1,0:T(8,128)S(1)}, f32[512,256]{1,0:T(8,128)S(1)}, u32[]{:S(2)}, u32[]{:S(2)}) collective-permute-start(f32[512,256]{1,0:T(8,128)S(1)} %get-tuple-element.81), channel_id=1, source_target_pairs={{4,0},{8,4},{12,8},{14,12},{10,14},{6,10},{2,6},{0,2},{5,1},{9,5},... | collective-permute-start | bytes 1572872 | tf_op jit(solution)/shard_map/ppermute | solution.py:331
  196.1 2.0 collective-permute-start.31
  196.4 2.5 %collective-permute-start.34 = (f32[512,256]{1,0:T(8,128)S(1)}, f32[512,256]{1,0:T(8,128)S(1)}, u32[]{:S(2)}, u32[]{:S(2)}) collective-permute-start(f32[512,256]{1,0:T(8,128)S(1)} %add_add_fusion), channel_id=1, source_target_pairs={{0,1},{1,0},{2,3},{3,2},{4,5},{5,4},{6,7},{7,6},{8,9},{9,8},{10,11... | collective-permute-start | bytes 1572872 | tf_op jit(solution)/shard_map/ppermute | solution.py:334

commit v4 on v3

--- a/solution.py
+++ b/solution.py
@@ -10,7 +10,7 @@
 BF16 = jnp.bfloat16
 F32 = jnp.float32
 MIB = 48
-SP_FLOPS = [10000000000,1,10000000000,1,10000000000,1,10000000000]
+SP_FLOPS = [10000000000,10000000000,10000000000,1,10000000000,1,10000000000]
 LAYER_MIB = 40
 SMALL = pl.CostEstimate(flops=10_000_000_000, transcendentals=0, bytes_accessed=8_000_000)
 
@@ -266,7 +266,7 @@
         in_specs=[whole] * 5,
         out_specs=(whole,) * 3,
         compiler_params=params(LAYER_MIB),
-        cost_estimate=pl.CostEstimate(flops=1, transcendentals=0, bytes_accessed=1),
+        cost_estimate=pl.CostEstimate(flops=10000000000, transcendentals=0, bytes_accessed=1),
         name="layer_grad",
     )(pre_grad, *far, w_hi, w_lo)
 

time: 201 us -> 198 us (0.985)
    ppermute x4, waiting for transfers between devices: 31.7 us -> 17.1 us  [exchange(): return lax.ppermute(block, 'row', [(i, i ^ distance) for i in range(size)])]
    ppermute x14, waiting for transfers between devices: 17.1 us -> 24.8 us  [forth(): return lax.ppermute(block, 'row', ahead)]
    ppermute x14, starting transfers between devices: 26.7 us -> 20.4 us  [forth(): return lax.ppermute(block, 'row', ahead)]
    ppermute x14, waiting for transfers between devices: 10.4 us -> 15.8 us  [rear(): return lax.ppermute(block, 'row', back)]
    ppermute x14, starting transfers between devices: 6.1 us -> 9.14 us  [rear(): return lax.ppermute(block, 'row', back)]
  transfers between devices with their start and end apart: 40 -> 40, of which waited for: 15 -> 19; matrix products, arithmetic and copies ran while one was open for 3% -> 3% of each run, Pallas kernels for 40% -> 42%
where the time goes in v4:
time: 198 us; the launch traced here: 197 us
  Pallas kernels  90.5 us (46%)
  waiting for transfers between devices  61.8 us (31%)
  starting transfers between devices  35.7 us (18%)
  other arithmetic  6.95 us (4%)
    pallas_call x7, Pallas kernels, scatter_product(): pl.pallas_call(scatter_kernel, out_shape=(jax.ShapeDtypeStruct((half, wid...  32.9 us
    ppermute x14, waiting for transfers between devices, forth(): return lax.ppermute(block, 'row', ahead)  24.8 us
    pallas_call x4, Pallas kernels, gather_product(): pl.pallas_call(functools.partial(gather_kernel, blocks), out_shape=jax.Sh...  24.4 us
    pallas_call x3, Pallas kernels, densify(): pl.pallas_call(functools.partial(densify_kernel, first, size // 2), out_s...  23 us
    ppermute x14, starting transfers between devices, forth(): return lax.ppermute(block, 'row', ahead)  20.4 us
    ppermute x4, waiting for transfers between devices, exchange(): return lax.ppermute(block, 'row', [(i, i ^ distance) for i in range(size)])  17.1 us
    ppermute x14, waiting for transfers between devices, rear(): return lax.ppermute(block, 'row', back)  15.8 us
    ppermute x14, starting transfers between devices, rear(): return lax.ppermute(block, 'row', back)  9.14 us
  transfers between devices with their start and end apart: 40, of which 19 were waited for; matrix products, arithmetic and copies ran while one was open for 3% of the time, Pallas kernels for 42%

profile of v4, /device:TPU:0, one launch (start us, length us, event | category | flops | bytes accessed | tf_op | source)
XLA Modules:
  0.0 197.2 jit_solution(16459773304997819968)
XLA Ops:
  1.2 1.3 constant_dynamic-slice_fusion
  2.5 2.7 %collective-permute-start = (f32[512,256]{1,0:T(8,128)S(1)}, f32[512,256]{1,0:T(8,128)S(1)}, u32[]{:S(2)}, u32[]{:S(2)}) collective-permute-start(f32[512,256]{1,0:T(8,128)S(1)} %get-tuple-element.94.refs_0_), channel_id=1, source_target_pairs={{0,4},{4,8},{8,12},{12,14},{14,10},{10,6},{6,2},{2,0},{1,5},{5,9},... | collective-permute-start | bytes 1572872 | tf_op jit(solution)/shard_map/ppermute | solution.py:328
  5.2 2.0 %collective-permute-start.6 = (f32[512,256]{1,0:T(8,128)S(1)}, f32[512,256]{1,0:T(8,128)}, u32[]{:S(2)}, u32[]{:S(2)}) collective-permute-start(f32[512,256]{1,0:T(8,128)S(1)} %get-tuple-element.93.refs_1_), channel_id=1, source_target_pairs={{0,4},{4,8},{8,12},{12,14},{14,10},{10,6},{6,2},{2,0},{1,5},{5,9},... | collective-permute-start | bytes 1572872 | tf_op jit(solution)/shard_map/ppermute | solution.py:328
  8.4 1.4 fusion
  9.8 8.1 %collective-permute-done.refs_0_ = f32[512,256]{1,0:T(8,128)S(1)} collective-permute-done((f32[512,256]{1,0:T(8,128)S(1)}, f32[512,256]{1,0:T(8,128)S(1)}, u32[]{:S(2)}, u32[]{:S(2)}) %collective-permute-start) | collective-permute-done | bytes 524320 | tf_op jit(solution)/shard_map/ppermute | solution.py:328
  17.9 2.1 %collective-permute-done.2.refs_3_ = f32[512,256]{1,0:T(8,128)S(1)} collective-permute-done((f32[512,256]{1,0:T(8,128)S(1)}, f32[512,256]{1,0:T(8,128)S(1)}, u32[]{:S(2)}, u32[]{:S(2)}) %collective-permute-start.2) | collective-permute-done | bytes 524320 | tf_op jit(solution)/shard_map/ppermute | solution.py:331
  19.9 1.2 collective-permute-done.3
  21.1 1.6 collective-permute-start.1
  23.0 8.5 %densify.3 = (bf16[8,1024,1024]{2,1,0:T(8,128)(2,1)}, bf16[8,1024,1024]{2,1,0:T(8,128)(2,1)}, bf16[1024,1024]{1,0:T(8,128)(2,1)S(1)}, bf16[1024,1024]{1,0:T(8,128)(2,1)S(1)}) custom-call(s32[2,2,8,16]{3,2,1,0:T(8,128)S(1)} %pad_add_fusion.place_ref, s32[2,8]{1,0:T(2,128)S(1)} %fusion.7.count_ref, f32[8,16,128,128]{3,2,1,0:T(8,128)} %bitcast.12, ...), custom_call_target="tpu_custom_call" | custom-call | bytes 18874368 | tf_op jit(solution)/shard_map/densify/pallas_call | solution.py:79
  33.5 8.6 %densify.4 = (bf16[8,1024,1024]{2,1,0:T(8,128)(2,1)}, bf16[8,1024,1024]{2,1,0:T(8,128)(2,1)}, bf16[1024,1024]{1,0:T(8,128)(2,1)S(1)}, bf16[1024,1024]{1,0:T(8,128)(2,1)S(1)}) custom-call(s32[2,2,8,16]{3,2,1,0:T(8,128)S(1)} %pad_add_fusion.place_ref, ...), custom_call_target="tpu_custom_call", output_to_operand_aliasing={{0}: (4, {}), {1}: (5, {}), {2}: (6, {}), {3}: (7, {})} | custom-call | bytes 18874368 | tf_op jit(solution)/shard_map/densify/pallas_call | solution.py:79
  44.4 6.0 %densify.5 = (bf16[8,1024,1024]{2,1,0:T(8,128)(2,1)}, bf16[8,1024,1024]{2,1,0:T(8,128)(2,1)}, bf16[1024,1024]{1,0:T(8,128)(2,1)S(1)}, bf16[1024,1024]{1,0:T(8,128)(2,1)S(1)}) custom-call(s32[2,2,8,16]{3,2,1,0:T(8,128)S(1)} %pad_add_fusion.place_ref, ...), custom_call_target="tpu_custom_call", output_to_operand_aliasing={{0}: (4, {}), {1}: (5, {}), {2}: (6, {}), {3}: (7, {})} | custom-call | bytes 12582912 | tf_op jit(solution)/shard_map/densify/pallas_call | solution.py:79
  50.4 3.7 %gather_product.4.refs_8_ = f32[1024,256]{1,0:T(8,128)S(1)} custom-call(f32[512,256]{1,0:T(8,128)S(1)} %get-tuple-element.94.refs_0_, f32[512,256]{1,0:T(8,128)S(1)} %get-tuple-element.93.refs_1_, bf16[8,1024,1024]{2,1,0:T(8,128)(2,1)} %get-tuple-element.59.refs_2_.refs_4_.refs_6_.refs_1_, ...), custom_call_target="tpu_custom_call" | custom-call | flops 1610612736 | bytes 7340032 | tf_op jit(solution)/shard_map/gather_product/pallas_call | solution.py:142
  54.2 1.7 collective-permute-start.17
  56.3 7.1 %gather_product.5.refs_8_ = f32[1024,256]{1,0:T(8,128)S(1)} custom-call(f32[512,256]{1,0:T(8,128)S(1)} %collective-permute-done.refs_0_, f32[512,256]{1,0:T(8,128)} %collective-permute-done.6.refs_1_, f32[512,256]{1,0:T(8,128)} %collective-permute-done.7.refs_2_, f32[512,256]{1,0:T(8,128)S(1)} %collective-permute-done.2.refs_3_, ...), custom_call_target="tpu_custom_call" | custom-call | flops 3221225472 | bytes 12582912 | tf_op jit(solution)/shard_map/gather_product/pallas_call | solution.py:142
  63.4 1.6 collective-permute-done.10.refs_3_
  65.0 2.0 %collective-permute-start.8 = (f32[512,256]{1,0:T(8,128)}, f32[512,256]{1,0:T(8,128)S(1)}, u32[]{:S(2)}, u32[]{:S(2)}) collective-permute-start(f32[512,256]{1,0:T(8,128)} %collective-permute-done.5.refs_0_), channel_id=1, source_target_pairs={{0,4},{4,8},{8,12},{12,14},{14,10},{10,6},{6,2},{2,0},{1,5},{5,9},... | collective-permute-start | bytes 1572872 | tf_op jit(solution)/shard_map/ppermute | solution.py:328
  67.0 6.2 %gather_product.6.refs_8_ = f32[1024,256]{1,0:T(8,128)S(1)} custom-call(f32[512,256]{1,0:T(8,128)S(1)} %collective-permute-done.1.refs_0_, f32[512,256]{1,0:T(8,128)S(1)} %collective-permute-done.14.refs_1_, f32[512,256]{1,0:T(8,128)S(1)} %collective-permute-done.16.refs_2_, f32[512,256]{1,0:T(8,128)S(1)} %collective-permute-done.9.refs_3_, ...), custom_call_target="tpu_custom_call" | custom-call | flops 3221225472 | bytes 12582912 | tf_op jit(solution)/shard_map/gather_product/pallas_call | solution.py:142
  73.2 2.9 %collective-permute-done.17.refs_2_ = f32[512,256]{1,0:T(8,128)S(1)} collective-permute-done((f32[512,256]{1,0:T(8,128)S(1)}, f32[512,256]{1,0:T(8,128)S(1)}, u32[]{:S(2)}, u32[]{:S(2)}) %collective-permute-start.17) | collective-permute-done | bytes 524320 | tf_op jit(solution)/shard_map/ppermute | solution.py:331
  76.1 7.4 %gather_product.7.refs_7_ = f32[1024,256]{1,0:T(8,128)S(1)} custom-call(f32[512,256]{1,0:T(8,128)} %collective-permute-done.5.refs_0_, f32[512,256]{1,0:T(8,128)S(1)} %collective-permute-done.15.refs_1_, f32[512,256]{1,0:T(8,128)S(1)} %collective-permute-done.17.refs_2_, f32[512,256]{1,0:T(8,128)} %collective-permute-done.10.refs_3_, ...), custom_call_target="tpu_custom_call" | custom-call | flops 3221225472 | bytes 12582912 | tf_op jit(solution)/shard_map/gather_product/pallas_call | solution.py:142
  83.6 3.0 %collective-permute-done.11.refs_2_ = f32[512,256]{1,0:T(8,128)S(1)} collective-permute-done((f32[512,256]{1,0:T(8,128)}, f32[512,256]{1,0:T(8,128)S(1)}, u32[]{:S(2)}, u32[]{:S(2)}) %collective-permute-start.11) | collective-permute-done | bytes 524320 | tf_op jit(solution)/shard_map/ppermute | solution.py:331
  87.1 1.4 collective-permute-done.13.refs_4_
  89.2 7.4 %layer.1 = (f32[1024,512]{1,0:T(8,128)}, bf16[2048,512]{1,0:T(8,128)(2,1)S(1)}, f32[128,512]{1,0:T(8,128)S(1)}, f32[128,512]{1,0:T(8,128)S(1)}) custom-call(s32[1]{0:T(128)} %bitcast.refs_0_, f32[512,256]{1,0:T(8,128)S(1)} %collective-permute-done.8.refs_1_, f32[512,256]{1,0:T(8,128)S(1)} %collective-permute-done.11.refs_2_, ...), custom_call_target="tpu_custom_call" | custom-call | flops 1 | bytes 1 | tf_op jit(solution)/shard_map/layer/pallas_call | solution.py:235
  97.0 2.7 %layer_grad.1 = (bf16[2048,256]{1,0:T(8,128)(2,1)S(1)}, f32[512,256]{1,0:T(8,128)S(1)}, f32[512,256]{1,0:T(8,128)S(1)}) custom-call(bf16[2048,512]{1,0:T(8,128)(2,1)S(1)} %get-tuple-element.72.refs_0_, bf16[1024,1024]{1,0:T(8,128)(2,1)S(1)} %get-tuple-element.65.refs_5_.refs_1_, bf16[1024,1024]{1,0:T(8,128)(2,1)S(1)} %get-tuple-element.66.refs_6_.refs_2_, ...), custom_call_target="tpu_custom_call" | custom-call | flops 10000000000 | bytes 1 | tf_op jit(solution)/shard_map/layer_grad/pallas_call | solution.py:259
  99.7 1.7 collective-permute-start.19
  101.8 4.5 %scatter_product.11 = (f32[512,256]{1,0:T(8,128)S(1)}, f32[512,256]{1,0:T(8,128)S(1)}) custom-call(bf16[2048,256]{1,0:T(8,128)(2,1)S(1)} %get-tuple-element.82.refs_0_, bf16[8,1024,1024]{2,1,0:T(8,128)(2,1)} %get-tuple-element.59.refs_2_.refs_4_.refs_6_.refs_1_, bf16[8,1024,1024]{2,1,0:T(8,128)(2,1)} %get-tuple-element.60.refs_3_.refs_5_.refs_7_.refs_2_), custom_call_target="tpu_custom_call" | custom-call | flops 10000000000 | bytes 1 | tf_op jit(solution)/shard_map/scatter_product/pallas_call | solution.py:305
  106.3 1.7 collective-permute-start.25
  108.4 1.7 collective-permute-start.36
  110.1 6.9 %collective-permute-done.19.refs_3_ = f32[512,256]{1,0:T(8,128)S(1)} collective-permute-done((f32[512,256]{1,0:T(8,128)S(1)}, f32[512,256]{1,0:T(8,128)S(1)}, u32[]{:S(2)}, u32[]{:S(2)}) %collective-permute-start.19) | collective-permute-done | bytes 524320 | tf_op jit(solution)/shard_map/ppermute | solution.py:328
  117.1 4.5 %scatter_product.7 = (f32[512,256]{1,0:T(8,128)S(1)}, f32[512,256]{1,0:T(8,128)S(1)}) custom-call(bf16[2048,256]{1,0:T(8,128)(2,1)S(1)} %get-tuple-element.82.refs_0_, bf16[8,1024,1024]{2,1,0:T(8,128)(2,1)} %get-tuple-element.59.refs_2_.refs_4_.refs_6_.refs_1_, bf16[8,1024,1024]{2,1,0:T(8,128)(2,1)} %get-tuple-element.60.refs_3_.refs_5_.refs_7_.refs_2_, ...), custom_call_target="tpu_custom_call" | custom-call | flops 10000000000 | bytes 1 | tf_op jit(solution)/shard_map/scatter_product/pallas_call | solution.py:305
  122.4 1.2 collective-permute-start.22
  123.7 9.4 %collective-permute-done.36 = f32[128,512]{1,0:T(8,128)S(1)} collective-permute-done((f32[128,512]{1,0:T(8,128)S(1)}, f32[128,512]{1,0:T(8,128)S(1)}, u32[]{:S(2)}, u32[]{:S(2)}) %collective-permute-start.36) | collective-permute-done | bytes 262176 | tf_op jit(solution)/shard_map/ppermute | solution.py:417
  133.2 2.7 %collective-permute-start.37 = (f32[128,512]{1,0:T(8,128)S(1)}, f32[128,512]{1,0:T(8,128)S(1)}, u32[]{:S(2)}, u32[]{:S(2)}) collective-permute-start(f32[128,512]{1,0:T(8,128)S(1)} %add.65), channel_id=1, source_target_pairs={{0,8},{2,10},{4,12},{6,14},{8,0},{10,2},{12,4},{14,6},{1,9},{3,11}... | collective-permute-start | bytes 786440 | tf_op jit(solution)/shard_map/ppermute | solution.py:417
  135.8 4.5 %scatter_product.12 = (f32[512,256]{1,0:T(8,128)S(1)}, f32[512,256]{1,0:T(8,128)S(1)}) custom-call(bf16[2048,256]{1,0:T(8,128)(2,1)S(1)} %get-tuple-element.82.refs_0_, bf16[8,1024,1024]{2,1,0:T(8,128)(2,1)} %get-tuple-element.59.refs_2_.refs_4_.refs_6_.refs_1_, bf16[8,1024,1024]{2,1,0:T(8,128)(2,1)} %get-tuple-element.60.refs_3_.refs_5_.refs_7_.refs_2_, ...), custom_call_target="tpu_custom_call" | custom-call | flops 1 | bytes 1 | tf_op jit(solution)/shard_map/scatter_product/pallas_call | solution.py:305
  140.4 2.0 %collective-permute-start.28 = (f32[512,256]{1,0:T(8,128)S(1)}, f32[512,256]{1,0:T(8,128)S(1)}, u32[]{:S(2)}, u32[]{:S(2)}) collective-permute-start(f32[512,256]{1,0:T(8,128)S(1)} %get-tuple-element.87), channel_id=1, source_target_pairs={{4,0},{8,4},{12,8},{14,12},{10,14},{6,10},{2,6},{0,2},{5,1},{9,5},... | collective-permute-start | bytes 1572872 | tf_op jit(solution)/shard_map/ppermute | solution.py:331
  142.5 7.6 %collective-permute-done.37 = f32[128,512]{1,0:T(8,128)S(1)} collective-permute-done((f32[128,512]{1,0:T(8,128)S(1)}, f32[128,512]{1,0:T(8,128)S(1)}, u32[]{:S(2)}, u32[]{:S(2)}) %collective-permute-start.37) | collective-permute-done | bytes 262176 | tf_op jit(solution)/shard_map/ppermute | solution.py:417
  150.2 5.5 %scatter_product.8 = (f32[512,256]{1,0:T(8,128)}, f32[512,256]{1,0:T(8,128)}) custom-call(bf16[2048,256]{1,0:T(8,128)(2,1)S(1)} %get-tuple-element.82.refs_0_, bf16[8,1024,1024]{2,1,0:T(8,128)(2,1)} %get-tuple-element.59.refs_2_.refs_4_.refs_6_.refs_1_, bf16[8,1024,1024]{2,1,0:T(8,128)(2,1)} %get-tuple-element.60.refs_3_.refs_5_.refs_7_.refs_2_, ...), custom_call_target="tpu_custom_call" | custom-call | flops 10000000000 | bytes 1 | tf_op jit(solution)/shard_map/scatter_product/pallas_call | solution.py:305
  155.7 2.6 %collective-permute-start.23 = (f32[512,256]{1,0:T(8,128)}, f32[512,256]{1,0:T(8,128)}, u32[]{:S(2)}, u32[]{:S(2)}) collective-permute-start(f32[512,256]{1,0:T(8,128)} %get-tuple-element.78), channel_id=1, source_target_pairs={{0,4},{4,8},{8,12},{12,14},{14,10},{10,6},{6,2},{2,0},{1,5},{5,9},... | collective-permute-start | bytes 1572872 | tf_op jit(solution)/shard_map/ppermute | solution.py:328
  159.5 1.7 collective-permute-done.28.refs_4_
  161.2 4.5 %scatter_product.13 = (f32[512,256]{1,0:T(8,128)S(1)}, f32[512,256]{1,0:T(8,128)S(1)}) custom-call(bf16[2048,256]{1,0:T(8,128)(2,1)S(1)} %get-tuple-element.82.refs_0_, bf16[8,1024,1024]{2,1,0:T(8,128)(2,1)} %get-tuple-element.59.refs_2_.refs_4_.refs_6_.refs_1_, bf16[8,1024,1024]{2,1,0:T(8,128)(2,1)} %get-tuple-element.60.refs_3_.refs_5_.refs_7_.refs_2_, ...), custom_call_target="tpu_custom_call" | custom-call | flops 1 | bytes 1 | tf_op jit(solution)/shard_map/scatter_product/pallas_call | solution.py:305
  166.0 1.8 collective-permute-start.32
  167.8 3.1 %collective-permute-done.23.refs_3_ = f32[512,256]{1,0:T(8,128)} collective-permute-done((f32[512,256]{1,0:T(8,128)}, f32[512,256]{1,0:T(8,128)}, u32[]{:S(2)}, u32[]{:S(2)}) %collective-permute-start.23) | collective-permute-done | bytes 524320 | tf_op jit(solution)/shard_map/ppermute | solution.py:328
  170.9 2.5 %collective-permute-done.24.refs_4_ = f32[512,256]{1,0:T(8,128)} collective-permute-done((f32[512,256]{1,0:T(8,128)}, f32[512,256]{1,0:T(8,128)}, u32[]{:S(2)}, u32[]{:S(2)}) %collective-permute-start.24) | collective-permute-done | bytes 524320 | tf_op jit(solution)/shard_map/ppermute | solution.py:331
  173.4 4.9 %scatter_product.9 = (f32[512,256]{1,0:T(8,128)S(1)}, f32[512,256]{1,0:T(8,128)S(1)}) custom-call(bf16[2048,256]{1,0:T(8,128)(2,1)S(1)} %get-tuple-element.82.refs_0_, bf16[8,1024,1024]{2,1,0:T(8,128)(2,1)} %get-tuple-element.59.refs_2_.refs_4_.refs_6_.refs_1_, bf16[8,1024,1024]{2,1,0:T(8,128)(2,1)} %get-tuple-element.60.refs_3_.refs_5_.refs_7_.refs_2_, ...), custom_call_target="tpu_custom_call" | custom-call | flops 10000000000 | bytes 1 | tf_op jit(solution)/shard_map/scatter_product/pallas_call | solution.py:305
  179.3 1.1 collective-permute-start.33
  180.4 4.5 %scatter_product.10 = (f32[512,256]{1,0:T(8,128)S(1)}, f32[512,256]{1,0:T(8,128)S(1)}) custom-call(bf16[2048,256]{1,0:T(8,128)(2,1)S(1)} %get-tuple-element.82.refs_0_, bf16[8,1024,1024]{2,1,0:T(8,128)(2,1)} %get-tuple-element.59.refs_2_.refs_4_.refs_6_.refs_1_, bf16[8,1024,1024]{2,1,0:T(8,128)(2,1)} %get-tuple-element.60.refs_3_.refs_5_.refs_7_.refs_2_), custom_call_target="tpu_custom_call" | custom-call | flops 10000000000 | bytes 1 | tf_op jit(solution)/shard_map/scatter_product/pallas_call | solution.py:305
  184.9 6.7 %collective-permute-done.30 = f32[512,256]{1,0:T(8,128)S(1)} collective-permute-done((f32[512,256]{1,0:T(8,128)S(1)}, f32[512,256]{1,0:T(8,128)S(1)}, u32[]{:S(2)}, u32[]{:S(2)}) %collective-permute-start.30) | collective-permute-done | bytes 524320 | tf_op jit(solution)/shard_map/ppermute | solution.py:328
  191.7 1.8 collective-permute-done.33
  195.6 1.6 maximum_maximum_fusion
  (76 shorter events, 15.2 us)
Async XLA Ops:
  0.6 6.6 %copy-start.1 = (f32[512,512]{1,0:T(8,128)S(1)}, f32[512,512]{1,0:T(8,128)}, u32[]{:S(2)}) copy-start(f32[512,512]{1,0:T(8,128)} %param.7) | copy-start | bytes 3145732
  0.6 22.3 %collective-permute-start.4 = (f32[8,16,128,128]{3,2,1,0:T(8,128)}, f32[8,16,128,128]{3,2,1,0:T(8,128)}, u32[]{:S(2)}, u32[]{:S(2)}) collective-permute-start(f32[8,16,128,128]{3,2,1,0:T(8,128)} %bitcast.11), channel_id=1, source_target_pairs={{0,1},{1,0},{2,3},{3,2},{4,5},{5,4},{6,7},{7,6},{8,9},{9,8},{10,11... | collective-permute-start | bytes 25165832 | tf_op jit(solution)/shard_map/ppermute | solution.py:334
  1.2 7.1 %copy-start.3 = (s32[8,1]{0,1:T(1,128)S(1)}, s32[8,1]{0,1:T(1,128)}, u32[]{:S(2)}) copy-start(s32[8,1]{0,1:T(1,128)} %param.11) | copy-start | bytes 100
  1.2 7.2 %copy-start.2 = (s32[8,1,16]{2,1,0:T(1,128)S(1)}, s32[8,1,16]{2,1,0:T(1,128)}, u32[]{:S(2)}) copy-start(s32[8,1,16]{2,1,0:T(1,128)} %param.10) | copy-start | bytes 1540
  2.5 15.4 %collective-permute-start = (f32[512,256]{1,0:T(8,128)S(1)}, f32[512,256]{1,0:T(8,128)S(1)}, u32[]{:S(2)}, u32[]{:S(2)}) collective-permute-start(f32[512,256]{1,0:T(8,128)S(1)} %get-tuple-element.94.refs_0_), channel_id=1, source_target_pairs={{0,4},{4,8},{8,12},{12,14},{14,10},{10,6},{6,2},{2,0},{1,5},{5,9},... | collective-permute-start | bytes 1572872 | tf_op jit(solution)/shard_map/ppermute | solution.py:328
  5.2 14.8 %collective-permute-start.2 = (f32[512,256]{1,0:T(8,128)S(1)}, f32[512,256]{1,0:T(8,128)S(1)}, u32[]{:S(2)}, u32[]{:S(2)}) collective-permute-start(f32[512,256]{1,0:T(8,128)S(1)} %get-tuple-element.93.refs_1_), channel_id=1, source_target_pairs={{4,0},{8,4},{12,8},{14,12},{10,14},{6,10},{2,6},{0,2},{5,1},{9,5},... | collective-permute-start | bytes 1572872 | tf_op jit(solution)/shard_map/ppermute | solution.py:331
  5.2 27.2 %collective-permute-start.6 = (f32[512,256]{1,0:T(8,128)S(1)}, f32[512,256]{1,0:T(8,128)}, u32[]{:S(2)}, u32[]{:S(2)}) collective-permute-start(f32[512,256]{1,0:T(8,128)S(1)} %get-tuple-element.93.refs_1_), channel_id=1, source_target_pairs={{0,4},{4,8},{8,12},{12,14},{14,10},{10,6},{6,2},{2,0},{1,5},{5,9},... | collective-permute-start | bytes 1572872 | tf_op jit(solution)/shard_map/ppermute | solution.py:328
  7.2 24.2 %collective-permute-start.7 = (f32[512,256]{1,0:T(8,128)S(1)}, f32[512,256]{1,0:T(8,128)}, u32[]{:S(2)}, u32[]{:S(2)}) collective-permute-start(f32[512,256]{1,0:T(8,128)S(1)} %get-tuple-element.94.refs_0_), channel_id=1, source_target_pairs={{4,0},{8,4},{12,8},{14,12},{10,14},{6,10},{2,6},{0,2},{5,1},{9,5},... | collective-permute-start | bytes 1572872 | tf_op jit(solution)/shard_map/ppermute | solution.py:331
  19.9 1.2 collective-permute-start.3
  19.9 22.5 %collective-permute-start.9 = (f32[512,256]{1,0:T(8,128)S(1)}, f32[512,256]{1,0:T(8,128)S(1)}, u32[]{:S(2)}, u32[]{:S(2)}) collective-permute-start(f32[512,256]{1,0:T(8,128)S(1)} %collective-permute-done.2.refs_3_), channel_id=1, source_target_pairs={{4,0},{8,4},{12,8},{14,12},{10,14},{6,10},{2,6},{0,2},{5,1},{9,5},... | collective-permute-start | bytes 1572872 | tf_op jit(solution)/shard_map/ppermute | solution.py:331
  21.1 22.4 %collective-permute-start.1 = (f32[512,256]{1,0:T(8,128)S(1)}, f32[512,256]{1,0:T(8,128)S(1)}, u32[]{:S(2)}, u32[]{:S(2)}) collective-permute-start(f32[512,256]{1,0:T(8,128)S(1)} %collective-permute-done.refs_0_), channel_id=1, source_target_pairs={{0,4},{4,8},{8,12},{12,14},{14,10},{10,6},{6,2},{2,0},{1,5},{5,9},... | collective-permute-start | bytes 1572872 | tf_op jit(solution)/shard_map/ppermute | solution.py:328
  31.4 22.7 %collective-permute-start.16 = (f32[512,256]{1,0:T(8,128)}, f32[512,256]{1,0:T(8,128)S(1)}, u32[]{:S(2)}, u32[]{:S(2)}) collective-permute-start(f32[512,256]{1,0:T(8,128)} %collective-permute-done.7.refs_2_), channel_id=1, source_target_pairs={{4,0},{8,4},{12,8},{14,12},{10,14},{6,10},{2,6},{0,2},{5,1},{9,5},... | collective-permute-start | bytes 1572872 | tf_op jit(solution)/shard_map/ppermute | solution.py:331
  32.4 23.4 %collective-permute-start.14 = (f32[512,256]{1,0:T(8,128)}, f32[512,256]{1,0:T(8,128)S(1)}, u32[]{:S(2)}, u32[]{:S(2)}) collective-permute-start(f32[512,256]{1,0:T(8,128)} %collective-permute-done.6.refs_1_), channel_id=1, source_target_pairs={{0,4},{4,8},{8,12},{12,14},{14,10},{10,6},{6,2},{2,0},{1,5},{5,9},... | collective-permute-start | bytes 1572872 | tf_op jit(solution)/shard_map/ppermute | solution.py:328
  42.4 22.6 %collective-permute-start.10 = (f32[512,256]{1,0:T(8,128)S(1)}, f32[512,256]{1,0:T(8,128)}, u32[]{:S(2)}, u32[]{:S(2)}) collective-permute-start(f32[512,256]{1,0:T(8,128)S(1)} %collective-permute-done.9.refs_3_), channel_id=1, source_target_pairs={{4,0},{8,4},{12,8},{14,12},{10,14},{6,10},{2,6},{0,2},{5,1},{9,5},... | collective-permute-start | bytes 1572872 | tf_op jit(solution)/shard_map/ppermute | solution.py:331
  43.5 21.5 %collective-permute-start.5 = (f32[512,256]{1,0:T(8,128)S(1)}, f32[512,256]{1,0:T(8,128)}, u32[]{:S(2)}, u32[]{:S(2)}) collective-permute-start(f32[512,256]{1,0:T(8,128)S(1)} %collective-permute-done.1.refs_0_), channel_id=1, source_target_pairs={{0,4},{4,8},{8,12},{12,14},{14,10},{10,6},{6,2},{2,0},{1,5},{5,9},... | collective-permute-start | bytes 1572872 | tf_op jit(solution)/shard_map/ppermute | solution.py:328
  54.2 22.0 %collective-permute-start.17 = (f32[512,256]{1,0:T(8,128)S(1)}, f32[512,256]{1,0:T(8,128)S(1)}, u32[]{:S(2)}, u32[]{:S(2)}) collective-permute-start(f32[512,256]{1,0:T(8,128)S(1)} %collective-permute-done.16.refs_2_), channel_id=1, source_target_pairs={{4,0},{8,4},{12,8},{14,12},{10,14},{6,10},{2,6},{0,2},{5,1},{9,5},... | collective-permute-start | bytes 1572872 | tf_op jit(solution)/shard_map/ppermute | solution.py:331
  55.8 20.3 %collective-permute-start.15 = (f32[512,256]{1,0:T(8,128)S(1)}, f32[512,256]{1,0:T(8,128)S(1)}, u32[]{:S(2)}, u32[]{:S(2)}) collective-permute-start(f32[512,256]{1,0:T(8,128)S(1)} %collective-permute-done.14.refs_1_), channel_id=1, source_target_pairs={{0,4},{4,8},{8,12},{12,14},{14,10},{10,6},{6,2},{2,0},{1,5},{5,9},... | collective-permute-start | bytes 1572872 | tf_op jit(solution)/shard_map/ppermute | solution.py:328
  65.0 21.6 %collective-permute-start.11 = (f32[512,256]{1,0:T(8,128)}, f32[512,256]{1,0:T(8,128)S(1)}, u32[]{:S(2)}, u32[]{:S(2)}) collective-permute-start(f32[512,256]{1,0:T(8,128)} %collective-permute-done.10.refs_3_), channel_id=1, source_target_pairs={{4,0},{8,4},{12,8},{14,12},{10,14},{6,10},{2,6},{0,2},{5,1},{9,5},... | collective-permute-start | bytes 1572872 | tf_op jit(solution)/shard_map/ppermute | solution.py:331
  65.0 21.6 %collective-permute-start.8 = (f32[512,256]{1,0:T(8,128)}, f32[512,256]{1,0:T(8,128)S(1)}, u32[]{:S(2)}, u32[]{:S(2)}) collective-permute-start(f32[512,256]{1,0:T(8,128)} %collective-permute-done.5.refs_0_), channel_id=1, source_target_pairs={{0,4},{4,8},{8,12},{12,14},{14,10},{10,6},{6,2},{2,0},{1,5},{5,9},... | collective-permute-start | bytes 1572872 | tf_op jit(solution)/shard_map/ppermute | solution.py:328
  73.2 16.0 %copy-start = (f32[1024,512]{1,0:T(8,128)S(1)}, f32[1024,512]{1,0:T(8,128)}, u32[]{:S(2)}) copy-start(f32[1024,512]{1,0:T(8,128)} %refs_9_.1) | copy-start | bytes 6291460
  83.5 5.7 %collective-permute-start.18 = (f32[1024,256]{1,0:T(8,128)S(1)}, f32[1024,256]{1,0:T(8,128)S(1)}, u32[]{:S(2)}, u32[]{:S(2)}) collective-permute-start(f32[1024,256]{1,0:T(8,128)S(1)} %gather_product.7.refs_7_), channel_id=1, source_target_pairs={{0,1},{1,0},{2,3},{3,2},{4,5},{5,4},{6,7},{7,6},{8,9},{9,8},{10,11... | collective-permute-start | bytes 3145736 | tf_op jit(solution)/shard_map/ppermute | solution.py:334
  86.6 1.9 collective-permute-start.13
  86.6 2.7 %collective-permute-start.12 = (f32[512,256]{1,0:T(8,128)S(1)}, f32[512,256]{1,0:T(8,128)S(1)}, u32[]{:S(2)}, u32[]{:S(2)}) collective-permute-start(f32[512,256]{1,0:T(8,128)S(1)} %collective-permute-done.8.refs_1_), channel_id=1, source_target_pairs={{0,1},{1,0},{2,3},{3,2},{4,5},{5,4},{6,7},{7,6},{8,9},{9,8},{10,11... | collective-permute-start | bytes 1572872 | tf_op jit(solution)/shard_map/ppermute | solution.py:334
  96.7 11.7 %collective-permute-start.35 = (f32[128,512]{1,0:T(8,128)S(1)}, f32[128,512]{1,0:T(8,128)S(1)}, u32[]{:S(2)}, u32[]{:S(2)}) collective-permute-start(f32[128,512]{1,0:T(8,128)S(1)} %get-tuple-element.92), channel_id=1, source_target_pairs={{0,2},{2,0},{4,6},{6,4},{8,10},{10,8},{12,14},{14,12},{1,3},{3,1},... | collective-permute-start | bytes 786440 | tf_op jit(solution)/shard_map/ppermute | solution.py:417
  99.7 17.4 %collective-permute-start.19 = (f32[512,256]{1,0:T(8,128)S(1)}, f32[512,256]{1,0:T(8,128)S(1)}, u32[]{:S(2)}, u32[]{:S(2)}) collective-permute-start(f32[512,256]{1,0:T(8,128)S(1)} %get-tuple-element.74), channel_id=1, source_target_pairs={{0,4},{4,8},{8,12},{12,14},{14,10},{10,6},{6,2},{2,0},{1,5},{5,9},... | collective-permute-start | bytes 1572872 | tf_op jit(solution)/shard_map/ppermute | solution.py:328
  101.4 15.6 %collective-permute-start.20 = (f32[512,256]{1,0:T(8,128)S(1)}, f32[512,256]{1,0:T(8,128)S(1)}, u32[]{:S(2)}, u32[]{:S(2)}) collective-permute-start(f32[512,256]{1,0:T(8,128)S(1)} %get-tuple-element.75), channel_id=1, source_target_pairs={{4,0},{8,4},{12,8},{14,12},{10,14},{6,10},{2,6},{0,2},{5,1},{9,5},... | collective-permute-start | bytes 1572872 | tf_op jit(solution)/shard_map/ppermute | solution.py:331
  106.3 29.5 %collective-permute-start.25 = (f32[512,256]{1,0:T(8,128)S(1)}, f32[512,256]{1,0:T(8,128)S(1)}, u32[]{:S(2)}, u32[]{:S(2)}) collective-permute-start(f32[512,256]{1,0:T(8,128)S(1)} %get-tuple-element.84), channel_id=1, source_target_pairs={{0,4},{4,8},{8,12},{12,14},{14,10},{10,6},{6,2},{2,0},{1,5},{5,9},... | collective-permute-start | bytes 1572872 | tf_op jit(solution)/shard_map/ppermute | solution.py:328
  108.0 27.8 %collective-permute-start.26 = (f32[512,256]{1,0:T(8,128)S(1)}, f32[512,256]{1,0:T(8,128)S(1)}, u32[]{:S(2)}, u32[]{:S(2)}) collective-permute-start(f32[512,256]{1,0:T(8,128)S(1)} %get-tuple-element.85), channel_id=1, source_target_pairs={{4,0},{8,4},{12,8},{14,12},{10,14},{6,10},{2,6},{0,2},{5,1},{9,5},... | collective-permute-start | bytes 1572872 | tf_op jit(solution)/shard_map/ppermute | solution.py:331
  108.4 24.7 %collective-permute-start.36 = (f32[128,512]{1,0:T(8,128)S(1)}, f32[128,512]{1,0:T(8,128)S(1)}, u32[]{:S(2)}, u32[]{:S(2)}) collective-permute-start(f32[128,512]{1,0:T(8,128)S(1)} %add.64), channel_id=1, source_target_pairs={{0,4},{2,6},{4,0},{6,2},{8,12},{10,14},{12,8},{14,10},{1,5},{3,7},... | collective-permute-start | bytes 786440 | tf_op jit(solution)/shard_map/ppermute | solution.py:417
  121.6 28.6 %collective-permute-start.21 = (f32[512,256]{1,0:T(8,128)S(1)}, f32[512,256]{1,0:T(8,128)S(1)}, u32[]{:S(2)}, u32[]{:S(2)}) collective-permute-start(f32[512,256]{1,0:T(8,128)S(1)} %get-tuple-element.76), channel_id=1, source_target_pairs={{0,4},{4,8},{8,12},{12,14},{14,10},{10,6},{6,2},{2,0},{1,5},{5,9},... | collective-permute-start | bytes 1572872 | tf_op jit(solution)/shard_map/ppermute | solution.py:328
  122.4 27.7 %collective-permute-start.22 = (f32[512,256]{1,0:T(8,128)S(1)}, f32[512,256]{1,0:T(8,128)S(1)}, u32[]{:S(2)}, u32[]{:S(2)}) collective-permute-start(f32[512,256]{1,0:T(8,128)S(1)} %get-tuple-element.77), channel_id=1, source_target_pairs={{4,0},{8,4},{12,8},{14,12},{10,14},{6,10},{2,6},{0,2},{5,1},{9,5},... | collective-permute-start | bytes 1572872 | tf_op jit(solution)/shard_map/ppermute | solution.py:331
  133.2 16.9 %collective-permute-start.37 = (f32[128,512]{1,0:T(8,128)S(1)}, f32[128,512]{1,0:T(8,128)S(1)}, u32[]{:S(2)}, u32[]{:S(2)}) collective-permute-start(f32[128,512]{1,0:T(8,128)S(1)} %add.65), channel_id=1, source_target_pairs={{0,8},{2,10},{4,12},{6,14},{8,0},{10,2},{12,4},{14,6},{1,9},{3,11}... | collective-permute-start | bytes 786440 | tf_op jit(solution)/shard_map/ppermute | solution.py:417
  140.4 19.1 %collective-permute-start.27 = (f32[512,256]{1,0:T(8,128)S(1)}, f32[512,256]{1,0:T(8,128)S(1)}, u32[]{:S(2)}, u32[]{:S(2)}) collective-permute-start(f32[512,256]{1,0:T(8,128)S(1)} %get-tuple-element.86), channel_id=1, source_target_pairs={{0,4},{4,8},{8,12},{12,14},{14,10},{10,6},{6,2},{2,0},{1,5},{5,9},... | collective-permute-start | bytes 1572872 | tf_op jit(solution)/shard_map/ppermute | solution.py:328
  140.4 20.8 %collective-permute-start.28 = (f32[512,256]{1,0:T(8,128)S(1)}, f32[512,256]{1,0:T(8,128)S(1)}, u32[]{:S(2)}, u32[]{:S(2)}) collective-permute-start(f32[512,256]{1,0:T(8,128)S(1)} %get-tuple-element.87), channel_id=1, source_target_pairs={{4,0},{8,4},{12,8},{14,12},{10,14},{6,10},{2,6},{0,2},{5,1},{9,5},... | collective-permute-start | bytes 1572872 | tf_op jit(solution)/shard_map/ppermute | solution.py:331
  150.1 8.3 %collective-permute-start.38 = (f32[128,512]{1,0:T(8,128)S(1)}, f32[128,512]{1,0:T(8,128)}, u32[]{:S(2)}, u32[]{:S(2)}) collective-permute-start(f32[128,512]{1,0:T(8,128)S(1)} %add.66), channel_id=1, source_target_pairs={{0,2},{2,0},{4,6},{6,4},{8,10},{10,8},{12,14},{14,12},{1,3},{3,1},... | collective-permute-start | bytes 786440 | tf_op jit(solution)/shard_map/ppermute | solution.py:417
  155.7 15.3 %collective-permute-start.23 = (f32[512,256]{1,0:T(8,128)}, f32[512,256]{1,0:T(8,128)}, u32[]{:S(2)}, u32[]{:S(2)}) collective-permute-start(f32[512,256]{1,0:T(8,128)} %get-tuple-element.78), channel_id=1, source_target_pairs={{0,4},{4,8},{8,12},{12,14},{14,10},{10,6},{6,2},{2,0},{1,5},{5,9},... | collective-permute-start | bytes 1572872 | tf_op jit(solution)/shard_map/ppermute | solution.py:328
  158.3 15.2 %collective-permute-start.24 = (f32[512,256]{1,0:T(8,128)}, f32[512,256]{1,0:T(8,128)}, u32[]{:S(2)}, u32[]{:S(2)}) collective-permute-start(f32[512,256]{1,0:T(8,128)} %get-tuple-element.79), channel_id=1, source_target_pairs={{4,0},{8,4},{12,8},{14,12},{10,14},{6,10},{2,6},{0,2},{5,1},{9,5},... | collective-permute-start | bytes 1572872 | tf_op jit(solution)/shard_map/ppermute | solution.py:331
  159.4 34.3 %collective-permute-start.39 = (f32[256,512]{1,0:T(8,128)S(1)}, f32[256,512]{1,0:T(8,128)S(1)}, u32[]{:S(2)}, u32[]{:S(2)}) collective-permute-start(f32[256,512]{1,0:T(8,128)S(1)} %pad_maximum_fusion.2), channel_id=1, source_target_pairs={{0,1},{1,0},{2,3},{3,2},{4,5},{5,4},{6,7},{7,6},{8,9},{9,8},{10,11... | collective-permute-start | bytes 1572872 | tf_op jit(solution)/shard_map/ppermute | solution.py:334
  165.7 19.1 %collective-permute-start.29 = (f32[512,256]{1,0:T(8,128)S(1)}, f32[512,256]{1,0:T(8,128)S(1)}, u32[]{:S(2)}, u32[]{:S(2)}) collective-permute-start(f32[512,256]{1,0:T(8,128)S(1)} %get-tuple-element.88), channel_id=1, source_target_pairs={{4,0},{8,4},{12,8},{14,12},{10,14},{6,10},{2,6},{0,2},{5,1},{9,5},... | collective-permute-start | bytes 1572872 | tf_op jit(solution)/shard_map/ppermute | solution.py:331
  166.0 25.7 %collective-permute-start.32 = (f32[512,256]{1,0:T(8,128)S(1)}, f32[512,256]{1,0:T(8,128)S(1)}, u32[]{:S(2)}, u32[]{:S(2)}) collective-permute-start(f32[512,256]{1,0:T(8,128)S(1)} %get-tuple-element.90), channel_id=1, source_target_pairs={{0,4},{4,8},{8,12},{12,14},{14,10},{10,6},{6,2},{2,0},{1,5},{5,9},... | collective-permute-start | bytes 1572872 | tf_op jit(solution)/shard_map/ppermute | solution.py:328
  178.3 13.2 %collective-permute-start.30 = (f32[512,256]{1,0:T(8,128)S(1)}, f32[512,256]{1,0:T(8,128)S(1)}, u32[]{:S(2)}, u32[]{:S(2)}) collective-permute-start(f32[512,256]{1,0:T(8,128)S(1)} %get-tuple-element.80), channel_id=1, source_target_pairs={{0,4},{4,8},{8,12},{12,14},{14,10},{10,6},{6,2},{2,0},{1,5},{5,9},... | collective-permute-start | bytes 1572872 | tf_op jit(solution)/shard_map/ppermute | solution.py:328
  179.3 14.2 %collective-permute-start.33 = (f32[512,256]{1,0:T(8,128)S(1)}, f32[512,256]{1,0:T(8,128)S(1)}, u32[]{:S(2)}, u32[]{:S(2)}) collective-permute-start(f32[512,256]{1,0:T(8,128)S(1)} %get-tuple-element.81), channel_id=1, source_target_pairs={{4,0},{8,4},{12,8},{14,12},{10,14},{6,10},{2,6},{0,2},{5,1},{9,5},... | collective-permute-start | bytes 1572872 | tf_op jit(solution)/shard_map/ppermute | solution.py:331
  191.6 3.2 %collective-permute-start.31 = (f32[512,256]{1,0:T(8,128)S(1)}, f32[512,256]{1,0:T(8,128)S(1)}, u32[]{:S(2)}, u32[]{:S(2)}) collective-permute-start(f32[512,256]{1,0:T(8,128)S(1)} %add_add_fusion.1), channel_id=1, source_target_pairs={{0,1},{1,0},{2,3},{3,2},{4,5},{5,4},{6,7},{7,6},{8,9},{9,8},{10,11... | collective-permute-start | bytes 1572872 | tf_op jit(solution)/shard_map/ppermute | solution.py:334
  193.6 2.0 %collective-permute-start.34 = (f32[512,256]{1,0:T(8,128)S(1)}, f32[512,256]{1,0:T(8,128)S(1)}, u32[]{:S(2)}, u32[]{:S(2)}) collective-permute-start(f32[512,256]{1,0:T(8,128)S(1)} %add_add_fusion), channel_id=1, source_target_pairs={{0,1},{1,0},{2,3},{3,2},{4,5},{5,4},{6,7},{7,6},{8,9},{9,8},{10,11... | collective-permute-start | bytes 1572872 | tf_op jit(solution)/shard_map/ppermute | solution.py:334

commit v5 on v4

--- a/solution.py
+++ b/solution.py
@@ -10,7 +10,7 @@
 BF16 = jnp.bfloat16
 F32 = jnp.float32
 MIB = 48
-SP_FLOPS = [10000000000,10000000000,10000000000,1,10000000000,1,10000000000]
+SP_FLOPS = [10_000_000_000, 1, 10_000_000_000, 1, 10_000_000_000, 1, 10_000_000_000]
 LAYER_MIB = 40
 SMALL = pl.CostEstimate(flops=10_000_000_000, transcendentals=0, bytes_accessed=8_000_000)
 
@@ -417,10 +417,19 @@
         return lax.ppermute(block, "row", [(i, i ^ distance) for i in range(size)])
 
     weight_mine = weight_mine + exchange(weight_sent, 1)
-    distance = 2
+    near_odd = jnp.mod(row // 2, 2)
+    quarter = weight_mine.shape[0] // 2
+    weight_sent = lax.dynamic_slice_in_dim(weight_mine, (1 - near_odd) * quarter, quarter, 0)
+    weight_part = lax.dynamic_slice_in_dim(weight_mine, near_odd * quarter, quarter, 0)
+    weight_part = weight_part + exchange(weight_sent, 2)
+    distance = 4
     while distance < size:
-        weight_mine = weight_mine + exchange(weight_mine, distance)
+        weight_part = weight_part + exchange(weight_part, distance)
         distance *= 2
+    weight_rest = exchange(weight_part, 2)
+    low = jnp.where(near_odd == 0, weight_part, weight_rest)
+    high = jnp.where(near_odd == 0, weight_rest, weight_part)
+    weight_mine = jnp.concatenate([low, high], 0)
     weight_theirs = exchange(weight_mine, 1)
     low = jnp.where(odd == 0, weight_mine, weight_theirs)
     high = jnp.where(odd == 0, weight_theirs, weight_mine)

time: 198 us -> 198 us (level)
  waiting for transfers between devices: 61.8 us -> 55 us
  other arithmetic: 6.95 us -> 10.5 us
  Pallas kernels: 90.5 us -> 94 us
    ppermute x14, waiting for transfers between devices: 15.8 us -> 9.74 us  [rear(): return lax.ppermute(block, 'row', back)]
    ppermute x14, waiting for transfers between devices: 24.8 us -> 21.4 us  [forth(): return lax.ppermute(block, 'row', ahead)]
    ppermute x4 -> x5, waiting for transfers between devices: 17.1 us -> 19.8 us  [exchange(): return lax.ppermute(block, 'row', [(i, i ^ distance) for i in range(size)])]
    pallas_call x7, Pallas kernels: 32.9 us -> 35.6 us  [scatter_product(): pl.pallas_call(scatter_kernel, out_shape=(jax.ShapeDtypeStruct((half, wid...]
    ppermute x4 -> x5, starting transfers between devices: 4.79 us -> 4.06 us  [exchange(): return lax.ppermute(block, 'row', [(i, i ^ distance) for i in range(size)])]
  transfers between devices with their start and end apart: 40 -> 41, of which waited for: 19 -> 19; matrix products, arithmetic and copies ran while one was open for 3% -> 5% of each run, Pallas kernels for 42% -> 44%
where the time goes in v5:
time: 198 us; the launch traced here: 197 us
  Pallas kernels  94 us (47%)
  waiting for transfers between devices  55 us (28%)
  starting transfers between devices  35.1 us (18%)
  other arithmetic  10.5 us (5%)
    pallas_call x7, Pallas kernels, scatter_product(): pl.pallas_call(scatter_kernel, out_shape=(jax.ShapeDtypeStruct((half, wid...  35.6 us
    pallas_call x4, Pallas kernels, gather_product(): pl.pallas_call(functools.partial(gather_kernel, blocks), out_shape=jax.Sh...  24.4 us
    pallas_call x3, Pallas kernels, densify(): pl.pallas_call(functools.partial(densify_kernel, first, size // 2), out_s...  23.6 us
    ppermute x14, starting transfers between devices, forth(): return lax.ppermute(block, 'row', ahead)  21.7 us
    ppermute x14, waiting for transfers between devices, forth(): return lax.ppermute(block, 'row', ahead)  21.4 us
    ppermute x5, waiting for transfers between devices, exchange(): return lax.ppermute(block, 'row', [(i, i ^ distance) for i in range(size)])  19.8 us
    ppermute x14, waiting for transfers between devices, rear(): return lax.ppermute(block, 'row', back)  9.74 us
    pallas_call x1, Pallas kernels, layer(): pl.pallas_call(layer_kernel, out_shape=(jax.ShapeDtypeStruct((rows, featu...  7.7 us
  transfers between devices with their start and end apart: 41, of which 19 were waited for; matrix products, arithmetic and copies ran while one was open for 5% of the time, Pallas kernels for 44%

profile of v5, /device:TPU:0, one launch (start us, length us, event | category | flops | bytes accessed | tf_op | source)
XLA Modules:
  0.0 197.0 jit_solution(9100699884125379966)
XLA Ops:
  1.2 1.3 constant_dynamic-slice_fusion.2
  2.5 2.7 %collective-permute-start = (f32[512,256]{1,0:T(8,128)S(1)}, f32[512,256]{1,0:T(8,128)S(1)}, u32[]{:S(2)}, u32[]{:S(2)}) collective-permute-start(f32[512,256]{1,0:T(8,128)S(1)} %get-tuple-element.94.refs_0_), channel_id=1, source_target_pairs={{0,4},{4,8},{8,12},{12,14},{14,10},{10,6},{6,2},{2,0},{1,5},{5,9},... | collective-permute-start | bytes 1572872 | tf_op jit(solution)/shard_map/ppermute | solution.py:328
  5.2 2.0 %collective-permute-start.6 = (f32[512,256]{1,0:T(8,128)S(1)}, f32[512,256]{1,0:T(8,128)}, u32[]{:S(2)}, u32[]{:S(2)}) collective-permute-start(f32[512,256]{1,0:T(8,128)S(1)} %get-tuple-element.93.refs_1_), channel_id=1, source_target_pairs={{0,4},{4,8},{8,12},{12,14},{14,10},{10,6},{6,2},{2,0},{1,5},{5,9},... | collective-permute-start | bytes 1572872 | tf_op jit(solution)/shard_map/ppermute | solution.py:328
  8.4 1.4 fusion
  9.8 8.1 %collective-permute-done.refs_0_ = f32[512,256]{1,0:T(8,128)S(1)} collective-permute-done((f32[512,256]{1,0:T(8,128)S(1)}, f32[512,256]{1,0:T(8,128)S(1)}, u32[]{:S(2)}, u32[]{:S(2)}) %collective-permute-start) | collective-permute-done | bytes 524320 | tf_op jit(solution)/shard_map/ppermute | solution.py:328
  17.9 2.1 %collective-permute-done.2.refs_3_ = f32[512,256]{1,0:T(8,128)S(1)} collective-permute-done((f32[512,256]{1,0:T(8,128)S(1)}, f32[512,256]{1,0:T(8,128)S(1)}, u32[]{:S(2)}, u32[]{:S(2)}) %collective-permute-start.2) | collective-permute-done | bytes 524320 | tf_op jit(solution)/shard_map/ppermute | solution.py:331
  19.9 1.2 collective-permute-done.3
  21.1 1.6 collective-permute-start.1
  23.0 8.5 %densify.3 = (bf16[8,1024,1024]{2,1,0:T(8,128)(2,1)}, bf16[8,1024,1024]{2,1,0:T(8,128)(2,1)}, bf16[1024,1024]{1,0:T(8,128)(2,1)S(1)}, bf16[1024,1024]{1,0:T(8,128)(2,1)S(1)}) custom-call(s32[2,2,8,16]{3,2,1,0:T(8,128)S(1)} %pad_add_fusion.place_ref, s32[2,8]{1,0:T(2,128)S(1)} %fusion.7.count_ref, f32[8,16,128,128]{3,2,1,0:T(8,128)} %bitcast.12, ...), custom_call_target="tpu_custom_call" | custom-call | bytes 18874368 | tf_op jit(solution)/shard_map/densify/pallas_call | solution.py:79
  32.1 1.4 collective-permute-start.14
  33.5 8.8 %densify.4 = (bf16[8,1024,1024]{2,1,0:T(8,128)(2,1)}, bf16[8,1024,1024]{2,1,0:T(8,128)(2,1)}, bf16[1024,1024]{1,0:T(8,128)(2,1)S(1)}, bf16[1024,1024]{1,0:T(8,128)(2,1)S(1)}) custom-call(s32[2,2,8,16]{3,2,1,0:T(8,128)S(1)} %pad_add_fusion.place_ref, ...), custom_call_target="tpu_custom_call", output_to_operand_aliasing={{0}: (4, {}), {1}: (5, {}), {2}: (6, {}), {3}: (7, {})} | custom-call | bytes 18874368 | tf_op jit(solution)/shard_map/densify/pallas_call | solution.py:79
  42.8 1.6 collective-permute-start.5
  44.4 6.3 %densify.5 = (bf16[8,1024,1024]{2,1,0:T(8,128)(2,1)}, bf16[8,1024,1024]{2,1,0:T(8,128)(2,1)}, bf16[1024,1024]{1,0:T(8,128)(2,1)S(1)}, bf16[1024,1024]{1,0:T(8,128)(2,1)S(1)}) custom-call(s32[2,2,8,16]{3,2,1,0:T(8,128)S(1)} %pad_add_fusion.place_ref, ...), custom_call_target="tpu_custom_call", output_to_operand_aliasing={{0}: (4, {}), {1}: (5, {}), {2}: (6, {}), {3}: (7, {})} | custom-call | bytes 12582912 | tf_op jit(solution)/shard_map/densify/pallas_call | solution.py:79
  50.8 3.7 %gather_product.4.refs_8_ = f32[1024,256]{1,0:T(8,128)S(1)} custom-call(f32[512,256]{1,0:T(8,128)S(1)} %get-tuple-element.94.refs_0_, f32[512,256]{1,0:T(8,128)S(1)} %get-tuple-element.93.refs_1_, bf16[8,1024,1024]{2,1,0:T(8,128)(2,1)} %get-tuple-element.59.refs_2_.refs_4_.refs_6_.refs_1_, ...), custom_call_target="tpu_custom_call" | custom-call | flops 1610612736 | bytes 7340032 | tf_op jit(solution)/shard_map/gather_product/pallas_call | solution.py:142
  54.9 1.7 collective-permute-start.15
  56.6 7.1 %gather_product.5.refs_8_ = f32[1024,256]{1,0:T(8,128)S(1)} custom-call(f32[512,256]{1,0:T(8,128)S(1)} %collective-permute-done.refs_0_, f32[512,256]{1,0:T(8,128)} %collective-permute-done.6.refs_1_, f32[512,256]{1,0:T(8,128)} %collective-permute-done.7.refs_2_, f32[512,256]{1,0:T(8,128)S(1)} %collective-permute-done.2.refs_3_, ...), custom_call_target="tpu_custom_call" | custom-call | flops 3221225472 | bytes 12582912 | tf_op jit(solution)/shard_map/gather_product/pallas_call | solution.py:142
  63.7 1.3 collective-permute-done.10.refs_3_
  65.0 2.0 %collective-permute-start.8 = (f32[512,256]{1,0:T(8,128)}, f32[512,256]{1,0:T(8,128)S(1)}, u32[]{:S(2)}, u32[]{:S(2)}) collective-permute-start(f32[512,256]{1,0:T(8,128)} %collective-permute-done.5.refs_0_), channel_id=1, source_target_pairs={{0,4},{4,8},{8,12},{12,14},{14,10},{10,6},{6,2},{2,0},{1,5},{5,9},... | collective-permute-start | bytes 1572872 | tf_op jit(solution)/shard_map/ppermute | solution.py:328
  67.0 6.2 %gather_product.6.refs_8_ = f32[1024,256]{1,0:T(8,128)S(1)} custom-call(f32[512,256]{1,0:T(8,128)S(1)} %collective-permute-done.1.refs_0_, f32[512,256]{1,0:T(8,128)S(1)} %collective-permute-done.14.refs_1_, f32[512,256]{1,0:T(8,128)S(1)} %collective-permute-done.16.refs_2_, f32[512,256]{1,0:T(8,128)S(1)} %collective-permute-done.9.refs_3_, ...), custom_call_target="tpu_custom_call" | custom-call | flops 3221225472 | bytes 12582912 | tf_op jit(solution)/shard_map/gather_product/pallas_call | solution.py:142
  73.2 2.9 %collective-permute-done.17.refs_2_ = f32[512,256]{1,0:T(8,128)S(1)} collective-permute-done((f32[512,256]{1,0:T(8,128)S(1)}, f32[512,256]{1,0:T(8,128)S(1)}, u32[]{:S(2)}, u32[]{:S(2)}) %collective-permute-start.17) | collective-permute-done | bytes 524320 | tf_op jit(solution)/shard_map/ppermute | solution.py:331
  76.1 7.4 %gather_product.7.refs_7_ = f32[1024,256]{1,0:T(8,128)S(1)} custom-call(f32[512,256]{1,0:T(8,128)} %collective-permute-done.5.refs_0_, f32[512,256]{1,0:T(8,128)S(1)} %collective-permute-done.15.refs_1_, f32[512,256]{1,0:T(8,128)S(1)} %collective-permute-done.17.refs_2_, f32[512,256]{1,0:T(8,128)} %collective-permute-done.10.refs_3_, ...), custom_call_target="tpu_custom_call" | custom-call | flops 3221225472 | bytes 12582912 | tf_op jit(solution)/shard_map/gather_product/pallas_call | solution.py:142
  83.6 3.0 %collective-permute-done.11.refs_2_ = f32[512,256]{1,0:T(8,128)S(1)} collective-permute-done((f32[512,256]{1,0:T(8,128)}, f32[512,256]{1,0:T(8,128)S(1)}, u32[]{:S(2)}, u32[]{:S(2)}) %collective-permute-start.11) | collective-permute-done | bytes 524320 | tf_op jit(solution)/shard_map/ppermute | solution.py:331
  87.1 1.4 collective-permute-done.13.refs_4_
  89.2 7.7 %layer.1 = (f32[1024,512]{1,0:T(8,128)}, bf16[2048,512]{1,0:T(8,128)(2,1)S(1)}, f32[128,512]{1,0:T(8,128)S(1)}, f32[128,512]{1,0:T(8,128)}) custom-call(s32[1]{0:T(128)} %bitcast.refs_0_, f32[512,256]{1,0:T(8,128)S(1)} %collective-permute-done.8.refs_1_, f32[512,256]{1,0:T(8,128)S(1)} %collective-permute-done.11.refs_2_, ...), custom_call_target="tpu_custom_call" | custom-call | flops 1 | bytes 1 | tf_op jit(solution)/shard_map/layer/pallas_call | solution.py:235
  97.2 2.8 %layer_grad.1 = (bf16[2048,256]{1,0:T(8,128)(2,1)S(1)}, f32[512,256]{1,0:T(8,128)S(1)}, f32[512,256]{1,0:T(8,128)S(1)}) custom-call(bf16[2048,512]{1,0:T(8,128)(2,1)S(1)} %get-tuple-element.72.refs_0_, bf16[1024,1024]{1,0:T(8,128)(2,1)S(1)} %get-tuple-element.65.refs_5_.refs_1_, bf16[1024,1024]{1,0:T(8,128)(2,1)S(1)} %get-tuple-element.66.refs_6_.refs_2_, ...), custom_call_target="tpu_custom_call" | custom-call | flops 10000000000 | bytes 1 | tf_op jit(solution)/shard_map/layer_grad/pallas_call | solution.py:259
  100.0 1.7 collective-permute-start.19
  102.1 4.3 %collective-permute-done.35 = f32[128,512]{1,0:T(8,128)} collective-permute-done((f32[128,512]{1,0:T(8,128)}, f32[128,512]{1,0:T(8,128)}, u32[]{:S(2)}, u32[]{:S(2)}) %collective-permute-start.35) | collective-permute-done | bytes 262176 | tf_op jit(solution)/shard_map/ppermute | solution.py:417
  108.3 5.5 %scatter_product.11 = (f32[512,256]{1,0:T(8,128)}, f32[512,256]{1,0:T(8,128)}) custom-call(bf16[2048,256]{1,0:T(8,128)(2,1)S(1)} %get-tuple-element.82.refs_0_, bf16[8,1024,1024]{2,1,0:T(8,128)(2,1)} %get-tuple-element.59.refs_2_.refs_4_.refs_6_.refs_1_, bf16[8,1024,1024]{2,1,0:T(8,128)(2,1)} %get-tuple-element.60.refs_3_.refs_5_.refs_7_.refs_2_), custom_call_target="tpu_custom_call" | custom-call | flops 1 | bytes 1 | tf_op jit(solution)/shard_map/scatter_product/pallas_call | solution.py:305
  113.7 1.3 collective-permute-start.25
  115.8 3.4 %collective-permute-done.36 = f32[64,512]{1,0:T(8,128)S(1)} collective-permute-done((f32[64,512]{1,0:T(8,128)S(1)}, f32[64,512]{1,0:T(8,128)S(1)}, u32[]{:S(2)}, u32[]{:S(2)}) %collective-permute-start.36) | collective-permute-done | bytes 131104 | tf_op jit(solution)/shard_map/ppermute | solution.py:417
  120.1 2.9 %collective-permute-start.37 = (f32[64,512]{1,0:T(8,128)S(1)}, f32[64,512]{1,0:T(8,128)S(1)}, u32[]{:S(2)}, u32[]{:S(2)}) collective-permute-start(f32[64,512]{1,0:T(8,128)S(1)} %dynamic-slice_add_fusion), channel_id=1, source_target_pairs={{0,8},{2,10},{4,12},{6,14},{8,0},{10,2},{12,4},{14,6},{1,9},{3,11}... | collective-permute-start | bytes 393224 | tf_op jit(solution)/shard_map/ppermute | solution.py:417
  123.0 5.8 %scatter_product.7 = (f32[512,256]{1,0:T(8,128)}, f32[512,256]{1,0:T(8,128)}) custom-call(bf16[2048,256]{1,0:T(8,128)(2,1)S(1)} %get-tuple-element.82.refs_0_, bf16[8,1024,1024]{2,1,0:T(8,128)(2,1)} %get-tuple-element.59.refs_2_.refs_4_.refs_6_.refs_1_, bf16[8,1024,1024]{2,1,0:T(8,128)(2,1)} %get-tuple-element.60.refs_3_.refs_5_.refs_7_.refs_2_, ...), custom_call_target="tpu_custom_call" | custom-call | flops 10000000000 | bytes 1 | tf_op jit(solution)/shard_map/scatter_product/pallas_call | solution.py:305
  128.8 2.0 %collective-permute-start.22 = (f32[512,256]{1,0:T(8,128)}, f32[512,256]{1,0:T(8,128)}, u32[]{:S(2)}, u32[]{:S(2)}) collective-permute-start(f32[512,256]{1,0:T(8,128)} %get-tuple-element.77), channel_id=1, source_target_pairs={{4,0},{8,4},{12,8},{14,12},{10,14},{6,10},{2,6},{0,2},{5,1},{9,5},... | collective-permute-start | bytes 1572872 | tf_op jit(solution)/shard_map/ppermute | solution.py:331
  130.8 6.9 %collective-permute-done.37 = f32[64,512]{1,0:T(8,128)S(1)} collective-permute-done((f32[64,512]{1,0:T(8,128)S(1)}, f32[64,512]{1,0:T(8,128)S(1)}, u32[]{:S(2)}, u32[]{:S(2)}) %collective-permute-start.37) | collective-permute-done | bytes 131104 | tf_op jit(solution)/shard_map/ppermute | solution.py:417
  137.9 4.5 %scatter_product.12 = (f32[512,256]{1,0:T(8,128)S(1)}, f32[512,256]{1,0:T(8,128)S(1)}) custom-call(bf16[2048,256]{1,0:T(8,128)(2,1)S(1)} %get-tuple-element.82.refs_0_, bf16[8,1024,1024]{2,1,0:T(8,128)(2,1)} %get-tuple-element.59.refs_2_.refs_4_.refs_6_.refs_1_, bf16[8,1024,1024]{2,1,0:T(8,128)(2,1)} %get-tuple-element.60.refs_3_.refs_5_.refs_7_.refs_2_, ...), custom_call_target="tpu_custom_call" | custom-call | flops 1 | bytes 1 | tf_op jit(solution)/shard_map/scatter_product/pallas_call | solution.py:305
  142.4 2.0 %collective-permute-start.27 = (f32[512,256]{1,0:T(8,128)S(1)}, f32[512,256]{1,0:T(8,128)S(1)}, u32[]{:S(2)}, u32[]{:S(2)}) collective-permute-start(f32[512,256]{1,0:T(8,128)S(1)} %get-tuple-element.86), channel_id=1, source_target_pairs={{0,4},{4,8},{8,12},{12,14},{14,10},{10,6},{6,2},{2,0},{1,5},{5,9},... | collective-permute-start | bytes 1572872 | tf_op jit(solution)/shard_map/ppermute | solution.py:328
  144.5 3.7 %collective-permute-done.38 = f32[64,512]{1,0:T(8,128)} collective-permute-done((f32[64,512]{1,0:T(8,128)S(1)}, f32[64,512]{1,0:T(8,128)}, u32[]{:S(2)}, u32[]{:S(2)}) %collective-permute-start.38) | collective-permute-done | bytes 131104 | tf_op jit(solution)/shard_map/ppermute | solution.py:417
  149.9 5.8 %scatter_product.8 = (f32[512,256]{1,0:T(8,128)}, f32[512,256]{1,0:T(8,128)}) custom-call(bf16[2048,256]{1,0:T(8,128)(2,1)S(1)} %get-tuple-element.82.refs_0_, bf16[8,1024,1024]{2,1,0:T(8,128)(2,1)} %get-tuple-element.59.refs_2_.refs_4_.refs_6_.refs_1_, bf16[8,1024,1024]{2,1,0:T(8,128)(2,1)} %get-tuple-element.60.refs_3_.refs_5_.refs_7_.refs_2_, ...), custom_call_target="tpu_custom_call" | custom-call | flops 10000000000 | bytes 1 | tf_op jit(solution)/shard_map/scatter_product/pallas_call | solution.py:305
  155.7 1.5 collective-permute-start.23
  157.7 1.5 collective-permute-done.39
  160.3 4.5 %scatter_product.13 = (f32[512,256]{1,0:T(8,128)S(1)}, f32[512,256]{1,0:T(8,128)S(1)}) custom-call(bf16[2048,256]{1,0:T(8,128)(2,1)S(1)} %get-tuple-element.82.refs_0_, bf16[8,1024,1024]{2,1,0:T(8,128)(2,1)} %get-tuple-element.59.refs_2_.refs_4_.refs_6_.refs_1_, bf16[8,1024,1024]{2,1,0:T(8,128)(2,1)} %get-tuple-element.60.refs_3_.refs_5_.refs_7_.refs_2_, ...), custom_call_target="tpu_custom_call" | custom-call | flops 1 | bytes 1 | tf_op jit(solution)/shard_map/scatter_product/pallas_call | solution.py:305
  164.9 2.4 %collective-permute-start.29 = (f32[512,256]{1,0:T(8,128)S(1)}, f32[512,256]{1,0:T(8,128)S(1)}, u32[]{:S(2)}, u32[]{:S(2)}) collective-permute-start(f32[512,256]{1,0:T(8,128)S(1)} %get-tuple-element.88), channel_id=1, source_target_pairs={{4,0},{8,4},{12,8},{14,12},{10,14},{6,10},{2,6},{0,2},{5,1},{9,5},... | collective-permute-start | bytes 1572872 | tf_op jit(solution)/shard_map/ppermute | solution.py:331
  167.2 1.4 collective-permute-done.23.refs_3_
  169.0 4.9 %scatter_product.9 = (f32[512,256]{1,0:T(8,128)S(1)}, f32[512,256]{1,0:T(8,128)S(1)}) custom-call(bf16[2048,256]{1,0:T(8,128)(2,1)S(1)} %get-tuple-element.82.refs_0_, bf16[8,1024,1024]{2,1,0:T(8,128)(2,1)} %get-tuple-element.59.refs_2_.refs_4_.refs_6_.refs_1_, bf16[8,1024,1024]{2,1,0:T(8,128)(2,1)} %get-tuple-element.60.refs_3_.refs_5_.refs_7_.refs_2_, ...), custom_call_target="tpu_custom_call" | custom-call | flops 10000000000 | bytes 1 | tf_op jit(solution)/shard_map/scatter_product/pallas_call | solution.py:305
  173.9 2.2 %collective-permute-start.30 = (f32[512,256]{1,0:T(8,128)S(1)}, f32[512,256]{1,0:T(8,128)S(1)}, u32[]{:S(2)}, u32[]{:S(2)}) collective-permute-start(f32[512,256]{1,0:T(8,128)S(1)} %get-tuple-element.80), channel_id=1, source_target_pairs={{0,4},{4,8},{8,12},{12,14},{14,10},{10,6},{6,2},{2,0},{1,5},{5,9},... | collective-permute-start | bytes 1572872 | tf_op jit(solution)/shard_map/ppermute | solution.py:328
  176.1 4.5 %scatter_product.10 = (f32[512,256]{1,0:T(8,128)S(1)}, f32[512,256]{1,0:T(8,128)S(1)}) custom-call(bf16[2048,256]{1,0:T(8,128)(2,1)S(1)} %get-tuple-element.82.refs_0_, bf16[8,1024,1024]{2,1,0:T(8,128)(2,1)} %get-tuple-element.59.refs_2_.refs_4_.refs_6_.refs_1_, bf16[8,1024,1024]{2,1,0:T(8,128)(2,1)} %get-tuple-element.60.refs_3_.refs_5_.refs_7_.refs_2_), custom_call_target="tpu_custom_call" | custom-call | flops 10000000000 | bytes 1 | tf_op jit(solution)/shard_map/scatter_product/pallas_call | solution.py:305
  180.6 11.9 %collective-permute-done.30 = f32[512,256]{1,0:T(8,128)S(1)} collective-permute-done((f32[512,256]{1,0:T(8,128)S(1)}, f32[512,256]{1,0:T(8,128)S(1)}, u32[]{:S(2)}, u32[]{:S(2)}) %collective-permute-start.30) | collective-permute-done | bytes 524320 | tf_op jit(solution)/shard_map/ppermute | solution.py:328
  195.4 1.6 maximum_maximum_fusion
  (83 shorter events, 15.8 us)
Async XLA Ops:
  0.6 6.6 %copy-start.1 = (f32[512,512]{1,0:T(8,128)S(1)}, f32[512,512]{1,0:T(8,128)}, u32[]{:S(2)}) copy-start(f32[512,512]{1,0:T(8,128)} %param.7) | copy-start | bytes 3145732
  0.6 22.3 %collective-permute-start.4 = (f32[8,16,128,128]{3,2,1,0:T(8,128)}, f32[8,16,128,128]{3,2,1,0:T(8,128)}, u32[]{:S(2)}, u32[]{:S(2)}) collective-permute-start(f32[8,16,128,128]{3,2,1,0:T(8,128)} %bitcast.11), channel_id=1, source_target_pairs={{0,1},{1,0},{2,3},{3,2},{4,5},{5,4},{6,7},{7,6},{8,9},{9,8},{10,11... | collective-permute-start | bytes 25165832 | tf_op jit(solution)/shard_map/ppermute | solution.py:334
  1.2 7.1 %copy-start.4 = (s32[8,1]{0,1:T(1,128)S(1)}, s32[8,1]{0,1:T(1,128)}, u32[]{:S(2)}) copy-start(s32[8,1]{0,1:T(1,128)} %param.11) | copy-start | bytes 100
  1.2 7.2 %copy-start.3 = (s32[8,1,16]{2,1,0:T(1,128)S(1)}, s32[8,1,16]{2,1,0:T(1,128)}, u32[]{:S(2)}) copy-start(s32[8,1,16]{2,1,0:T(1,128)} %param.10) | copy-start | bytes 1540
  2.5 15.4 %collective-permute-start = (f32[512,256]{1,0:T(8,128)S(1)}, f32[512,256]{1,0:T(8,128)S(1)}, u32[]{:S(2)}, u32[]{:S(2)}) collective-permute-start(f32[512,256]{1,0:T(8,128)S(1)} %get-tuple-element.94.refs_0_), channel_id=1, source_target_pairs={{0,4},{4,8},{8,12},{12,14},{14,10},{10,6},{6,2},{2,0},{1,5},{5,9},... | collective-permute-start | bytes 1572872 | tf_op jit(solution)/shard_map/ppermute | solution.py:328
  5.2 14.8 %collective-permute-start.2 = (f32[512,256]{1,0:T(8,128)S(1)}, f32[512,256]{1,0:T(8,128)S(1)}, u32[]{:S(2)}, u32[]{:S(2)}) collective-permute-start(f32[512,256]{1,0:T(8,128)S(1)} %get-tuple-element.93.refs_1_), channel_id=1, source_target_pairs={{4,0},{8,4},{12,8},{14,12},{10,14},{6,10},{2,6},{0,2},{5,1},{9,5},... | collective-permute-start | bytes 1572872 | tf_op jit(solution)/shard_map/ppermute | solution.py:331
  5.2 26.9 %collective-permute-start.6 = (f32[512,256]{1,0:T(8,128)S(1)}, f32[512,256]{1,0:T(8,128)}, u32[]{:S(2)}, u32[]{:S(2)}) collective-permute-start(f32[512,256]{1,0:T(8,128)S(1)} %get-tuple-element.93.refs_1_), channel_id=1, source_target_pairs={{0,4},{4,8},{8,12},{12,14},{14,10},{10,6},{6,2},{2,0},{1,5},{5,9},... | collective-permute-start | bytes 1572872 | tf_op jit(solution)/shard_map/ppermute | solution.py:328
  7.2 24.2 %collective-permute-start.7 = (f32[512,256]{1,0:T(8,128)S(1)}, f32[512,256]{1,0:T(8,128)}, u32[]{:S(2)}, u32[]{:S(2)}) collective-permute-start(f32[512,256]{1,0:T(8,128)S(1)} %get-tuple-element.94.refs_0_), channel_id=1, source_target_pairs={{4,0},{8,4},{12,8},{14,12},{10,14},{6,10},{2,6},{0,2},{5,1},{9,5},... | collective-permute-start | bytes 1572872 | tf_op jit(solution)/shard_map/ppermute | solution.py:331
  19.9 1.2 collective-permute-start.3
  19.9 22.5 %collective-permute-start.9 = (f32[512,256]{1,0:T(8,128)S(1)}, f32[512,256]{1,0:T(8,128)S(1)}, u32[]{:S(2)}, u32[]{:S(2)}) collective-permute-start(f32[512,256]{1,0:T(8,128)S(1)} %collective-permute-done.2.refs_3_), channel_id=1, source_target_pairs={{4,0},{8,4},{12,8},{14,12},{10,14},{6,10},{2,6},{0,2},{5,1},{9,5},... | collective-permute-start | bytes 1572872 | tf_op jit(solution)/shard_map/ppermute | solution.py:331
  21.1 21.7 %collective-permute-start.1 = (f32[512,256]{1,0:T(8,128)S(1)}, f32[512,256]{1,0:T(8,128)S(1)}, u32[]{:S(2)}, u32[]{:S(2)}) collective-permute-start(f32[512,256]{1,0:T(8,128)S(1)} %collective-permute-done.refs_0_), channel_id=1, source_target_pairs={{0,4},{4,8},{8,12},{12,14},{14,10},{10,6},{6,2},{2,0},{1,5},{5,9},... | collective-permute-start | bytes 1572872 | tf_op jit(solution)/shard_map/ppermute | solution.py:328
  31.4 23.1 %collective-permute-start.16 = (f32[512,256]{1,0:T(8,128)}, f32[512,256]{1,0:T(8,128)S(1)}, u32[]{:S(2)}, u32[]{:S(2)}) collective-permute-start(f32[512,256]{1,0:T(8,128)} %collective-permute-done.7.refs_2_), channel_id=1, source_target_pairs={{4,0},{8,4},{12,8},{14,12},{10,14},{6,10},{2,6},{0,2},{5,1},{9,5},... | collective-permute-start | bytes 1572872 | tf_op jit(solution)/shard_map/ppermute | solution.py:331
  32.1 22.8 %collective-permute-start.14 = (f32[512,256]{1,0:T(8,128)}, f32[512,256]{1,0:T(8,128)S(1)}, u32[]{:S(2)}, u32[]{:S(2)}) collective-permute-start(f32[512,256]{1,0:T(8,128)} %collective-permute-done.6.refs_1_), channel_id=1, source_target_pairs={{0,4},{4,8},{8,12},{12,14},{14,10},{10,6},{6,2},{2,0},{1,5},{5,9},... | collective-permute-start | bytes 1572872 | tf_op jit(solution)/shard_map/ppermute | solution.py:328
  42.4 22.6 %collective-permute-start.10 = (f32[512,256]{1,0:T(8,128)S(1)}, f32[512,256]{1,0:T(8,128)}, u32[]{:S(2)}, u32[]{:S(2)}) collective-permute-start(f32[512,256]{1,0:T(8,128)S(1)} %collective-permute-done.9.refs_3_), channel_id=1, source_target_pairs={{4,0},{8,4},{12,8},{14,12},{10,14},{6,10},{2,6},{0,2},{5,1},{9,5},... | collective-permute-start | bytes 1572872 | tf_op jit(solution)/shard_map/ppermute | solution.py:331
  42.8 22.2 %collective-permute-start.5 = (f32[512,256]{1,0:T(8,128)S(1)}, f32[512,256]{1,0:T(8,128)}, u32[]{:S(2)}, u32[]{:S(2)}) collective-permute-start(f32[512,256]{1,0:T(8,128)S(1)} %collective-permute-done.1.refs_0_), channel_id=1, source_target_pairs={{0,4},{4,8},{8,12},{12,14},{14,10},{10,6},{6,2},{2,0},{1,5},{5,9},... | collective-permute-start | bytes 1572872 | tf_op jit(solution)/shard_map/ppermute | solution.py:328
  54.5 21.6 %collective-permute-start.17 = (f32[512,256]{1,0:T(8,128)S(1)}, f32[512,256]{1,0:T(8,128)S(1)}, u32[]{:S(2)}, u32[]{:S(2)}) collective-permute-start(f32[512,256]{1,0:T(8,128)S(1)} %collective-permute-done.16.refs_2_), channel_id=1, source_target_pairs={{4,0},{8,4},{12,8},{14,12},{10,14},{6,10},{2,6},{0,2},{5,1},{9,5},... | collective-permute-start | bytes 1572872 | tf_op jit(solution)/shard_map/ppermute | solution.py:331
  54.9 21.3 %collective-permute-start.15 = (f32[512,256]{1,0:T(8,128)S(1)}, f32[512,256]{1,0:T(8,128)S(1)}, u32[]{:S(2)}, u32[]{:S(2)}) collective-permute-start(f32[512,256]{1,0:T(8,128)S(1)} %collective-permute-done.14.refs_1_), channel_id=1, source_target_pairs={{0,4},{4,8},{8,12},{12,14},{14,10},{10,6},{6,2},{2,0},{1,5},{5,9},... | collective-permute-start | bytes 1572872 | tf_op jit(solution)/shard_map/ppermute | solution.py:328
  65.0 21.6 %collective-permute-start.11 = (f32[512,256]{1,0:T(8,128)}, f32[512,256]{1,0:T(8,128)S(1)}, u32[]{:S(2)}, u32[]{:S(2)}) collective-permute-start(f32[512,256]{1,0:T(8,128)} %collective-permute-done.10.refs_3_), channel_id=1, source_target_pairs={{4,0},{8,4},{12,8},{14,12},{10,14},{6,10},{2,6},{0,2},{5,1},{9,5},... | collective-permute-start | bytes 1572872 | tf_op jit(solution)/shard_map/ppermute | solution.py:331
  65.0 21.6 %collective-permute-start.8 = (f32[512,256]{1,0:T(8,128)}, f32[512,256]{1,0:T(8,128)S(1)}, u32[]{:S(2)}, u32[]{:S(2)}) collective-permute-start(f32[512,256]{1,0:T(8,128)} %collective-permute-done.5.refs_0_), channel_id=1, source_target_pairs={{0,4},{4,8},{8,12},{12,14},{14,10},{10,6},{6,2},{2,0},{1,5},{5,9},... | collective-permute-start | bytes 1572872 | tf_op jit(solution)/shard_map/ppermute | solution.py:328
  73.2 16.0 %copy-start = (f32[1024,512]{1,0:T(8,128)S(1)}, f32[1024,512]{1,0:T(8,128)}, u32[]{:S(2)}) copy-start(f32[1024,512]{1,0:T(8,128)} %refs_9_.1) | copy-start | bytes 6291460
  83.5 5.8 %collective-permute-start.18 = (f32[1024,256]{1,0:T(8,128)S(1)}, f32[1024,256]{1,0:T(8,128)S(1)}, u32[]{:S(2)}, u32[]{:S(2)}) collective-permute-start(f32[1024,256]{1,0:T(8,128)S(1)} %gather_product.7.refs_7_), channel_id=1, source_target_pairs={{0,1},{1,0},{2,3},{3,2},{4,5},{5,4},{6,7},{7,6},{8,9},{9,8},{10,11... | collective-permute-start | bytes 3145736 | tf_op jit(solution)/shard_map/ppermute | solution.py:334
  86.6 1.9 collective-permute-start.13
  86.6 2.7 %collective-permute-start.12 = (f32[512,256]{1,0:T(8,128)S(1)}, f32[512,256]{1,0:T(8,128)S(1)}, u32[]{:S(2)}, u32[]{:S(2)}) collective-permute-start(f32[512,256]{1,0:T(8,128)S(1)} %collective-permute-done.8.refs_1_), channel_id=1, source_target_pairs={{0,1},{1,0},{2,3},{3,2},{4,5},{5,4},{6,7},{7,6},{8,9},{9,8},{10,11... | collective-permute-start | bytes 1572872 | tf_op jit(solution)/shard_map/ppermute | solution.py:334
  96.9 9.5 %collective-permute-start.35 = (f32[128,512]{1,0:T(8,128)}, f32[128,512]{1,0:T(8,128)}, u32[]{:S(2)}, u32[]{:S(2)}) collective-permute-start(f32[128,512]{1,0:T(8,128)} %get-tuple-element.92), channel_id=1, source_target_pairs={{0,2},{2,0},{4,6},{6,4},{8,10},{10,8},{12,14},{14,12},{1,3},{3,1},... | collective-permute-start | bytes 786440 | tf_op jit(solution)/shard_map/ppermute | solution.py:417
  100.0 23.0 %collective-permute-start.19 = (f32[512,256]{1,0:T(8,128)S(1)}, f32[512,256]{1,0:T(8,128)}, u32[]{:S(2)}, u32[]{:S(2)}) collective-permute-start(f32[512,256]{1,0:T(8,128)S(1)} %get-tuple-element.74), channel_id=1, source_target_pairs={{0,4},{4,8},{8,12},{12,14},{14,10},{10,6},{6,2},{2,0},{1,5},{5,9},... | collective-permute-start | bytes 1572872 | tf_op jit(solution)/shard_map/ppermute | solution.py:328
  101.7 21.3 %collective-permute-start.20 = (f32[512,256]{1,0:T(8,128)S(1)}, f32[512,256]{1,0:T(8,128)}, u32[]{:S(2)}, u32[]{:S(2)}) collective-permute-start(f32[512,256]{1,0:T(8,128)S(1)} %get-tuple-element.75), channel_id=1, source_target_pairs={{4,0},{8,4},{12,8},{14,12},{10,14},{6,10},{2,6},{0,2},{5,1},{9,5},... | collective-permute-start | bytes 1572872 | tf_op jit(solution)/shard_map/ppermute | solution.py:331
  107.4 6.3 %copy-start.2 = (f32[128,512]{1,0:T(8,128)}, f32[128,512]{1,0:T(8,128)S(1)}, u32[]{:S(2)}) copy-start(f32[128,512]{1,0:T(8,128)S(1)} %add.74) | copy-start | bytes 786436
  107.4 11.8 %collective-permute-start.36 = (f32[64,512]{1,0:T(8,128)S(1)}, f32[64,512]{1,0:T(8,128)S(1)}, u32[]{:S(2)}, u32[]{:S(2)}) collective-permute-start(f32[64,512]{1,0:T(8,128)S(1)} %constant_dynamic-slice_fusion), channel_id=1, source_target_pairs={{0,4},{2,6},{4,0},{6,2},{8,12},{10,14},{12,8},{14,10},{1,5},{3,7},... | collective-permute-start | bytes 393224 | tf_op jit(solution)/shard_map/ppermute | solution.py:417
  113.7 24.1 %collective-permute-start.25 = (f32[512,256]{1,0:T(8,128)}, f32[512,256]{1,0:T(8,128)S(1)}, u32[]{:S(2)}, u32[]{:S(2)}) collective-permute-start(f32[512,256]{1,0:T(8,128)} %get-tuple-element.84), channel_id=1, source_target_pairs={{0,4},{4,8},{8,12},{12,14},{14,10},{10,6},{6,2},{2,0},{1,5},{5,9},... | collective-permute-start | bytes 1572872 | tf_op jit(solution)/shard_map/ppermute | solution.py:328
  115.0 22.9 %collective-permute-start.26 = (f32[512,256]{1,0:T(8,128)}, f32[512,256]{1,0:T(8,128)S(1)}, u32[]{:S(2)}, u32[]{:S(2)}) collective-permute-start(f32[512,256]{1,0:T(8,128)} %get-tuple-element.85), channel_id=1, source_target_pairs={{4,0},{8,4},{12,8},{14,12},{10,14},{6,10},{2,6},{0,2},{5,1},{9,5},... | collective-permute-start | bytes 1572872 | tf_op jit(solution)/shard_map/ppermute | solution.py:331
  120.1 17.7 %collective-permute-start.37 = (f32[64,512]{1,0:T(8,128)S(1)}, f32[64,512]{1,0:T(8,128)S(1)}, u32[]{:S(2)}, u32[]{:S(2)}) collective-permute-start(f32[64,512]{1,0:T(8,128)S(1)} %dynamic-slice_add_fusion), channel_id=1, source_target_pairs={{0,8},{2,10},{4,12},{6,14},{8,0},{10,2},{12,4},{14,6},{1,9},{3,11}... | collective-permute-start | bytes 393224 | tf_op jit(solution)/shard_map/ppermute | solution.py:417
  128.8 21.1 %collective-permute-start.21 = (f32[512,256]{1,0:T(8,128)}, f32[512,256]{1,0:T(8,128)}, u32[]{:S(2)}, u32[]{:S(2)}) collective-permute-start(f32[512,256]{1,0:T(8,128)} %get-tuple-element.76), channel_id=1, source_target_pairs={{0,4},{4,8},{8,12},{12,14},{14,10},{10,6},{6,2},{2,0},{1,5},{5,9},... | collective-permute-start | bytes 1572872 | tf_op jit(solution)/shard_map/ppermute | solution.py:328
  128.8 21.1 %collective-permute-start.22 = (f32[512,256]{1,0:T(8,128)}, f32[512,256]{1,0:T(8,128)}, u32[]{:S(2)}, u32[]{:S(2)}) collective-permute-start(f32[512,256]{1,0:T(8,128)} %get-tuple-element.77), channel_id=1, source_target_pairs={{4,0},{8,4},{12,8},{14,12},{10,14},{6,10},{2,6},{0,2},{5,1},{9,5},... | collective-permute-start | bytes 1572872 | tf_op jit(solution)/shard_map/ppermute | solution.py:331
  137.8 10.4 %collective-permute-start.38 = (f32[64,512]{1,0:T(8,128)S(1)}, f32[64,512]{1,0:T(8,128)}, u32[]{:S(2)}, u32[]{:S(2)}) collective-permute-start(f32[64,512]{1,0:T(8,128)S(1)} %add.78), channel_id=1, source_target_pairs={{0,4},{2,6},{4,0},{6,2},{8,12},{10,14},{12,8},{14,10},{1,5},{3,7},... | collective-permute-start | bytes 393224 | tf_op jit(solution)/shard_map/ppermute | solution.py:417
  142.4 17.9 %collective-permute-start.27 = (f32[512,256]{1,0:T(8,128)S(1)}, f32[512,256]{1,0:T(8,128)S(1)}, u32[]{:S(2)}, u32[]{:S(2)}) collective-permute-start(f32[512,256]{1,0:T(8,128)S(1)} %get-tuple-element.86), channel_id=1, source_target_pairs={{0,4},{4,8},{8,12},{12,14},{14,10},{10,6},{6,2},{2,0},{1,5},{5,9},... | collective-permute-start | bytes 1572872 | tf_op jit(solution)/shard_map/ppermute | solution.py:328
  144.5 15.8 %collective-permute-start.28 = (f32[512,256]{1,0:T(8,128)S(1)}, f32[512,256]{1,0:T(8,128)S(1)}, u32[]{:S(2)}, u32[]{:S(2)}) collective-permute-start(f32[512,256]{1,0:T(8,128)S(1)} %get-tuple-element.87), channel_id=1, source_target_pairs={{4,0},{8,4},{12,8},{14,12},{10,14},{6,10},{2,6},{0,2},{5,1},{9,5},... | collective-permute-start | bytes 1572872 | tf_op jit(solution)/shard_map/ppermute | solution.py:331
  149.8 9.3 %collective-permute-start.39 = (f32[128,512]{1,0:T(8,128)}, f32[128,512]{1,0:T(8,128)}, u32[]{:S(2)}, u32[]{:S(2)}) collective-permute-start(f32[128,512]{1,0:T(8,128)} %pad_maximum_fusion.3), channel_id=1, source_target_pairs={{0,2},{2,0},{4,6},{6,4},{8,10},{10,8},{12,14},{14,12},{1,3},{3,1},... | collective-permute-start | bytes 786440 | tf_op jit(solution)/shard_map/ppermute | solution.py:417
  155.7 12.9 %collective-permute-start.23 = (f32[512,256]{1,0:T(8,128)}, f32[512,256]{1,0:T(8,128)}, u32[]{:S(2)}, u32[]{:S(2)}) collective-permute-start(f32[512,256]{1,0:T(8,128)} %get-tuple-element.78), channel_id=1, source_target_pairs={{0,4},{4,8},{8,12},{12,14},{14,10},{10,6},{6,2},{2,0},{1,5},{5,9},... | collective-permute-start | bytes 1572872 | tf_op jit(solution)/shard_map/ppermute | solution.py:328
  157.1 11.9 %collective-permute-start.24 = (f32[512,256]{1,0:T(8,128)}, f32[512,256]{1,0:T(8,128)}, u32[]{:S(2)}, u32[]{:S(2)}) collective-permute-start(f32[512,256]{1,0:T(8,128)} %get-tuple-element.79), channel_id=1, source_target_pairs={{4,0},{8,4},{12,8},{14,12},{10,14},{6,10},{2,6},{0,2},{5,1},{9,5},... | collective-permute-start | bytes 1572872 | tf_op jit(solution)/shard_map/ppermute | solution.py:331
  160.2 33.1 %collective-permute-start.40 = (f32[256,512]{1,0:T(8,128)S(1)}, f32[256,512]{1,0:T(8,128)S(1)}, u32[]{:S(2)}, u32[]{:S(2)}) collective-permute-start(f32[256,512]{1,0:T(8,128)S(1)} %pad_maximum_fusion.2), channel_id=1, source_target_pairs={{0,1},{1,0},{2,3},{3,2},{4,5},{5,4},{6,7},{7,6},{8,9},{9,8},{10,11... | collective-permute-start | bytes 1572872 | tf_op jit(solution)/shard_map/ppermute | solution.py:334
  164.9 15.7 %collective-permute-start.29 = (f32[512,256]{1,0:T(8,128)S(1)}, f32[512,256]{1,0:T(8,128)S(1)}, u32[]{:S(2)}, u32[]{:S(2)}) collective-permute-start(f32[512,256]{1,0:T(8,128)S(1)} %get-tuple-element.88), channel_id=1, source_target_pairs={{4,0},{8,4},{12,8},{14,12},{10,14},{6,10},{2,6},{0,2},{5,1},{9,5},... | collective-permute-start | bytes 1572872 | tf_op jit(solution)/shard_map/ppermute | solution.py:331
  167.2 25.4 %collective-permute-start.32 = (f32[512,256]{1,0:T(8,128)S(1)}, f32[512,256]{1,0:T(8,128)S(1)}, u32[]{:S(2)}, u32[]{:S(2)}) collective-permute-start(f32[512,256]{1,0:T(8,128)S(1)} %get-tuple-element.90), channel_id=1, source_target_pairs={{0,4},{4,8},{8,12},{12,14},{14,10},{10,6},{6,2},{2,0},{1,5},{5,9},... | collective-permute-start | bytes 1572872 | tf_op jit(solution)/shard_map/ppermute | solution.py:328
  173.9 18.6 %collective-permute-start.30 = (f32[512,256]{1,0:T(8,128)S(1)}, f32[512,256]{1,0:T(8,128)S(1)}, u32[]{:S(2)}, u32[]{:S(2)}) collective-permute-start(f32[512,256]{1,0:T(8,128)S(1)} %get-tuple-element.80), channel_id=1, source_target_pairs={{0,4},{4,8},{8,12},{12,14},{14,10},{10,6},{6,2},{2,0},{1,5},{5,9},... | collective-permute-start | bytes 1572872 | tf_op jit(solution)/shard_map/ppermute | solution.py:328
  176.1 16.6 %collective-permute-start.33 = (f32[512,256]{1,0:T(8,128)S(1)}, f32[512,256]{1,0:T(8,128)S(1)}, u32[]{:S(2)}, u32[]{:S(2)}) collective-permute-start(f32[512,256]{1,0:T(8,128)S(1)} %get-tuple-element.81), channel_id=1, source_target_pairs={{4,0},{8,4},{12,8},{14,12},{10,14},{6,10},{2,6},{0,2},{5,1},{9,5},... | collective-permute-start | bytes 1572872 | tf_op jit(solution)/shard_map/ppermute | solution.py:331
  192.6 2.0 %collective-permute-start.31 = (f32[512,256]{1,0:T(8,128)S(1)}, f32[512,256]{1,0:T(8,128)S(1)}, u32[]{:S(2)}, u32[]{:S(2)}) collective-permute-start(f32[512,256]{1,0:T(8,128)S(1)} %add_add_fusion.1), channel_id=1, source_target_pairs={{0,1},{1,0},{2,3},{3,2},{4,5},{5,4},{6,7},{7,6},{8,9},{9,8},{10,11... | collective-permute-start | bytes 1572872 | tf_op jit(solution)/shard_map/ppermute | solution.py:334
  192.8 2.5 %collective-permute-start.34 = (f32[512,256]{1,0:T(8,128)S(1)}, f32[512,256]{1,0:T(8,128)S(1)}, u32[]{:S(2)}, u32[]{:S(2)}) collective-permute-start(f32[512,256]{1,0:T(8,128)S(1)} %add_add_fusion), channel_id=1, source_target_pairs={{0,1},{1,0},{2,3},{3,2},{4,5},{5,4},{6,7},{7,6},{8,9},{9,8},{10,11... | collective-permute-start | bytes 1572872 | tf_op jit(solution)/shard_map/ppermute | solution.py:334

commit v6 on v5

--- a/solution.py
+++ b/solution.py
@@ -445,10 +445,15 @@
         tops = (forth(result[0]), rear(result[1]))
     home_top, home_bottom = scatter_product(dense[:2], after(grad, *result), (0, 0), (0, 1))
     weight_grad = order(weight_half, swap(weight_half), 0)
-    home_bottom = home_bottom + bottoms[0] + tops[1]
-    home_top = home_top + bottoms[1] + tops[0]
+    early = (home_top + bottoms[1], home_bottom + bottoms[0])
+    other_early = tuple(swap(v) for v in early)
+    other_tops = tuple(swap(v) for v in tops)
     input_grad = jnp.concatenate(
-        [order(home_top, swap(home_top), 1), order(home_bottom, swap(home_bottom), 1)], 0
+        [
+            order(early[n] + tops[n], other_early[n] + other_tops[n], 1)
+            for n in range(2)
+        ],
+        0,
     )
     return (output, input_grad, weight_grad)
 

time: 198 us -> 198 us (level)
    ppermute x8 -> x10, waiting for transfers between devices: 4.05 us -> 4.69 us  [swap(): return lax.ppermute(block, 'rep', [(0, 1), (1, 0)])]
  transfers between devices with their start and end apart: 41 -> 43, of which waited for: 19 -> 19; matrix products, arithmetic and copies ran while one was open for 5% -> 5% of each run, Pallas kernels for 44% -> 43%
where the time goes in v6:
time: 198 us; the launch traced here: 197 us
  Pallas kernels  93 us (47%)
  waiting for transfers between devices  56.5 us (29%)
  starting transfers between devices  35.1 us (18%)
  other arithmetic  10.5 us (5%)
    pallas_call x7, Pallas kernels, scatter_product(): pl.pallas_call(scatter_kernel, out_shape=(jax.ShapeDtypeStruct((half, wid...  35.6 us
    pallas_call x4, Pallas kernels, gather_product(): pl.pallas_call(functools.partial(gather_kernel, blocks), out_shape=jax.Sh...  24.3 us
    pallas_call x3, Pallas kernels, densify(): pl.pallas_call(functools.partial(densify_kernel, first, size // 2), out_s...  22.7 us
    ppermute x14, waiting for transfers between devices, forth(): return lax.ppermute(block, 'row', ahead)  21.1 us
    ppermute x14, starting transfers between devices, forth(): return lax.ppermute(block, 'row', ahead)  20.5 us
    ppermute x5, waiting for transfers between devices, exchange(): return lax.ppermute(block, 'row', [(i, i ^ distance) for i in range(size)])  19.7 us
    ppermute x14, waiting for transfers between devices, rear(): return lax.ppermute(block, 'row', back)  11 us
    ppermute x14, starting transfers between devices, rear(): return lax.ppermute(block, 'row', back)  8.63 us
  transfers between devices with their start and end apart: 43, of which 19 were waited for; matrix products, arithmetic and copies ran while one was open for 5% of the time, Pallas kernels for 43%

profile of v6, /device:TPU:0, one launch (start us, length us, event | category | flops | bytes accessed | tf_op | source)
XLA Modules:
  0.0 197.4 jit_solution(14339994178581106103)
XLA Ops:
  1.2 1.3 constant_dynamic-slice_fusion.2
  2.5 2.7 %collective-permute-start = (f32[512,256]{1,0:T(8,128)S(1)}, f32[512,256]{1,0:T(8,128)S(1)}, u32[]{:S(2)}, u32[]{:S(2)}) collective-permute-start(f32[512,256]{1,0:T(8,128)S(1)} %get-tuple-element.98.refs_0_), channel_id=1, source_target_pairs={{0,4},{4,8},{8,12},{12,14},{14,10},{10,6},{6,2},{2,0},{1,5},{5,9},... | collective-permute-start | bytes 1572872 | tf_op jit(solution)/shard_map/ppermute | solution.py:328
  5.2 2.0 %collective-permute-start.6 = (f32[512,256]{1,0:T(8,128)S(1)}, f32[512,256]{1,0:T(8,128)}, u32[]{:S(2)}, u32[]{:S(2)}) collective-permute-start(f32[512,256]{1,0:T(8,128)S(1)} %get-tuple-element.97.refs_1_), channel_id=1, source_target_pairs={{0,4},{4,8},{8,12},{12,14},{14,10},{10,6},{6,2},{2,0},{1,5},{5,9},... | collective-permute-start | bytes 1572872 | tf_op jit(solution)/shard_map/ppermute | solution.py:328
  8.4 1.4 fusion
  9.8 8.1 %collective-permute-done.refs_0_ = f32[512,256]{1,0:T(8,128)S(1)} collective-permute-done((f32[512,256]{1,0:T(8,128)S(1)}, f32[512,256]{1,0:T(8,128)S(1)}, u32[]{:S(2)}, u32[]{:S(2)}) %collective-permute-start) | collective-permute-done | bytes 524320 | tf_op jit(solution)/shard_map/ppermute | solution.py:328
  17.9 2.1 %collective-permute-done.2.refs_3_ = f32[512,256]{1,0:T(8,128)S(1)} collective-permute-done((f32[512,256]{1,0:T(8,128)S(1)}, f32[512,256]{1,0:T(8,128)S(1)}, u32[]{:S(2)}, u32[]{:S(2)}) %collective-permute-start.2) | collective-permute-done | bytes 524320 | tf_op jit(solution)/shard_map/ppermute | solution.py:331
  19.9 1.2 collective-permute-done.3
  21.1 1.6 collective-permute-start.1
  23.0 8.3 %densify.3 = (bf16[8,1024,1024]{2,1,0:T(8,128)(2,1)}, bf16[8,1024,1024]{2,1,0:T(8,128)(2,1)}, bf16[1024,1024]{1,0:T(8,128)(2,1)S(1)}, bf16[1024,1024]{1,0:T(8,128)(2,1)S(1)}) custom-call(s32[2,2,8,16]{3,2,1,0:T(8,128)S(1)} %pad_add_fusion.place_ref, s32[2,8]{1,0:T(2,128)S(1)} %fusion.7.count_ref, f32[8,16,128,128]{3,2,1,0:T(8,128)} %bitcast.12, ...), custom_call_target="tpu_custom_call" | custom-call | bytes 18874368 | tf_op jit(solution)/shard_map/densify/pallas_call | solution.py:79
  32.0 1.3 collective-permute-start.14
  33.3 8.4 %densify.4 = (bf16[8,1024,1024]{2,1,0:T(8,128)(2,1)}, bf16[8,1024,1024]{2,1,0:T(8,128)(2,1)}, bf16[1024,1024]{1,0:T(8,128)(2,1)S(1)}, bf16[1024,1024]{1,0:T(8,128)(2,1)S(1)}) custom-call(s32[2,2,8,16]{3,2,1,0:T(8,128)S(1)} %pad_add_fusion.place_ref, ...), custom_call_target="tpu_custom_call", output_to_operand_aliasing={{0}: (4, {}), {1}: (5, {}), {2}: (6, {}), {3}: (7, {})} | custom-call | bytes 18874368 | tf_op jit(solution)/shard_map/densify/pallas_call | solution.py:79
  43.1 1.4 collective-permute-start.5
  44.4 6.0 %densify.5 = (bf16[8,1024,1024]{2,1,0:T(8,128)(2,1)}, bf16[8,1024,1024]{2,1,0:T(8,128)(2,1)}, bf16[1024,1024]{1,0:T(8,128)(2,1)S(1)}, bf16[1024,1024]{1,0:T(8,128)(2,1)S(1)}) custom-call(s32[2,2,8,16]{3,2,1,0:T(8,128)S(1)} %pad_add_fusion.place_ref, ...), custom_call_target="tpu_custom_call", output_to_operand_aliasing={{0}: (4, {}), {1}: (5, {}), {2}: (6, {}), {3}: (7, {})} | custom-call | bytes 12582912 | tf_op jit(solution)/shard_map/densify/pallas_call | solution.py:79
  50.5 3.7 %gather_product.4.refs_8_ = f32[1024,256]{1,0:T(8,128)S(1)} custom-call(f32[512,256]{1,0:T(8,128)S(1)} %get-tuple-element.98.refs_0_, f32[512,256]{1,0:T(8,128)S(1)} %get-tuple-element.97.refs_1_, bf16[8,1024,1024]{2,1,0:T(8,128)(2,1)} %get-tuple-element.59.refs_2_.refs_4_.refs_6_.refs_1_, ...), custom_call_target="tpu_custom_call" | custom-call | flops 1610612736 | bytes 7340032 | tf_op jit(solution)/shard_map/gather_product/pallas_call | solution.py:142
  55.2 1.2 collective-permute-start.15
  56.3 7.1 %gather_product.5.refs_8_ = f32[1024,256]{1,0:T(8,128)S(1)} custom-call(f32[512,256]{1,0:T(8,128)S(1)} %collective-permute-done.refs_0_, f32[512,256]{1,0:T(8,128)} %collective-permute-done.6.refs_1_, f32[512,256]{1,0:T(8,128)} %collective-permute-done.7.refs_2_, f32[512,256]{1,0:T(8,128)S(1)} %collective-permute-done.2.refs_3_, ...), custom_call_target="tpu_custom_call" | custom-call | flops 3221225472 | bytes 12582912 | tf_op jit(solution)/shard_map/gather_product/pallas_call | solution.py:142
  63.4 1.6 collective-permute-done.10.refs_3_
  65.0 2.0 %collective-permute-start.8 = (f32[512,256]{1,0:T(8,128)}, f32[512,256]{1,0:T(8,128)S(1)}, u32[]{:S(2)}, u32[]{:S(2)}) collective-permute-start(f32[512,256]{1,0:T(8,128)} %collective-permute-done.5.refs_0_), channel_id=1, source_target_pairs={{0,4},{4,8},{8,12},{12,14},{14,10},{10,6},{6,2},{2,0},{1,5},{5,9},... | collective-permute-start | bytes 1572872 | tf_op jit(solution)/shard_map/ppermute | solution.py:328
  67.0 6.2 %gather_product.6.refs_8_ = f32[1024,256]{1,0:T(8,128)S(1)} custom-call(f32[512,256]{1,0:T(8,128)S(1)} %collective-permute-done.1.refs_0_, f32[512,256]{1,0:T(8,128)S(1)} %collective-permute-done.14.refs_1_, f32[512,256]{1,0:T(8,128)S(1)} %collective-permute-done.16.refs_2_, f32[512,256]{1,0:T(8,128)S(1)} %collective-permute-done.9.refs_3_, ...), custom_call_target="tpu_custom_call" | custom-call | flops 3221225472 | bytes 12582912 | tf_op jit(solution)/shard_map/gather_product/pallas_call | solution.py:142
  73.2 2.9 %collective-permute-done.17.refs_2_ = f32[512,256]{1,0:T(8,128)S(1)} collective-permute-done((f32[512,256]{1,0:T(8,128)S(1)}, f32[512,256]{1,0:T(8,128)S(1)}, u32[]{:S(2)}, u32[]{:S(2)}) %collective-permute-start.17) | collective-permute-done | bytes 524320 | tf_op jit(solution)/shard_map/ppermute | solution.py:331
  76.1 7.3 %gather_product.7.refs_7_ = f32[1024,256]{1,0:T(8,128)S(1)} custom-call(f32[512,256]{1,0:T(8,128)} %collective-permute-done.5.refs_0_, f32[512,256]{1,0:T(8,128)S(1)} %collective-permute-done.15.refs_1_, f32[512,256]{1,0:T(8,128)S(1)} %collective-permute-done.17.refs_2_, f32[512,256]{1,0:T(8,128)} %collective-permute-done.10.refs_3_, ...), custom_call_target="tpu_custom_call" | custom-call | flops 3221225472 | bytes 12582912 | tf_op jit(solution)/shard_map/gather_product/pallas_call | solution.py:142
  83.5 3.0 %collective-permute-done.11.refs_2_ = f32[512,256]{1,0:T(8,128)S(1)} collective-permute-done((f32[512,256]{1,0:T(8,128)}, f32[512,256]{1,0:T(8,128)S(1)}, u32[]{:S(2)}, u32[]{:S(2)}) %collective-permute-start.11) | collective-permute-done | bytes 524320 | tf_op jit(solution)/shard_map/ppermute | solution.py:331
  87.1 1.4 collective-permute-done.13.refs_4_
  89.2 7.7 %layer.1 = (f32[1024,512]{1,0:T(8,128)}, bf16[2048,512]{1,0:T(8,128)(2,1)S(1)}, f32[128,512]{1,0:T(8,128)S(1)}, f32[128,512]{1,0:T(8,128)}) custom-call(s32[1]{0:T(128)} %bitcast.refs_0_, f32[512,256]{1,0:T(8,128)S(1)} %collective-permute-done.8.refs_1_, f32[512,256]{1,0:T(8,128)S(1)} %collective-permute-done.11.refs_2_, ...), custom_call_target="tpu_custom_call" | custom-call | flops 1 | bytes 1 | tf_op jit(solution)/shard_map/layer/pallas_call | solution.py:235
  97.2 2.8 %layer_grad.1 = (bf16[2048,256]{1,0:T(8,128)(2,1)S(1)}, f32[512,256]{1,0:T(8,128)S(1)}, f32[512,256]{1,0:T(8,128)S(1)}) custom-call(bf16[2048,512]{1,0:T(8,128)(2,1)S(1)} %get-tuple-element.72.refs_0_, bf16[1024,1024]{1,0:T(8,128)(2,1)S(1)} %get-tuple-element.65.refs_5_.refs_1_, bf16[1024,1024]{1,0:T(8,128)(2,1)S(1)} %get-tuple-element.66.refs_6_.refs_2_, ...), custom_call_target="tpu_custom_call" | custom-call | flops 10000000000 | bytes 1 | tf_op jit(solution)/shard_map/layer_grad/pallas_call | solution.py:259
  100.0 1.7 collective-permute-start.19
  102.1 4.3 %collective-permute-done.37 = f32[128,512]{1,0:T(8,128)} collective-permute-done((f32[128,512]{1,0:T(8,128)}, f32[128,512]{1,0:T(8,128)}, u32[]{:S(2)}, u32[]{:S(2)}) %collective-permute-start.37) | collective-permute-done | bytes 262176 | tf_op jit(solution)/shard_map/ppermute | solution.py:417
  108.3 5.4 %scatter_product.11 = (f32[512,256]{1,0:T(8,128)}, f32[512,256]{1,0:T(8,128)}) custom-call(bf16[2048,256]{1,0:T(8,128)(2,1)S(1)} %get-tuple-element.82.refs_0_, bf16[8,1024,1024]{2,1,0:T(8,128)(2,1)} %get-tuple-element.59.refs_2_.refs_4_.refs_6_.refs_1_, bf16[8,1024,1024]{2,1,0:T(8,128)(2,1)} %get-tuple-element.60.refs_3_.refs_5_.refs_7_.refs_2_), custom_call_target="tpu_custom_call" | custom-call | flops 1 | bytes 1 | tf_op jit(solution)/shard_map/scatter_product/pallas_call | solution.py:305
  113.7 1.3 collective-permute-start.25
  115.7 3.5 %collective-permute-done.38 = f32[64,512]{1,0:T(8,128)S(1)} collective-permute-done((f32[64,512]{1,0:T(8,128)S(1)}, f32[64,512]{1,0:T(8,128)S(1)}, u32[]{:S(2)}, u32[]{:S(2)}) %collective-permute-start.38) | collective-permute-done | bytes 131104 | tf_op jit(solution)/shard_map/ppermute | solution.py:417
  120.1 2.8 %collective-permute-start.39 = (f32[64,512]{1,0:T(8,128)S(1)}, f32[64,512]{1,0:T(8,128)S(1)}, u32[]{:S(2)}, u32[]{:S(2)}) collective-permute-start(f32[64,512]{1,0:T(8,128)S(1)} %dynamic-slice_add_fusion), channel_id=1, source_target_pairs={{0,8},{2,10},{4,12},{6,14},{8,0},{10,2},{12,4},{14,6},{1,9},{3,11}... | collective-permute-start | bytes 393224 | tf_op jit(solution)/shard_map/ppermute | solution.py:417
  123.0 5.9 %scatter_product.7 = (f32[512,256]{1,0:T(8,128)}, f32[512,256]{1,0:T(8,128)}) custom-call(bf16[2048,256]{1,0:T(8,128)(2,1)S(1)} %get-tuple-element.82.refs_0_, bf16[8,1024,1024]{2,1,0:T(8,128)(2,1)} %get-tuple-element.59.refs_2_.refs_4_.refs_6_.refs_1_, bf16[8,1024,1024]{2,1,0:T(8,128)(2,1)} %get-tuple-element.60.refs_3_.refs_5_.refs_7_.refs_2_, ...), custom_call_target="tpu_custom_call" | custom-call | flops 10000000000 | bytes 1 | tf_op jit(solution)/shard_map/scatter_product/pallas_call | solution.py:305
  128.8 2.0 %collective-permute-start.22 = (f32[512,256]{1,0:T(8,128)}, f32[512,256]{1,0:T(8,128)}, u32[]{:S(2)}, u32[]{:S(2)}) collective-permute-start(f32[512,256]{1,0:T(8,128)} %get-tuple-element.77), channel_id=1, source_target_pairs={{4,0},{8,4},{12,8},{14,12},{10,14},{6,10},{2,6},{0,2},{5,1},{9,5},... | collective-permute-start | bytes 1572872 | tf_op jit(solution)/shard_map/ppermute | solution.py:331
  130.9 6.8 %collective-permute-done.39 = f32[64,512]{1,0:T(8,128)S(1)} collective-permute-done((f32[64,512]{1,0:T(8,128)S(1)}, f32[64,512]{1,0:T(8,128)S(1)}, u32[]{:S(2)}, u32[]{:S(2)}) %collective-permute-start.39) | collective-permute-done | bytes 131104 | tf_op jit(solution)/shard_map/ppermute | solution.py:417
  137.8 4.5 %scatter_product.12 = (f32[512,256]{1,0:T(8,128)S(1)}, f32[512,256]{1,0:T(8,128)S(1)}) custom-call(bf16[2048,256]{1,0:T(8,128)(2,1)S(1)} %get-tuple-element.82.refs_0_, bf16[8,1024,1024]{2,1,0:T(8,128)(2,1)} %get-tuple-element.59.refs_2_.refs_4_.refs_6_.refs_1_, bf16[8,1024,1024]{2,1,0:T(8,128)(2,1)} %get-tuple-element.60.refs_3_.refs_5_.refs_7_.refs_2_, ...), custom_call_target="tpu_custom_call" | custom-call | flops 1 | bytes 1 | tf_op jit(solution)/shard_map/scatter_product/pallas_call | solution.py:305
  142.3 2.0 %collective-permute-start.27 = (f32[512,256]{1,0:T(8,128)S(1)}, f32[512,256]{1,0:T(8,128)S(1)}, u32[]{:S(2)}, u32[]{:S(2)}) collective-permute-start(f32[512,256]{1,0:T(8,128)S(1)} %get-tuple-element.86), channel_id=1, source_target_pairs={{0,4},{4,8},{8,12},{12,14},{14,10},{10,6},{6,2},{2,0},{1,5},{5,9},... | collective-permute-start | bytes 1572872 | tf_op jit(solution)/shard_map/ppermute | solution.py:328
  144.4 3.8 %collective-permute-done.40 = f32[64,512]{1,0:T(8,128)} collective-permute-done((f32[64,512]{1,0:T(8,128)S(1)}, f32[64,512]{1,0:T(8,128)}, u32[]{:S(2)}, u32[]{:S(2)}) %collective-permute-start.40) | collective-permute-done | bytes 131104 | tf_op jit(solution)/shard_map/ppermute | solution.py:417
  149.9 5.8 %scatter_product.8 = (f32[512,256]{1,0:T(8,128)}, f32[512,256]{1,0:T(8,128)}) custom-call(bf16[2048,256]{1,0:T(8,128)(2,1)S(1)} %get-tuple-element.82.refs_0_, bf16[8,1024,1024]{2,1,0:T(8,128)(2,1)} %get-tuple-element.59.refs_2_.refs_4_.refs_6_.refs_1_, bf16[8,1024,1024]{2,1,0:T(8,128)(2,1)} %get-tuple-element.60.refs_3_.refs_5_.refs_7_.refs_2_, ...), custom_call_target="tpu_custom_call" | custom-call | flops 10000000000 | bytes 1 | tf_op jit(solution)/shard_map/scatter_product/pallas_call | solution.py:305
  155.7 1.4 collective-permute-start.23
  157.7 1.3 collective-permute-done.41
  160.1 4.5 %scatter_product.13 = (f32[512,256]{1,0:T(8,128)S(1)}, f32[512,256]{1,0:T(8,128)S(1)}) custom-call(bf16[2048,256]{1,0:T(8,128)(2,1)S(1)} %get-tuple-element.82.refs_0_, bf16[8,1024,1024]{2,1,0:T(8,128)(2,1)} %get-tuple-element.59.refs_2_.refs_4_.refs_6_.refs_1_, bf16[8,1024,1024]{2,1,0:T(8,128)(2,1)} %get-tuple-element.60.refs_3_.refs_5_.refs_7_.refs_2_, ...), custom_call_target="tpu_custom_call" | custom-call | flops 1 | bytes 1 | tf_op jit(solution)/shard_map/scatter_product/pallas_call | solution.py:305
  164.7 2.4 %collective-permute-start.29 = (f32[512,256]{1,0:T(8,128)S(1)}, f32[512,256]{1,0:T(8,128)S(1)}, u32[]{:S(2)}, u32[]{:S(2)}) collective-permute-start(f32[512,256]{1,0:T(8,128)S(1)} %get-tuple-element.88), channel_id=1, source_target_pairs={{4,0},{8,4},{12,8},{14,12},{10,14},{6,10},{2,6},{0,2},{5,1},{9,5},... | collective-permute-start | bytes 1572872 | tf_op jit(solution)/shard_map/ppermute | solution.py:331
  167.0 1.5 collective-permute-done.23.refs_3_
  169.2 4.9 %scatter_product.9 = (f32[512,256]{1,0:T(8,128)S(1)}, f32[512,256]{1,0:T(8,128)S(1)}) custom-call(bf16[2048,256]{1,0:T(8,128)(2,1)S(1)} %get-tuple-element.82.refs_0_, bf16[8,1024,1024]{2,1,0:T(8,128)(2,1)} %get-tuple-element.59.refs_2_.refs_4_.refs_6_.refs_1_, bf16[8,1024,1024]{2,1,0:T(8,128)(2,1)} %get-tuple-element.60.refs_3_.refs_5_.refs_7_.refs_2_, ...), custom_call_target="tpu_custom_call" | custom-call | flops 10000000000 | bytes 1 | tf_op jit(solution)/shard_map/scatter_product/pallas_call | solution.py:305
  174.1 2.0 collective-permute-start.30
  176.2 4.5 %scatter_product.10 = (f32[512,256]{1,0:T(8,128)S(1)}, f32[512,256]{1,0:T(8,128)S(1)}) custom-call(bf16[2048,256]{1,0:T(8,128)(2,1)S(1)} %get-tuple-element.82.refs_0_, bf16[8,1024,1024]{2,1,0:T(8,128)(2,1)} %get-tuple-element.59.refs_2_.refs_4_.refs_6_.refs_1_, bf16[8,1024,1024]{2,1,0:T(8,128)(2,1)} %get-tuple-element.60.refs_3_.refs_5_.refs_7_.refs_2_), custom_call_target="tpu_custom_call" | custom-call | flops 10000000000 | bytes 1 | tf_op jit(solution)/shard_map/scatter_product/pallas_call | solution.py:305
  180.8 11.5 %collective-permute-done.30 = f32[512,256]{1,0:T(8,128)S(1)} collective-permute-done((f32[512,256]{1,0:T(8,128)S(1)}, f32[512,256]{1,0:T(8,128)S(1)}, u32[]{:S(2)}, u32[]{:S(2)}) %collective-permute-start.30) | collective-permute-done | bytes 524320 | tf_op jit(solution)/shard_map/ppermute | solution.py:328
  195.8 1.6 maximum_maximum_fusion
  (87 shorter events, 18.7 us)
Async XLA Ops:
  0.6 6.6 %copy-start.1 = (f32[512,512]{1,0:T(8,128)S(1)}, f32[512,512]{1,0:T(8,128)}, u32[]{:S(2)}) copy-start(f32[512,512]{1,0:T(8,128)} %param.7) | copy-start | bytes 3145732
  0.6 22.3 %collective-permute-start.4 = (f32[8,16,128,128]{3,2,1,0:T(8,128)}, f32[8,16,128,128]{3,2,1,0:T(8,128)}, u32[]{:S(2)}, u32[]{:S(2)}) collective-permute-start(f32[8,16,128,128]{3,2,1,0:T(8,128)} %bitcast.11), channel_id=1, source_target_pairs={{0,1},{1,0},{2,3},{3,2},{4,5},{5,4},{6,7},{7,6},{8,9},{9,8},{10,11... | collective-permute-start | bytes 25165832 | tf_op jit(solution)/shard_map/ppermute | solution.py:334
  1.2 7.1 %copy-start.4 = (s32[8,1]{0,1:T(1,128)S(1)}, s32[8,1]{0,1:T(1,128)}, u32[]{:S(2)}) copy-start(s32[8,1]{0,1:T(1,128)} %param.11) | copy-start | bytes 100
  1.2 7.2 %copy-start.3 = (s32[8,1,16]{2,1,0:T(1,128)S(1)}, s32[8,1,16]{2,1,0:T(1,128)}, u32[]{:S(2)}) copy-start(s32[8,1,16]{2,1,0:T(1,128)} %param.10) | copy-start | bytes 1540
  2.5 15.4 %collective-permute-start = (f32[512,256]{1,0:T(8,128)S(1)}, f32[512,256]{1,0:T(8,128)S(1)}, u32[]{:S(2)}, u32[]{:S(2)}) collective-permute-start(f32[512,256]{1,0:T(8,128)S(1)} %get-tuple-element.98.refs_0_), channel_id=1, source_target_pairs={{0,4},{4,8},{8,12},{12,14},{14,10},{10,6},{6,2},{2,0},{1,5},{5,9},... | collective-permute-start | bytes 1572872 | tf_op jit(solution)/shard_map/ppermute | solution.py:328
  5.2 14.8 %collective-permute-start.2 = (f32[512,256]{1,0:T(8,128)S(1)}, f32[512,256]{1,0:T(8,128)S(1)}, u32[]{:S(2)}, u32[]{:S(2)}) collective-permute-start(f32[512,256]{1,0:T(8,128)S(1)} %get-tuple-element.97.refs_1_), channel_id=1, source_target_pairs={{4,0},{8,4},{12,8},{14,12},{10,14},{6,10},{2,6},{0,2},{5,1},{9,5},... | collective-permute-start | bytes 1572872 | tf_op jit(solution)/shard_map/ppermute | solution.py:331
  5.2 26.9 %collective-permute-start.6 = (f32[512,256]{1,0:T(8,128)S(1)}, f32[512,256]{1,0:T(8,128)}, u32[]{:S(2)}, u32[]{:S(2)}) collective-permute-start(f32[512,256]{1,0:T(8,128)S(1)} %get-tuple-element.97.refs_1_), channel_id=1, source_target_pairs={{0,4},{4,8},{8,12},{12,14},{14,10},{10,6},{6,2},{2,0},{1,5},{5,9},... | collective-permute-start | bytes 1572872 | tf_op jit(solution)/shard_map/ppermute | solution.py:328
  7.2 24.1 %collective-permute-start.7 = (f32[512,256]{1,0:T(8,128)S(1)}, f32[512,256]{1,0:T(8,128)}, u32[]{:S(2)}, u32[]{:S(2)}) collective-permute-start(f32[512,256]{1,0:T(8,128)S(1)} %get-tuple-element.98.refs_0_), channel_id=1, source_target_pairs={{4,0},{8,4},{12,8},{14,12},{10,14},{6,10},{2,6},{0,2},{5,1},{9,5},... | collective-permute-start | bytes 1572872 | tf_op jit(solution)/shard_map/ppermute | solution.py:331
  19.9 1.2 collective-permute-start.3
  19.9 22.5 %collective-permute-start.9 = (f32[512,256]{1,0:T(8,128)S(1)}, f32[512,256]{1,0:T(8,128)S(1)}, u32[]{:S(2)}, u32[]{:S(2)}) collective-permute-start(f32[512,256]{1,0:T(8,128)S(1)} %collective-permute-done.2.refs_3_), channel_id=1, source_target_pairs={{4,0},{8,4},{12,8},{14,12},{10,14},{6,10},{2,6},{0,2},{5,1},{9,5},... | collective-permute-start | bytes 1572872 | tf_op jit(solution)/shard_map/ppermute | solution.py:331
  21.1 22.0 %collective-permute-start.1 = (f32[512,256]{1,0:T(8,128)S(1)}, f32[512,256]{1,0:T(8,128)S(1)}, u32[]{:S(2)}, u32[]{:S(2)}) collective-permute-start(f32[512,256]{1,0:T(8,128)S(1)} %collective-permute-done.refs_0_), channel_id=1, source_target_pairs={{0,4},{4,8},{8,12},{12,14},{14,10},{10,6},{6,2},{2,0},{1,5},{5,9},... | collective-permute-start | bytes 1572872 | tf_op jit(solution)/shard_map/ppermute | solution.py:328
  31.3 22.9 %collective-permute-start.16 = (f32[512,256]{1,0:T(8,128)}, f32[512,256]{1,0:T(8,128)S(1)}, u32[]{:S(2)}, u32[]{:S(2)}) collective-permute-start(f32[512,256]{1,0:T(8,128)} %collective-permute-done.7.refs_2_), channel_id=1, source_target_pairs={{4,0},{8,4},{12,8},{14,12},{10,14},{6,10},{2,6},{0,2},{5,1},{9,5},... | collective-permute-start | bytes 1572872 | tf_op jit(solution)/shard_map/ppermute | solution.py:331
  32.0 23.1 %collective-permute-start.14 = (f32[512,256]{1,0:T(8,128)}, f32[512,256]{1,0:T(8,128)S(1)}, u32[]{:S(2)}, u32[]{:S(2)}) collective-permute-start(f32[512,256]{1,0:T(8,128)} %collective-permute-done.6.refs_1_), channel_id=1, source_target_pairs={{0,4},{4,8},{8,12},{12,14},{14,10},{10,6},{6,2},{2,0},{1,5},{5,9},... | collective-permute-start | bytes 1572872 | tf_op jit(solution)/shard_map/ppermute | solution.py:328
  42.4 22.6 %collective-permute-start.10 = (f32[512,256]{1,0:T(8,128)S(1)}, f32[512,256]{1,0:T(8,128)}, u32[]{:S(2)}, u32[]{:S(2)}) collective-permute-start(f32[512,256]{1,0:T(8,128)S(1)} %collective-permute-done.9.refs_3_), channel_id=1, source_target_pairs={{4,0},{8,4},{12,8},{14,12},{10,14},{6,10},{2,6},{0,2},{5,1},{9,5},... | collective-permute-start | bytes 1572872 | tf_op jit(solution)/shard_map/ppermute | solution.py:331
  43.1 21.9 %collective-permute-start.5 = (f32[512,256]{1,0:T(8,128)S(1)}, f32[512,256]{1,0:T(8,128)}, u32[]{:S(2)}, u32[]{:S(2)}) collective-permute-start(f32[512,256]{1,0:T(8,128)S(1)} %collective-permute-done.1.refs_0_), channel_id=1, source_target_pairs={{0,4},{4,8},{8,12},{12,14},{14,10},{10,6},{6,2},{2,0},{1,5},{5,9},... | collective-permute-start | bytes 1572872 | tf_op jit(solution)/shard_map/ppermute | solution.py:328
  54.2 21.9 %collective-permute-start.17 = (f32[512,256]{1,0:T(8,128)S(1)}, f32[512,256]{1,0:T(8,128)S(1)}, u32[]{:S(2)}, u32[]{:S(2)}) collective-permute-start(f32[512,256]{1,0:T(8,128)S(1)} %collective-permute-done.16.refs_2_), channel_id=1, source_target_pairs={{4,0},{8,4},{12,8},{14,12},{10,14},{6,10},{2,6},{0,2},{5,1},{9,5},... | collective-permute-start | bytes 1572872 | tf_op jit(solution)/shard_map/ppermute | solution.py:331
  55.2 21.0 %collective-permute-start.15 = (f32[512,256]{1,0:T(8,128)S(1)}, f32[512,256]{1,0:T(8,128)S(1)}, u32[]{:S(2)}, u32[]{:S(2)}) collective-permute-start(f32[512,256]{1,0:T(8,128)S(1)} %collective-permute-done.14.refs_1_), channel_id=1, source_target_pairs={{0,4},{4,8},{8,12},{12,14},{14,10},{10,6},{6,2},{2,0},{1,5},{5,9},... | collective-permute-start | bytes 1572872 | tf_op jit(solution)/shard_map/ppermute | solution.py:328
  65.0 21.6 %collective-permute-start.11 = (f32[512,256]{1,0:T(8,128)}, f32[512,256]{1,0:T(8,128)S(1)}, u32[]{:S(2)}, u32[]{:S(2)}) collective-permute-start(f32[512,256]{1,0:T(8,128)} %collective-permute-done.10.refs_3_), channel_id=1, source_target_pairs={{4,0},{8,4},{12,8},{14,12},{10,14},{6,10},{2,6},{0,2},{5,1},{9,5},... | collective-permute-start | bytes 1572872 | tf_op jit(solution)/shard_map/ppermute | solution.py:331
  65.0 21.6 %collective-permute-start.8 = (f32[512,256]{1,0:T(8,128)}, f32[512,256]{1,0:T(8,128)S(1)}, u32[]{:S(2)}, u32[]{:S(2)}) collective-permute-start(f32[512,256]{1,0:T(8,128)} %collective-permute-done.5.refs_0_), channel_id=1, source_target_pairs={{0,4},{4,8},{8,12},{12,14},{14,10},{10,6},{6,2},{2,0},{1,5},{5,9},... | collective-permute-start | bytes 1572872 | tf_op jit(solution)/shard_map/ppermute | solution.py:328
  73.2 16.0 %copy-start = (f32[1024,512]{1,0:T(8,128)S(1)}, f32[1024,512]{1,0:T(8,128)}, u32[]{:S(2)}) copy-start(f32[1024,512]{1,0:T(8,128)} %refs_9_.1) | copy-start | bytes 6291460
  83.4 5.8 %collective-permute-start.18 = (f32[1024,256]{1,0:T(8,128)S(1)}, f32[1024,256]{1,0:T(8,128)S(1)}, u32[]{:S(2)}, u32[]{:S(2)}) collective-permute-start(f32[1024,256]{1,0:T(8,128)S(1)} %gather_product.7.refs_7_), channel_id=1, source_target_pairs={{0,1},{1,0},{2,3},{3,2},{4,5},{5,4},{6,7},{7,6},{8,9},{9,8},{10,11... | collective-permute-start | bytes 3145736 | tf_op jit(solution)/shard_map/ppermute | solution.py:334
  86.6 1.9 collective-permute-start.13
  86.6 2.7 %collective-permute-start.12 = (f32[512,256]{1,0:T(8,128)S(1)}, f32[512,256]{1,0:T(8,128)S(1)}, u32[]{:S(2)}, u32[]{:S(2)}) collective-permute-start(f32[512,256]{1,0:T(8,128)S(1)} %collective-permute-done.8.refs_1_), channel_id=1, source_target_pairs={{0,1},{1,0},{2,3},{3,2},{4,5},{5,4},{6,7},{7,6},{8,9},{9,8},{10,11... | collective-permute-start | bytes 1572872 | tf_op jit(solution)/shard_map/ppermute | solution.py:334
  96.9 9.5 %collective-permute-start.37 = (f32[128,512]{1,0:T(8,128)}, f32[128,512]{1,0:T(8,128)}, u32[]{:S(2)}, u32[]{:S(2)}) collective-permute-start(f32[128,512]{1,0:T(8,128)} %get-tuple-element.92), channel_id=1, source_target_pairs={{0,2},{2,0},{4,6},{6,4},{8,10},{10,8},{12,14},{14,12},{1,3},{3,1},... | collective-permute-start | bytes 786440 | tf_op jit(solution)/shard_map/ppermute | solution.py:417
  100.0 23.0 %collective-permute-start.19 = (f32[512,256]{1,0:T(8,128)S(1)}, f32[512,256]{1,0:T(8,128)}, u32[]{:S(2)}, u32[]{:S(2)}) collective-permute-start(f32[512,256]{1,0:T(8,128)S(1)} %get-tuple-element.74), channel_id=1, source_target_pairs={{0,4},{4,8},{8,12},{12,14},{14,10},{10,6},{6,2},{2,0},{1,5},{5,9},... | collective-permute-start | bytes 1572872 | tf_op jit(solution)/shard_map/ppermute | solution.py:328
  101.7 21.3 %collective-permute-start.20 = (f32[512,256]{1,0:T(8,128)S(1)}, f32[512,256]{1,0:T(8,128)}, u32[]{:S(2)}, u32[]{:S(2)}) collective-permute-start(f32[512,256]{1,0:T(8,128)S(1)} %get-tuple-element.75), channel_id=1, source_target_pairs={{4,0},{8,4},{12,8},{14,12},{10,14},{6,10},{2,6},{0,2},{5,1},{9,5},... | collective-permute-start | bytes 1572872 | tf_op jit(solution)/shard_map/ppermute | solution.py:331
  107.4 6.3 %copy-start.2 = (f32[128,512]{1,0:T(8,128)}, f32[128,512]{1,0:T(8,128)S(1)}, u32[]{:S(2)}) copy-start(f32[128,512]{1,0:T(8,128)S(1)} %add.82) | copy-start | bytes 786436
  107.4 11.8 %collective-permute-start.38 = (f32[64,512]{1,0:T(8,128)S(1)}, f32[64,512]{1,0:T(8,128)S(1)}, u32[]{:S(2)}, u32[]{:S(2)}) collective-permute-start(f32[64,512]{1,0:T(8,128)S(1)} %constant_dynamic-slice_fusion), channel_id=1, source_target_pairs={{0,4},{2,6},{4,0},{6,2},{8,12},{10,14},{12,8},{14,10},{1,5},{3,7},... | collective-permute-start | bytes 393224 | tf_op jit(solution)/shard_map/ppermute | solution.py:417
  113.7 24.1 %collective-permute-start.25 = (f32[512,256]{1,0:T(8,128)}, f32[512,256]{1,0:T(8,128)S(1)}, u32[]{:S(2)}, u32[]{:S(2)}) collective-permute-start(f32[512,256]{1,0:T(8,128)} %get-tuple-element.84), channel_id=1, source_target_pairs={{0,4},{4,8},{8,12},{12,14},{14,10},{10,6},{6,2},{2,0},{1,5},{5,9},... | collective-permute-start | bytes 1572872 | tf_op jit(solution)/shard_map/ppermute | solution.py:328
  115.0 22.8 %collective-permute-start.26 = (f32[512,256]{1,0:T(8,128)}, f32[512,256]{1,0:T(8,128)S(1)}, u32[]{:S(2)}, u32[]{:S(2)}) collective-permute-start(f32[512,256]{1,0:T(8,128)} %get-tuple-element.85), channel_id=1, source_target_pairs={{4,0},{8,4},{12,8},{14,12},{10,14},{6,10},{2,6},{0,2},{5,1},{9,5},... | collective-permute-start | bytes 1572872 | tf_op jit(solution)/shard_map/ppermute | solution.py:331
  120.1 17.5 %collective-permute-start.39 = (f32[64,512]{1,0:T(8,128)S(1)}, f32[64,512]{1,0:T(8,128)S(1)}, u32[]{:S(2)}, u32[]{:S(2)}) collective-permute-start(f32[64,512]{1,0:T(8,128)S(1)} %dynamic-slice_add_fusion), channel_id=1, source_target_pairs={{0,8},{2,10},{4,12},{6,14},{8,0},{10,2},{12,4},{14,6},{1,9},{3,11}... | collective-permute-start | bytes 393224 | tf_op jit(solution)/shard_map/ppermute | solution.py:417
  128.8 21.0 %collective-permute-start.21 = (f32[512,256]{1,0:T(8,128)}, f32[512,256]{1,0:T(8,128)}, u32[]{:S(2)}, u32[]{:S(2)}) collective-permute-start(f32[512,256]{1,0:T(8,128)} %get-tuple-element.76), channel_id=1, source_target_pairs={{0,4},{4,8},{8,12},{12,14},{14,10},{10,6},{6,2},{2,0},{1,5},{5,9},... | collective-permute-start | bytes 1572872 | tf_op jit(solution)/shard_map/ppermute | solution.py:328
  128.8 21.0 %collective-permute-start.22 = (f32[512,256]{1,0:T(8,128)}, f32[512,256]{1,0:T(8,128)}, u32[]{:S(2)}, u32[]{:S(2)}) collective-permute-start(f32[512,256]{1,0:T(8,128)} %get-tuple-element.77), channel_id=1, source_target_pairs={{4,0},{8,4},{12,8},{14,12},{10,14},{6,10},{2,6},{0,2},{5,1},{9,5},... | collective-permute-start | bytes 1572872 | tf_op jit(solution)/shard_map/ppermute | solution.py:331
  137.7 10.5 %collective-permute-start.40 = (f32[64,512]{1,0:T(8,128)S(1)}, f32[64,512]{1,0:T(8,128)}, u32[]{:S(2)}, u32[]{:S(2)}) collective-permute-start(f32[64,512]{1,0:T(8,128)S(1)} %add.86), channel_id=1, source_target_pairs={{0,4},{2,6},{4,0},{6,2},{8,12},{10,14},{12,8},{14,10},{1,5},{3,7},... | collective-permute-start | bytes 393224 | tf_op jit(solution)/shard_map/ppermute | solution.py:417
  142.3 17.8 %collective-permute-start.27 = (f32[512,256]{1,0:T(8,128)S(1)}, f32[512,256]{1,0:T(8,128)S(1)}, u32[]{:S(2)}, u32[]{:S(2)}) collective-permute-start(f32[512,256]{1,0:T(8,128)S(1)} %get-tuple-element.86), channel_id=1, source_target_pairs={{0,4},{4,8},{8,12},{12,14},{14,10},{10,6},{6,2},{2,0},{1,5},{5,9},... | collective-permute-start | bytes 1572872 | tf_op jit(solution)/shard_map/ppermute | solution.py:328
  144.4 15.7 %collective-permute-start.28 = (f32[512,256]{1,0:T(8,128)S(1)}, f32[512,256]{1,0:T(8,128)S(1)}, u32[]{:S(2)}, u32[]{:S(2)}) collective-permute-start(f32[512,256]{1,0:T(8,128)S(1)} %get-tuple-element.87), channel_id=1, source_target_pairs={{4,0},{8,4},{12,8},{14,12},{10,14},{6,10},{2,6},{0,2},{5,1},{9,5},... | collective-permute-start | bytes 1572872 | tf_op jit(solution)/shard_map/ppermute | solution.py:331
  149.9 9.1 %collective-permute-start.41 = (f32[128,512]{1,0:T(8,128)}, f32[128,512]{1,0:T(8,128)}, u32[]{:S(2)}, u32[]{:S(2)}) collective-permute-start(f32[128,512]{1,0:T(8,128)} %pad_maximum_fusion.3), channel_id=1, source_target_pairs={{0,2},{2,0},{4,6},{6,4},{8,10},{10,8},{12,14},{14,12},{1,3},{3,1},... | collective-permute-start | bytes 786440 | tf_op jit(solution)/shard_map/ppermute | solution.py:417
  155.7 12.8 %collective-permute-start.23 = (f32[512,256]{1,0:T(8,128)}, f32[512,256]{1,0:T(8,128)}, u32[]{:S(2)}, u32[]{:S(2)}) collective-permute-start(f32[512,256]{1,0:T(8,128)} %get-tuple-element.78), channel_id=1, source_target_pairs={{0,4},{4,8},{8,12},{12,14},{14,10},{10,6},{6,2},{2,0},{1,5},{5,9},... | collective-permute-start | bytes 1572872 | tf_op jit(solution)/shard_map/ppermute | solution.py:328
  157.1 12.1 %collective-permute-start.24 = (f32[512,256]{1,0:T(8,128)}, f32[512,256]{1,0:T(8,128)}, u32[]{:S(2)}, u32[]{:S(2)}) collective-permute-start(f32[512,256]{1,0:T(8,128)} %get-tuple-element.79), channel_id=1, source_target_pairs={{4,0},{8,4},{12,8},{14,12},{10,14},{6,10},{2,6},{0,2},{5,1},{9,5},... | collective-permute-start | bytes 1572872 | tf_op jit(solution)/shard_map/ppermute | solution.py:331
  160.0 33.0 %collective-permute-start.42 = (f32[256,512]{1,0:T(8,128)S(1)}, f32[256,512]{1,0:T(8,128)S(1)}, u32[]{:S(2)}, u32[]{:S(2)}) collective-permute-start(f32[256,512]{1,0:T(8,128)S(1)} %pad_maximum_fusion.2), channel_id=1, source_target_pairs={{0,1},{1,0},{2,3},{3,2},{4,5},{5,4},{6,7},{7,6},{8,9},{9,8},{10,11... | collective-permute-start | bytes 1572872 | tf_op jit(solution)/shard_map/ppermute | solution.py:334
  164.7 16.0 %collective-permute-start.29 = (f32[512,256]{1,0:T(8,128)S(1)}, f32[512,256]{1,0:T(8,128)S(1)}, u32[]{:S(2)}, u32[]{:S(2)}) collective-permute-start(f32[512,256]{1,0:T(8,128)S(1)} %get-tuple-element.88), channel_id=1, source_target_pairs={{4,0},{8,4},{12,8},{14,12},{10,14},{6,10},{2,6},{0,2},{5,1},{9,5},... | collective-permute-start | bytes 1572872 | tf_op jit(solution)/shard_map/ppermute | solution.py:331
  167.0 25.3 %collective-permute-start.33 = (f32[512,256]{1,0:T(8,128)S(1)}, f32[512,256]{1,0:T(8,128)S(1)}, u32[]{:S(2)}, u32[]{:S(2)}) collective-permute-start(f32[512,256]{1,0:T(8,128)S(1)} %get-tuple-element.90), channel_id=1, source_target_pairs={{0,4},{4,8},{8,12},{12,14},{14,10},{10,6},{6,2},{2,0},{1,5},{5,9},... | collective-permute-start | bytes 1572872 | tf_op jit(solution)/shard_map/ppermute | solution.py:328
  174.1 18.2 %collective-permute-start.30 = (f32[512,256]{1,0:T(8,128)S(1)}, f32[512,256]{1,0:T(8,128)S(1)}, u32[]{:S(2)}, u32[]{:S(2)}) collective-permute-start(f32[512,256]{1,0:T(8,128)S(1)} %get-tuple-element.80), channel_id=1, source_target_pairs={{0,4},{4,8},{8,12},{12,14},{14,10},{10,6},{6,2},{2,0},{1,5},{5,9},... | collective-permute-start | bytes 1572872 | tf_op jit(solution)/shard_map/ppermute | solution.py:328
  176.1 16.9 %collective-permute-start.34 = (f32[512,256]{1,0:T(8,128)S(1)}, f32[512,256]{1,0:T(8,128)S(1)}, u32[]{:S(2)}, u32[]{:S(2)}) collective-permute-start(f32[512,256]{1,0:T(8,128)S(1)} %get-tuple-element.81), channel_id=1, source_target_pairs={{4,0},{8,4},{12,8},{14,12},{10,14},{6,10},{2,6},{0,2},{5,1},{9,5},... | collective-permute-start | bytes 1572872 | tf_op jit(solution)/shard_map/ppermute | solution.py:331
  180.8 13.4 %collective-permute-start.31 = (f32[512,256]{1,0:T(8,128)S(1)}, f32[512,256]{1,0:T(8,128)S(1)}, u32[]{:S(2)}, u32[]{:S(2)}) collective-permute-start(f32[512,256]{1,0:T(8,128)S(1)} %add.75), channel_id=1, source_target_pairs={{0,1},{1,0},{2,3},{3,2},{4,5},{5,4},{6,7},{7,6},{8,9},{9,8},{10,11... | collective-permute-start | bytes 1572872 | tf_op jit(solution)/shard_map/ppermute | solution.py:334
  192.3 1.9 collective-permute-start.32
  192.4 2.6 %collective-permute-start.35 = (f32[512,256]{1,0:T(8,128)S(1)}, f32[512,256]{1,0:T(8,128)S(1)}, u32[]{:S(2)}, u32[]{:S(2)}) collective-permute-start(f32[512,256]{1,0:T(8,128)S(1)} %add.78), channel_id=1, source_target_pairs={{0,1},{1,0},{2,3},{3,2},{4,5},{5,4},{6,7},{7,6},{8,9},{9,8},{10,11... | collective-permute-start | bytes 1572872 | tf_op jit(solution)/shard_map/ppermute | solution.py:334
  192.9 2.8 %collective-permute-start.36 = (f32[512,256]{1,0:T(8,128)S(1)}, f32[512,256]{1,0:T(8,128)S(1)}, u32[]{:S(2)}, u32[]{:S(2)}) collective-permute-start(f32[512,256]{1,0:T(8,128)S(1)} %collective-permute-done.34), channel_id=1, source_target_pairs={{0,1},{1,0},{2,3},{3,2},{4,5},{5,4},{6,7},{7,6},{8,9},{9,8},{10,11... | collective-permute-start | bytes 1572872 | tf_op jit(solution)/shard_map/ppermute | solution.py:334
